TPU v7x, 256 devices: a whole 4x4x8 slice. The times are simulated.
256 devices in a mesh: rows: 8 (over y, x_lo), cols: 32 (over z, x_hi, core).
Axes of the slice: x: 4 (x_hi: 2, x_lo: 2; x = x_hi * 2 + x_lo), y: 4, z: 8, core: 2. Of those that a mesh axis runs over, the one named last changes fastest.
Arguments:
- counts: bfloat16 [4096, 262144], P('rows', 'cols'), may hold values from 0 to 12, as said below
- start_a: float32 [4096, 128], P(('rows', 'cols')), may hold values from -0.4 to 0.4
- start_b: float32 [16384, 128], P(('cols', 'rows')), may hold values from -0.4 to 0.4
- start_c: float32 [16, 128], replicated, may hold values from -0.4 to 0.4
Outputs:
- factor_a: float32 [4096, 128], P(('rows', 'cols'))
- factor_b: float32 [16384, 128], P(('cols', 'rows'))
- factor_c: float32 [16, 128], replicated
Inputs may be any that keep to these rules, and one draw needn't show every extreme that they name: counts holds whole numbers.
All inputs are finite; a program needn't handle non-finite values.
Results may differ from a plain program's by a relative error of at most 0.009.
Values may be sent and summed in bfloat16 or wider, within the bound.
No kernel may reach another device: no remote copies, remote signals or barrier semaphores. Data moves between devices by JAX's collectives and lax.ppermute only.
A program may use at most 128 MiB of HBM per device.

v0:
```python
import math

import jax
import jax.numpy as jnp
from jax import lax
from jax.sharding import PartitionSpec as P

ITERS = 2


def local(counts, start_a, start_b, start_c):
    rows_here, flat_width = counts.shape
    depth = start_c.shape[0]
    cols_here = flat_width // depth
    total_i = rows_here * lax.axis_size("rows")
    total_j = cols_here * lax.axis_size("cols")
    rate_a = 0.3 / math.sqrt(total_j * depth)
    rate_b = 0.3 / math.sqrt(total_i * depth)
    rate_c = 0.3 / math.sqrt(total_i * total_j)
    local_a, local_b, shared_c = (start_a, start_b, start_c)
    for iteration in range(ITERS):
        low_a = lax.all_gather(local_a.astype(jnp.bfloat16), "cols", axis=0, tiled=True)
        low_b = lax.all_gather(local_b.astype(jnp.bfloat16), "rows", axis=0, tiled=True)
        low_b_wide = low_b.astype(jnp.float32)
        scaled = (low_b_wide[:, None, :] * shared_c[None, :, :]).astype(jnp.bfloat16)
        scaled = scaled.reshape(cols_here * depth, shared_c.shape[1])
        log_rate = lax.dot_general(
            low_a, scaled, (((1,), (1,)), ((), ())), preferred_element_type=jnp.float32
        )
        residual = (jnp.exp(log_rate) - counts.astype(jnp.float32)).astype(jnp.bfloat16)
        grad_a = jnp.dot(residual, scaled, preferred_element_type=jnp.float32)
        mixed = lax.dot_general(
            residual, low_a, (((0,), (0,)), ((), ())), preferred_element_type=jnp.float32
        )
        mixed = mixed.reshape(cols_here, depth, shared_c.shape[1])
        grad_b = jnp.sum(mixed * shared_c[None, :, :], axis=1)
        grad_c = jnp.sum(mixed * low_b_wide[:, None, :], axis=0)
        summed_a = lax.psum_scatter(grad_a, "cols", scatter_dimension=0, tiled=True)
        summed_b = lax.psum_scatter(grad_b, "rows", scatter_dimension=0, tiled=True)
        local_a = local_a - rate_a * summed_a
        local_b = local_b - rate_b * summed_b
        summed_c = lax.psum(grad_c, ("rows", "cols"))
        shared_c = shared_c - rate_c * summed_c
    return (local_a, local_b, shared_c)


def solution(mesh):
    placed = (P("rows", "cols"), P(("rows", "cols"), None), P(("cols", "rows"), None), P())
    return jax.shard_map(
        local,
        mesh=mesh,
        in_specs=placed,
        out_specs=(P(("rows", "cols"), None), P(("cols", "rows"), None), P()),
        check_vma=False,
    )
```

profile of v0, /device:TPU:1, one launch (start us, length us, event | category | flops | bytes accessed | tf_op | source)
XLA Modules:
  0.0 451.3 jit_solution(1326504930640590621)
XLA Ops:
  7.2 0.0 copy-start.2
  7.2 0.0 copy-start.4
  7.2 0.0 copy-start.5
  7.2 0.0 reduce-scatter.5.cloned.1.call-start
  7.2 12.0 %copy.7 = bf16[512,8192]{0,1:T(8,128)(2,1)} copy(bf16[512,8192]{1,0:T(8,128)(2,1)} %param.4) | data formatting | bytes 16777216 | tf_op args[0]
  19.2 0.0 copy-done.2
  19.2 23.8 %all_gather.12 = bf16[512,128]{1,0:T(8,128)(2,1)S(1)} all-gather(bf16[64,128]{1,0:T(8,128)(2,1)S(1)} %convert_element_type.42), channel_id=1, replica_groups=mesh['rows'=8,'cols'=32] {'rows'}, dimensions={0}, use_global_device_ids=true | all-gather | bytes 147456 | tf_op jit(solution)/shard_map/all_gather | solution.py:23
  43.1 0.0 copy-done.4
  43.1 51.2 %all_gather.13 = bf16[512,128]{1,0:T(8,128)(2,1)S(1)} all-gather(bf16[16,128]{1,0:T(8,128)(2,1)S(1)} %convert_element_type.46), channel_id=1, replica_groups=mesh['rows'=8,'cols'=32] {'cols'}, dimensions={0}, use_global_device_ids=true | all-gather | bytes 135168 | tf_op jit(solution)/shard_map/all_gather | solution.py:22
  94.3 0.0 copy-done.5
  94.3 0.4 multiply_convert_fusion.1
  94.7 5.0 %fusion = bf16[512,8192]{0,1:T(8,128)(2,1)S(1)} fusion(bf16[512,8192]{0,1:T(8,128)(2,1)} %copy.7, bf16[8192,128]{1,0:T(8,128)(2,1)S(1)} %bitcast.22, bf16[512,128]{1,0:T(8,128)(2,1)S(1)} %all_gather.13), kind=kOutput, calls=%fused_computation.2 | convolution fusion | flops 1086324736 | bytes 19005440 | tf_op jit(solution)/shard_map/dot_general | solution.py:27
  99.7 0.0 copy-start
  99.7 3.2 copy-done
  102.9 3.0 fusion.4
  106.0 0.0 reduce-scatter.5.cloned.1.call-update
  106.0 0.0 reduce-scatter.7.cloned.1.call-start
  106.0 8.4 %multiply_reduce_fusion.3 = (f32[512,128]{1,0:T(8,128)}, f32[8192,128]{1,0:T(8,128)}) fusion(f32[16,128]{1,0:T(8,128)S(1)} %copy-done.5, bf16[512,8192]{0,1:T(8,128)(2,1)} %copy-done, bf16[512,128]{1,0:T(8,128)(2,1)S(1)} %all_gather.13), kind=kOutput, calls=%fused_computation.8 | convolution fusion | flops 1075773440 | bytes 12984320 | tf_op jit(solution)/shard_map/dot_general | solution.py:32
  114.4 0.0 reduce-scatter.7.cloned.1.call-update
  114.4 0.0 reduce-scatter.9.cloned.1.call-start
  114.5 2.8 multiply_reduce_fusion.2
  117.3 73.5 %psum.14 = f32[16,128]{1,0:T(8,128)S(1)} all-reduce(f32[16,128]{1,0:T(8,128)S(1)} %multiply_reduce_fusion.2), channel_id=1, replica_groups=mesh['rows'=8,'cols'=32] {'rows','cols'}, use_global_device_ids=true, to_apply=%region_4.0 | all-reduce | flops 2048 | bytes 16384 | tf_op jit(solution)/shard_map/psum | solution.py:42
  190.8 18.2 %reduce-scatter.5.cloned.1.call-done = f32[16,128]{1,0:T(8,128)} async-done(((f32[512,128]{1,0:T(8,128)}), f32[16,128]{1,0:T(8,128)}) %reduce-scatter.5.cloned.1.call-update) | async-done | bytes 8208 | tf_op jit(solution)/shard_map/reduce_scatter | solution.py:38
  209.0 0.7 fusion.3
  209.7 45.2 %all_gather.14 = bf16[512,128]{1,0:T(8,128)(2,1)S(1)} all-gather(bf16[16,128]{1,0:T(8,128)(2,1)S(1)} %fusion.3), channel_id=1, replica_groups=mesh['rows'=8,'cols'=32] {'cols'}, dimensions={0}, use_global_device_ids=true | all-gather | bytes 135168 | tf_op jit(solution)/shard_map/all_gather | solution.py:22
  254.9 0.0 reduce-scatter.7.cloned.1.call-done
  254.9 0.8 fusion.2
  255.7 22.2 %all_gather.15 = bf16[512,128]{1,0:T(8,128)(2,1)S(1)} all-gather(bf16[64,128]{1,0:T(8,128)(2,1)S(1)} %fusion.2), channel_id=1, replica_groups=mesh['rows'=8,'cols'=32] {'rows'}, dimensions={0}, use_global_device_ids=true | all-gather | bytes 147456 | tf_op jit(solution)/shard_map/all_gather | solution.py:23
  277.9 0.4 multiply_convert_fusion
  278.3 5.0 %fusion.1 = bf16[512,8192]{0,1:T(8,128)(2,1)S(1)} fusion(bf16[512,8192]{0,1:T(8,128)(2,1)} %copy.7, bf16[512,128]{1,0:T(8,128)(2,1)S(1)} %all_gather.14, bf16[8192,128]{1,0:T(8,128)(2,1)S(1)} %bitcast.24), kind=kOutput, calls=%fused_computation.3 | convolution fusion | flops 1086324736 | bytes 19005440 | tf_op jit(solution)/shard_map/dot_general | solution.py:27
  283.3 0.0 copy-start.1
  283.3 3.2 copy-done.1
  286.5 3.1 fusion.5
  289.6 0.0 reduce-scatter.9.cloned.1.call-update
  289.6 0.0 reduce-scatter.11.cloned.1.call-start
  289.7 8.4 %multiply_reduce_fusion.1 = (f32[512,128]{1,0:T(8,128)}, f32[8192,128]{1,0:T(8,128)}) fusion(f32[16,128]{1,0:T(8,128)S(1)} %multiply_subtract_fusion.4, bf16[512,8192]{0,1:T(8,128)(2,1)} %copy-done.1, bf16[512,128]{1,0:T(8,128)(2,1)S(1)} %all_gather.14), kind=kOutput, calls=%fused_computation.5 | convolution fusion | flops 1075773440 | bytes 12984320 | tf_op jit(solution)/shard_map/dot_general | solution.py:32
  298.1 0.0 copy-start.6
  298.1 0.0 copy-start.3
  298.1 0.0 reduce-scatter.11.cloned.1.call-update
  298.1 2.8 multiply_reduce_fusion
  300.9 79.8 %psum.15 = f32[16,128]{1,0:T(8,128)S(1)} all-reduce(f32[16,128]{1,0:T(8,128)S(1)} %multiply_reduce_fusion), channel_id=1, replica_groups=mesh['rows'=8,'cols'=32] {'rows','cols'}, use_global_device_ids=true, to_apply=%region_9.0 | all-reduce | flops 2048 | bytes 16384 | tf_op jit(solution)/shard_map/psum | solution.py:42
  380.7 0.6 multiply_subtract_fusion.2
  381.3 21.2 %reduce-scatter.9.cloned.1.call-done = f32[16,128]{1,0:T(8,128)} async-done(((f32[512,128]{1,0:T(8,128)}), f32[16,128]{1,0:T(8,128)}) %reduce-scatter.9.cloned.1.call-update) | async-done | bytes 8208 | tf_op jit(solution)/shard_map/reduce_scatter | solution.py:38
  402.6 0.0 copy-done.6
  402.6 1.3 multiply_subtract_fusion.3
  403.9 39.5 %reduce-scatter.11.cloned.1.call-done = f32[64,128]{1,0:T(8,128)} async-done(((f32[512,128]{1,0:T(8,128)}), f32[64,128]{1,0:T(8,128)}) %reduce-scatter.11.cloned.1.call-update) | async-done | bytes 32784 | tf_op jit(solution)/shard_map/reduce_scatter | solution.py:39
  443.4 0.0 copy-done.3
  443.4 1.4 multiply_subtract_fusion
  (5 shorter events, 0.0 us)
Async XLA Ops:
  7.2 12.0 %copy-start.2 = (f32[64,128]{1,0:T(8,128)S(1)}, f32[64,128]{1,0:T(8,128)}, u32[]{:S(2)}) copy-start(f32[64,128]{1,0:T(8,128)} %param.6) | copy-start | bytes 98308
  7.2 35.9 %copy-start.4 = (f32[16,128]{1,0:T(8,128)S(1)}, f32[16,128]{1,0:T(8,128)}, u32[]{:S(2)}) copy-start(f32[16,128]{1,0:T(8,128)} %param.5) | copy-start | bytes 24580
  7.2 87.1 %copy-start.5 = (f32[16,128]{1,0:T(8,128)S(1)}, f32[16,128]{1,0:T(8,128)}, u32[]{:S(2)}) copy-start(f32[16,128]{1,0:T(8,128)} %param.7) | copy-start | bytes 24580
  7.2 201.8 %reduce-scatter.5.cloned.1.call-start = ((), (), s32[]{:S(2)}) async-start(), calls=%async_computation.4 | async-start | bytes 270336 | tf_op jit(solution)/shard_map/reduce_scatter | solution.py:38
  99.7 3.2 copy-start
  106.0 148.9 %reduce-scatter.7.cloned.1.call-start = ((), (), s32[]{:S(2)}) async-start(), calls=%async_computation.5 | async-start | bytes 294912 | tf_op jit(solution)/shard_map/reduce_scatter | solution.py:39
  114.4 288.1 %reduce-scatter.9.cloned.1.call-start = ((), (), s32[]{:S(2)}) async-start(), calls=%async_computation.6 | async-start | bytes 270336 | tf_op jit(solution)/shard_map/reduce_scatter | solution.py:38
  283.3 3.2 copy-start.1
  289.6 153.8 %reduce-scatter.11.cloned.1.call-start = ((), (), s32[]{:S(2)}) async-start(), calls=%async_computation.7 | async-start | bytes 294912 | tf_op jit(solution)/shard_map/reduce_scatter | solution.py:39
  298.1 104.5 %copy-start.6 = (f32[16,128]{1,0:T(8,128)S(1)}, f32[16,128]{1,0:T(8,128)}, u32[]{:S(2)}) copy-start(f32[16,128]{1,0:T(8,128)} %reduce-scatter.5.cloned.1.call-done) | copy-start | bytes 24580
  298.1 145.3 %copy-start.3 = (f32[64,128]{1,0:T(8,128)S(1)}, f32[64,128]{1,0:T(8,128)}, u32[]{:S(2)}) copy-start(f32[64,128]{1,0:T(8,128)} %reduce-scatter.7.cloned.1.call-done) | copy-start | bytes 98308
Sparse Core Ops, SparseCore 0:
  106.1 102.8 reduce-scatter.4
  211.5 38.2 reduce-scatter.6
  289.7 112.7 reduce-scatter.8
  405.1 38.2 reduce-scatter.10
where the time goes:
time: 456 us; the launch traced here: 451 us
  blocking collectives  296 us (65%)
  waiting for transfers between devices  79 us (17%)
  matrix products  33 us (7%)
  local copies, waits for them, and re-layouts  18.4 us (4%)
  between operations  13.9 us (3%)
  other arithmetic  11.1 us (2%)
    psum x2, blocking collectives, local(): summed_c = lax.psum(grad_c, ('rows', 'cols'))  153 us
    all_gather x2, blocking collectives, local(): lax.all_gather(local_a.astype(jnp.bfloat16), 'cols', axis=0, tiled=True)  96.4 us
    all_gather x2, blocking collectives, local(): lax.all_gather(local_b.astype(jnp.bfloat16), 'rows', axis=0, tiled=True)  46 us
    reduce_scatter x2, waiting for transfers between devices, local(): summed_b = lax.psum_scatter(grad_b, 'rows', scatter_dimension=0, tiled=True)  39.5 us
    reduce_scatter x2, waiting for transfers between devices, local(): summed_a = lax.psum_scatter(grad_a, 'cols', scatter_dimension=0, tiled=True)  39.4 us
    unnamed x15, local copies, waits for them, and re-layouts  18.4 us
    dot_general x2, matrix products, local(): lax.dot_general(residual, low_a, (((0,), (0,)), ((), ())), preferred_elem...  16.8 us
    dot_general x2, matrix products, local(): lax.dot_general(low_a, scaled, (((1,), (1,)), ((), ())), preferred_elemen...  10.1 us
  transfers between devices with their start and end apart: 4, of which 3 were waited for; matrix products, arithmetic and copies ran while one was open for 6% of the time, Pallas kernels for 0%

commit v1 on v0

v1 whole, which is shorter than its diff:
```python
import functools
import math

import jax
import jax.numpy as jnp
from jax import lax
from jax.experimental import pallas as pl
from jax.experimental.pallas import tpu as pltpu
from jax.sharding import PartitionSpec as P

ITERS = 2
BF16 = jnp.bfloat16
F32 = jnp.float32
TILE = 1024


def grads_body(n_ref, a_ref, b_ref, c_ref, ga_ref, gb_ref, gc_ref):
    depth, rank = c_ref.shape
    flat = n_ref.shape[1]
    tile = math.gcd(flat, TILE)
    wide = tile // depth
    low_a = a_ref[...]
    c = c_ref[...]
    ga_ref[...] = jnp.zeros_like(ga_ref)
    gc_ref[...] = jnp.zeros_like(gc_ref)
    for q in range(flat // tile):
        columns = slice(q * tile, (q + 1) * tile)
        here = slice(q * wide, (q + 1) * wide)
        low_b = b_ref[here].astype(F32)
        scaled = (low_b[:, None, :] * c[None]).astype(BF16).reshape(tile, rank)
        log_rate = lax.dot_general(
            low_a, scaled, (((1,), (1,)), ((), ())), preferred_element_type=F32
        )
        residual = (jnp.exp(log_rate) - n_ref[:, columns].astype(F32)).astype(BF16)
        mixed = lax.dot_general(
            residual, low_a, (((0,), (0,)), ((), ())), preferred_element_type=F32
        ).reshape(wide, depth, rank)
        gb_ref[here] = jnp.sum(mixed * c[None], axis=1)
        gc_ref[...] += jnp.sum(mixed * low_b[:, None, :], axis=0)
        ga_ref[...] += jnp.dot(residual, scaled, preferred_element_type=F32)


def grads(counts, low_a, low_b, c):
    rows, flat = counts.shape
    depth, rank = c.shape
    whole = pl.BlockSpec(memory_space=pltpu.VMEM)
    return pl.pallas_call(
        grads_body,
        in_specs=[whole] * 4,
        out_specs=[whole] * 3,
        out_shape=[
            jax.ShapeDtypeStruct((rows, rank), F32),
            jax.ShapeDtypeStruct((flat // depth, rank), F32),
            jax.ShapeDtypeStruct((depth, rank), F32),
        ],
        compiler_params=pltpu.CompilerParams(vmem_limit_bytes=20 << 20),
        cost_estimate=pl.CostEstimate(
            flops=6 * rows * flat * rank,
            transcendentals=rows * flat,
            bytes_accessed=2 * rows * flat,
        ),
    )(counts, low_a, low_b, c)


def gather(piece, axis):
    n = lax.axis_size(axis)
    out = lax.all_to_all(jnp.broadcast_to(piece[None], (n, *piece.shape)), axis, 0, 0)
    return out.reshape(n * piece.shape[0], piece.shape[1])


def reduce_with(whole, extra, axis):
    n = lax.axis_size(axis)
    rows = whole.shape[0] // n
    pieces = whole.astype(BF16).reshape(n, rows, whole.shape[1])
    extras = jnp.broadcast_to(extra.astype(BF16)[None], (n, *extra.shape))
    got = lax.all_to_all(jnp.concatenate([pieces, extras], axis=1), axis, 0, 0)
    total = jnp.sum(got.astype(F32), axis=0)
    return total[:rows], total[rows:]


def local(counts, start_a, start_b, start_c):
    rows_here, flat_width = counts.shape
    depth = start_c.shape[0]
    cols_here = flat_width // depth
    total_i = rows_here * lax.axis_size("rows")
    total_j = cols_here * lax.axis_size("cols")
    rate_a = 0.3 / math.sqrt(total_j * depth)
    rate_b = 0.3 / math.sqrt(total_i * depth)
    rate_c = 0.3 / math.sqrt(total_i * total_j)
    local_a, local_b, shared_c = (start_a, start_b, start_c)
    for iteration in range(ITERS):
        low_b = gather(local_b.astype(BF16), "rows")
        low_a = gather(local_a.astype(BF16), "cols")
        grad_a, grad_b, grad_c = grads(counts, low_a, low_b, shared_c)
        summed_b, part_c = reduce_with(grad_b, grad_c, "rows")
        summed_a, summed_c = reduce_with(grad_a, part_c, "cols")
        local_a = local_a - rate_a * summed_a
        local_b = local_b - rate_b * summed_b
        shared_c = shared_c - rate_c * summed_c
    return (local_a, local_b, shared_c)


def solution(mesh):
    placed = (P("rows", "cols"), P(("rows", "cols"), None), P(("cols", "rows"), None), P())
    return jax.shard_map(
        local,
        mesh=mesh,
        in_specs=placed,
        out_specs=(P(("rows", "cols"), None), P(("cols", "rows"), None), P()),
        check_vma=False,
    )
```

time: 456 us -> 143 us (0.31)
  blocking collectives: 296 us -> 39.2 us
  matrix products: 33 us -> 0 us
  waiting for transfers between devices: 79 us -> 47.2 us
  starting transfers between devices: 0.16 us -> 25.9 us
  Pallas kernels: 0 us -> 14.2 us
  between operations: 13.9 us -> 0.86 us
  local copies, waits for them, and re-layouts: 18.4 us -> 8.9 us
  other arithmetic: 11.1 us -> 5.77 us
    psum x2 -> x0, blocking collectives: 153 us -> none  [local(): summed_c = lax.psum(grad_c, ('rows', 'cols'))]
    all_gather x4 -> x0, blocking collectives: 142 us -> none  [the longest x2 96.4 us: local(): lax.all_gather(local_a.astype(jnp.bfloat16), 'cols', axis=0, tiled=True)]
    reduce_scatter x4 -> x0, waiting for transfers between devices: 78.9 us -> none  [the longest x2 39.5 us: local(): summed_b = lax.psum_scatter(grad_b, 'rows', scatter_dimension=0, tiled=True)]
    all_to_all x0 -> x6, waiting for transfers between devices: none -> 47.2 us  [the longest x4 36.8 us: reduce_with(): got = lax.all_to_all(jnp.concatenate([pieces, extras], axis=1), axis, 0, 0)]
    all_to_all x0 -> x2, blocking collectives: none -> 39.2 us  [gather(): lax.all_to_all(jnp.broadcast_to(piece[None], (n, *piece.shape)), axis, 0, 0)]
    dot_general x6 -> x0, matrix products: 33 us -> none  [the longest x2 16.8 us: local(): lax.dot_general(residual, low_a, (((0,), (0,)), ((), ())), preferred_elem...]
    all_to_all x0 -> x6, starting transfers between devices: none -> 25.9 us  [the longest x4 16.6 us: reduce_with(): got = lax.all_to_all(jnp.concatenate([pieces, extras], axis=1), axis, 0, 0)]
    pallas_call x0 -> x2, Pallas kernels: none -> 14.2 us  [grads(): pl.pallas_call(grads_body, in_specs=[whole] * 4, out_specs=[whole] * 3, o...]
  transfers between devices with their start and end apart: 4 -> 6, of which waited for: 3 -> 6; matrix products, arithmetic and copies ran while one was open for 6% -> 1% of each run, Pallas kernels for 0% -> 0%
where the time goes in v1:
time: 143 us; the launch traced here: 142 us
  waiting for transfers between devices  47.2 us (33%)
  blocking collectives  39.2 us (27%)
  starting transfers between devices  25.9 us (18%)
  Pallas kernels  14.2 us (10%)
  local copies, waits for them, and re-layouts  8.9 us (6%)
  other arithmetic  5.77 us (4%)
    all_to_all x2, blocking collectives, gather(): lax.all_to_all(jnp.broadcast_to(piece[None], (n, *piece.shape)), axis, 0, 0)  39.2 us
    all_to_all x4, waiting for transfers between devices, reduce_with(): got = lax.all_to_all(jnp.concatenate([pieces, extras], axis=1), axis, 0, 0)  36.8 us
    all_to_all x4, starting transfers between devices, reduce_with(): got = lax.all_to_all(jnp.concatenate([pieces, extras], axis=1), axis, 0, 0)  16.6 us
    pallas_call x2, Pallas kernels, grads(): pl.pallas_call(grads_body, in_specs=[whole] * 4, out_specs=[whole] * 3, o...  14.2 us
    all_to_all x2, waiting for transfers between devices, gather(): lax.all_to_all(jnp.broadcast_to(piece[None], (n, *piece.shape)), axis, 0, 0)  10.4 us
    all_to_all x2, starting transfers between devices, gather(): lax.all_to_all(jnp.broadcast_to(piece[None], (n, *piece.shape)), axis, 0, 0)  9.32 us
    unnamed x12, local copies, waits for them, and re-layouts  7.48 us
  transfers between devices with their start and end apart: 6, of which 6 were waited for; matrix products, arithmetic and copies ran while one was open for 1% of the time, Pallas kernels for 0%

profile of v1, /device:TPU:1, one launch (start us, length us, event | category | flops | bytes accessed | tf_op | source)
XLA Modules:
  0.0 142.0 jit_solution(4728863871501996892)
XLA Ops:
  0.6 0.0 copy-start.4
  0.6 0.0 copy-start.5
  0.7 0.0 copy-start.1
  0.7 0.8 convert_element_type.45
  1.5 0.7 broadcast_in_dim.17
  2.1 5.9 %all-to-all-start.1 = ((bf16[8,64,128]{2,1,0:T(8,128)(2,1)}), bf16[8,64,128]{2,1,0:T(8,128)(2,1)S(1)}, u32[]{:S(2)}, u32[]{:S(2)}) async-start(bf16[8,64,128]{2,1,0:T(8,128)(2,1)} %broadcast_in_dim.17), calls=%async_computation.1 | async-start | bytes 262144 | tf_op jit(solution)/shard_map/all_to_all | solution.py:67
  8.1 0.7 convert_element_type.44
  8.8 4.9 %all-to-all-done.1 = bf16[8,64,128]{2,1,0:T(8,128)(2,1)S(1)} async-done(((bf16[8,64,128]{2,1,0:T(8,128)(2,1)}), bf16[8,64,128]{2,1,0:T(8,128)(2,1)S(1)}, u32[]{:S(2)}, u32[]{:S(2)}) %all-to-all-start.1) | async-done | bytes 131104 | tf_op jit(solution)/shard_map/all_to_all | solution.py:67
  13.7 23.4 %all_to_all.40 = bf16[32,16,128]{2,1,0:T(8,128)(2,1)S(1)} all-to-all(bf16[32,16,128]{2,1,0:T(8,128)(2,1)S(1)} %broadcast_in_dim.16), channel_id=1, replica_groups=mesh['rows'=8,'cols'=32] {'cols'}, dimensions={0} | all-to-all | bytes 262144 | tf_op jit(solution)/shard_map/all_to_all | solution.py:67
  37.1 0.0 copy-start
  37.1 0.7 copy-done
  37.8 0.0 copy-start.2
  37.8 3.4 %copy-done.2 = bf16[512,8192]{1,0:T(8,128)(2,1)S(1)} copy-done((bf16[512,8192]{1,0:T(8,128)(2,1)S(1)}, bf16[512,8192]{1,0:T(8,128)(2,1)}, u32[]{:S(2)}) %copy-start.2) | copy-done | bytes 8388632
  41.2 7.1 %shard_map.67 = (f32[512,128]{1,0:T(8,128)S(1)}, f32[512,128]{1,0:T(8,128)S(1)}, f32[16,128]{1,0:T(8,128)S(1)}) custom-call(bf16[512,8192]{1,0:T(8,128)(2,1)S(1)} %copy-done.2, bf16[512,128]{1,0:T(8,128)(2,1)S(1)} %bitcast.11, bf16[512,128]{1,0:T(8,128)(2,1)S(1)} %bitcast.9, f32[16,128]{1,0:T(8,128)S(1)} %copy-done), custom_call_target="tpu_custom_call" | custom-call | flops 3221225472 | bytes 8388608 | tf_op jit(solution)/shard_map/pallas_call | solution.py:47
  48.3 0.7 pad_maximum_fusion.2
  49.0 3.4 %all-to-all-start.2 = ((bf16[8,80,128]{2,1,0:T(8,128)(2,1)}), bf16[8,80,128]{2,1,0:T(8,128)(2,1)S(1)}, u32[]{:S(2)}, u32[]{:S(2)}) async-start(bf16[8,80,128]{2,1,0:T(8,128)(2,1)} %pad_maximum_fusion.2), calls=%async_computation.2 | async-start | bytes 327680 | tf_op jit(solution)/shard_map/all_to_all | solution.py:76
  52.4 5.8 %all-to-all-done.2 = bf16[8,80,128]{2,1,0:T(8,128)(2,1)S(1)} async-done(((bf16[8,80,128]{2,1,0:T(8,128)(2,1)}), bf16[8,80,128]{2,1,0:T(8,128)(2,1)S(1)}, u32[]{:S(2)}, u32[]{:S(2)}) %all-to-all-start.2) | async-done | bytes 163872 | tf_op jit(solution)/shard_map/all_to_all | solution.py:76
  58.2 0.7 pad_maximum_fusion
  59.0 4.9 %all-to-all-start.3 = ((bf16[32,32,128]{2,1,0:T(8,128)(2,1)}), bf16[32,32,128]{2,1,0:T(8,128)(2,1)S(1)}, u32[]{:S(2)}, u32[]{:S(2)}) async-start(bf16[32,32,128]{2,1,0:T(8,128)(2,1)} %pad_maximum_fusion), calls=%async_computation.3 | async-start | bytes 524288 | tf_op jit(solution)/shard_map/all_to_all | solution.py:76
  63.9 0.0 copy-done.4
  63.9 12.9 %all-to-all-done.3 = bf16[32,32,128]{2,1,0:T(8,128)(2,1)S(1)} async-done(((bf16[32,32,128]{2,1,0:T(8,128)(2,1)}), bf16[32,32,128]{2,1,0:T(8,128)(2,1)S(1)}, u32[]{:S(2)}, u32[]{:S(2)}) %all-to-all-start.3) | async-done | bytes 262176 | tf_op jit(solution)/shard_map/all_to_all | solution.py:76
  76.9 0.7 broadcast_in_dim.21
  77.5 3.4 %all-to-all-start.5 = ((bf16[8,64,128]{2,1,0:T(8,128)(2,1)}), bf16[8,64,128]{2,1,0:T(8,128)(2,1)S(1)}, u32[]{:S(2)}, u32[]{:S(2)}) async-start(bf16[8,64,128]{2,1,0:T(8,128)(2,1)} %broadcast_in_dim.21), calls=%async_computation.5 | async-start | bytes 262144 | tf_op jit(solution)/shard_map/all_to_all | solution.py:67
  80.9 0.0 copy-done.5
  81.0 0.0 copy-done.1
  81.0 5.6 %all-to-all-done.5 = bf16[8,64,128]{2,1,0:T(8,128)(2,1)S(1)} async-done(((bf16[8,64,128]{2,1,0:T(8,128)(2,1)}), bf16[8,64,128]{2,1,0:T(8,128)(2,1)S(1)}, u32[]{:S(2)}, u32[]{:S(2)}) %all-to-all-start.5) | async-done | bytes 131104 | tf_op jit(solution)/shard_map/all_to_all | solution.py:67
  86.6 15.7 %all_to_all.41 = bf16[32,16,128]{2,1,0:T(8,128)(2,1)S(1)} all-to-all(bf16[32,16,128]{2,1,0:T(8,128)(2,1)S(1)} %broadcast_in_dim.20), channel_id=1, replica_groups=mesh['rows'=8,'cols'=32] {'cols'}, dimensions={0} | all-to-all | bytes 262144 | tf_op jit(solution)/shard_map/all_to_all | solution.py:67
  102.3 0.0 copy-start.3
  102.3 3.4 %copy-done.3 = bf16[512,8192]{1,0:T(8,128)(2,1)S(1)} copy-done((bf16[512,8192]{1,0:T(8,128)(2,1)S(1)}, bf16[512,8192]{1,0:T(8,128)(2,1)}, u32[]{:S(2)}) %copy-start.3) | copy-done | bytes 8388632
  105.7 7.1 %shard_map.68 = (f32[512,128]{1,0:T(8,128)S(1)}, f32[512,128]{1,0:T(8,128)S(1)}, f32[16,128]{1,0:T(8,128)S(1)}) custom-call(bf16[512,8192]{1,0:T(8,128)(2,1)S(1)} %copy-done.3, bf16[512,128]{1,0:T(8,128)(2,1)S(1)} %bitcast.10, bf16[512,128]{1,0:T(8,128)(2,1)S(1)} %bitcast.8, f32[16,128]{1,0:T(8,128)S(1)} %get-tuple-element.17.c_ref), custom_call_target="tpu_custom_call" | custom-call | flops 3221225472 | bytes 8388608 | tf_op jit(solution)/shard_map/pallas_call | solution.py:47
  112.8 0.7 pad_maximum_fusion.3
  113.5 3.4 %all-to-all-start.6 = ((bf16[8,80,128]{2,1,0:T(8,128)(2,1)}), bf16[8,80,128]{2,1,0:T(8,128)(2,1)S(1)}, u32[]{:S(2)}, u32[]{:S(2)}) async-start(bf16[8,80,128]{2,1,0:T(8,128)(2,1)} %pad_maximum_fusion.3), calls=%async_computation.6 | async-start | bytes 327680 | tf_op jit(solution)/shard_map/all_to_all | solution.py:76
  116.9 5.8 %all-to-all-done.6 = bf16[8,80,128]{2,1,0:T(8,128)(2,1)S(1)} async-done(((bf16[8,80,128]{2,1,0:T(8,128)(2,1)}), bf16[8,80,128]{2,1,0:T(8,128)(2,1)S(1)}, u32[]{:S(2)}, u32[]{:S(2)}) %all-to-all-start.6) | async-done | bytes 163872 | tf_op jit(solution)/shard_map/all_to_all | solution.py:76
  122.7 0.7 pad_maximum_fusion.1
  123.5 4.9 %all-to-all-start.7 = ((bf16[32,32,128]{2,1,0:T(8,128)(2,1)}), bf16[32,32,128]{2,1,0:T(8,128)(2,1)S(1)}, u32[]{:S(2)}, u32[]{:S(2)}) async-start(bf16[32,32,128]{2,1,0:T(8,128)(2,1)} %pad_maximum_fusion.1), calls=%async_computation.7 | async-start | bytes 524288 | tf_op jit(solution)/shard_map/all_to_all | solution.py:76
  128.4 0.6 fusion
  129.0 12.3 %all-to-all-done.7 = bf16[32,32,128]{2,1,0:T(8,128)(2,1)S(1)} async-done(((bf16[32,32,128]{2,1,0:T(8,128)(2,1)}), bf16[32,32,128]{2,1,0:T(8,128)(2,1)S(1)}, u32[]{:S(2)}, u32[]{:S(2)}) %all-to-all-start.7) | async-done | bytes 262176 | tf_op jit(solution)/shard_map/all_to_all | solution.py:76
  141.4 0.6 fusion.3
  (20 shorter events, 0.3 us)
Async XLA Ops:
  0.6 63.3 %copy-start.4 = (f32[64,128]{1,0:T(8,128)S(1)}, f32[64,128]{1,0:T(8,128)}, u32[]{:S(2)}) copy-start(f32[64,128]{1,0:T(8,128)} %param.6) | copy-start | bytes 98308
  0.6 80.3 %copy-start.5 = (f32[16,128]{1,0:T(8,128)S(1)}, f32[16,128]{1,0:T(8,128)}, u32[]{:S(2)}) copy-start(f32[16,128]{1,0:T(8,128)} %param.5) | copy-start | bytes 24580
  0.7 80.3 %copy-start.1 = (f32[16,128]{1,0:T(8,128)S(1)}, f32[16,128]{1,0:T(8,128)}, u32[]{:S(2)}) copy-start(f32[16,128]{1,0:T(8,128)} %c_ref.1) | copy-start | bytes 24580
  2.1 11.5 %all-to-all-start.1 = ((bf16[8,64,128]{2,1,0:T(8,128)(2,1)}), bf16[8,64,128]{2,1,0:T(8,128)(2,1)S(1)}, u32[]{:S(2)}, u32[]{:S(2)}) async-start(bf16[8,64,128]{2,1,0:T(8,128)(2,1)} %broadcast_in_dim.17), calls=%async_computation.1 | async-start | bytes 262144 | tf_op jit(solution)/shard_map/all_to_all | solution.py:67
  37.1 0.7 copy-start
  37.8 3.4 %copy-start.2 = (bf16[512,8192]{1,0:T(8,128)(2,1)S(1)}, bf16[512,8192]{1,0:T(8,128)(2,1)}, u32[]{:S(2)}) copy-start(bf16[512,8192]{1,0:T(8,128)(2,1)} %n_ref.3) | copy-start | bytes 25165828
  49.0 9.2 %all-to-all-start.2 = ((bf16[8,80,128]{2,1,0:T(8,128)(2,1)}), bf16[8,80,128]{2,1,0:T(8,128)(2,1)S(1)}, u32[]{:S(2)}, u32[]{:S(2)}) async-start(bf16[8,80,128]{2,1,0:T(8,128)(2,1)} %pad_maximum_fusion.2), calls=%async_computation.2 | async-start | bytes 327680 | tf_op jit(solution)/shard_map/all_to_all | solution.py:76
  59.0 17.9 %all-to-all-start.3 = ((bf16[32,32,128]{2,1,0:T(8,128)(2,1)}), bf16[32,32,128]{2,1,0:T(8,128)(2,1)S(1)}, u32[]{:S(2)}, u32[]{:S(2)}) async-start(bf16[32,32,128]{2,1,0:T(8,128)(2,1)} %pad_maximum_fusion), calls=%async_computation.3 | async-start | bytes 524288 | tf_op jit(solution)/shard_map/all_to_all | solution.py:76
  77.5 9.0 %all-to-all-start.5 = ((bf16[8,64,128]{2,1,0:T(8,128)(2,1)}), bf16[8,64,128]{2,1,0:T(8,128)(2,1)S(1)}, u32[]{:S(2)}, u32[]{:S(2)}) async-start(bf16[8,64,128]{2,1,0:T(8,128)(2,1)} %broadcast_in_dim.21), calls=%async_computation.5 | async-start | bytes 262144 | tf_op jit(solution)/shard_map/all_to_all | solution.py:67
  102.3 3.4 %copy-start.3 = (bf16[512,8192]{1,0:T(8,128)(2,1)S(1)}, bf16[512,8192]{1,0:T(8,128)(2,1)}, u32[]{:S(2)}) copy-start(bf16[512,8192]{1,0:T(8,128)(2,1)} %n_ref.3) | copy-start | bytes 25165828
  113.5 9.2 %all-to-all-start.6 = ((bf16[8,80,128]{2,1,0:T(8,128)(2,1)}), bf16[8,80,128]{2,1,0:T(8,128)(2,1)S(1)}, u32[]{:S(2)}, u32[]{:S(2)}) async-start(bf16[8,80,128]{2,1,0:T(8,128)(2,1)} %pad_maximum_fusion.3), calls=%async_computation.6 | async-start | bytes 327680 | tf_op jit(solution)/shard_map/all_to_all | solution.py:76
  123.5 17.9 %all-to-all-start.7 = ((bf16[32,32,128]{2,1,0:T(8,128)(2,1)}), bf16[32,32,128]{2,1,0:T(8,128)(2,1)S(1)}, u32[]{:S(2)}, u32[]{:S(2)}) async-start(bf16[32,32,128]{2,1,0:T(8,128)(2,1)} %pad_maximum_fusion.1), calls=%async_computation.7 | async-start | bytes 524288 | tf_op jit(solution)/shard_map/all_to_all | solution.py:76

commit v2 on v1

v2 whole, which is shorter than its diff:
```python
import functools
import math

import jax
import jax.numpy as jnp
from jax import lax
from jax.experimental import pallas as pl
from jax.experimental.pallas import tpu as pltpu
from jax.sharding import PartitionSpec as P

ITERS = 2
BF16 = jnp.bfloat16
F32 = jnp.float32


def grads_body(last, n_ref, a_ref, *refs):
    b_refs, (c_ref, xa_ref, xb_ref, acc_ref, held_ref, sems) = refs[:-6], refs[-6:]
    depth, rank = c_ref.shape
    flat = n_ref.shape[1]
    blocks = lax.axis_size("rows")
    me = lax.axis_index("rows")
    tile = flat // blocks
    wide = tile // depth

    def fetch(p):
        columns = pl.ds(pl.multiple_of((me ^ p) * tile, tile), tile)
        return pltpu.make_async_copy(n_ref.at[:, columns], held_ref.at[p], sems.at[p])

    for p in range(blocks):
        fetch(p).start()
    low_a = a_ref[...]
    c = c_ref[...]
    acc_ref[...] = jnp.zeros_like(acc_ref)
    grad_c = jnp.zeros((depth, rank), F32)
    for p in range(blocks):
        owner = me ^ p
        level = p.bit_length()
        first = (p - (1 << level >> 1)) * wide if p else 0
        low_b = b_refs[level][first : first + wide].astype(F32)
        scaled = (low_b[:, None, :] * c[None]).astype(BF16).reshape(tile, rank)
        log_rate = lax.dot_general(
            low_a, scaled, (((1,), (1,)), ((), ())), preferred_element_type=F32
        )
        fetch(p).wait()
        residual = (jnp.exp(log_rate) - held_ref[p].astype(F32)).astype(BF16)
        mixed = lax.dot_general(
            residual, low_a, (((0,), (0,)), ((), ())), preferred_element_type=F32
        ).reshape(wide, depth, rank)
        grad_b = jnp.sum(mixed * c[None], axis=1).astype(BF16)
        if last:
            xb_ref[owner, :wide] = grad_b
        else:
            xb_ref[p * wide : (p + 1) * wide] = grad_b
        grad_c = grad_c + jnp.sum(mixed * low_b[:, None, :], axis=0)
        acc_ref[...] += jnp.dot(residual, scaled, preferred_element_type=F32)
    parts, rows = xa_ref.shape[0], low_a.shape[0] // xa_ref.shape[0]
    low_c = grad_c.astype(BF16)
    xa_ref[:, :rows] = acc_ref[...].astype(BF16).reshape(parts, rows, rank)
    if last:
        xb_ref[:, wide:] = jnp.broadcast_to(low_c[None], (blocks, depth, rank))
    else:
        xa_ref[:, rows:] = jnp.broadcast_to(low_c[None], (parts, depth, rank))


def grads(counts, low_a, b_parts, c, last):
    rows, flat = counts.shape
    depth, rank = c.shape
    wide = flat // depth
    blocks, parts = lax.axis_size("rows"), lax.axis_size("cols")
    whole = pl.BlockSpec(memory_space=pltpu.VMEM)
    shape_a = (parts, rows // parts + (0 if last else depth), rank)
    shape_b = (blocks, wide // blocks + depth, rank) if last else (wide, rank)
    return pl.pallas_call(
        functools.partial(grads_body, last),
        in_specs=[pl.BlockSpec(memory_space=pltpu.HBM)] + [whole] * (2 + len(b_parts)),
        out_specs=[whole] * 2,
        out_shape=[
            jax.ShapeDtypeStruct(shape_a, BF16),
            jax.ShapeDtypeStruct(shape_b, BF16),
        ],
        scratch_shapes=[
            pltpu.VMEM((rows, rank), F32),
            pltpu.VMEM((blocks, rows, flat // blocks), BF16),
            pltpu.SemaphoreType.DMA((blocks,)),
        ],
        compiler_params=pltpu.CompilerParams(vmem_limit_bytes=32 << 20),
        cost_estimate=pl.CostEstimate(
            flops=6 * rows * flat * rank,
            transcendentals=rows * flat,
            bytes_accessed=2 * rows * flat,
        ),
    )(counts, low_a, *b_parts, c)


def swap(piece, bit):
    n = lax.axis_size("rows")
    return lax.ppermute(piece, "rows", [(i, i ^ bit) for i in range(n)])


def gather_cols(piece):
    n = lax.axis_size("cols")
    out = lax.all_to_all(jnp.broadcast_to(piece[None], (n, *piece.shape)), "cols", 0, 0)
    return out.reshape(n * piece.shape[0], piece.shape[1])


def exchange(pieces, axis):
    return jnp.sum(lax.all_to_all(pieces, axis, 0, 0).astype(F32), axis=0)


def gather_rows(piece, extra=None):
    held = [piece]
    bit = 1
    while bit < lax.axis_size("rows"):
        held.append(swap(jnp.concatenate(held), bit))
        if extra is not None:
            low = extra.astype(BF16)
            extra = low.astype(F32) + swap(low, bit).astype(F32)
        bit *= 2
    return held, extra


def scatter_rows(whole):
    bit = lax.axis_size("rows") // 2
    while bit:
        half = whole.shape[0] // 2
        got = swap(whole[half:], bit)
        whole = whole[:half].astype(F32) + got.astype(F32)
        if bit > 1:
            whole = whole.astype(BF16)
        bit //= 2
    return whole


def local(counts, start_a, start_b, start_c):
    rows_here, flat_width = counts.shape
    depth = start_c.shape[0]
    cols_here = flat_width // depth
    total_i = rows_here * lax.axis_size("rows")
    total_j = cols_here * lax.axis_size("cols")
    rate_a = 0.3 / math.sqrt(total_j * depth)
    rate_b = 0.3 / math.sqrt(total_i * depth)
    rate_c = 0.3 / math.sqrt(total_i * total_j)
    counts = pltpu.with_memory_space_constraint(counts, pltpu.HBM)
    local_a, local_b, shared_c = (start_a, start_b, start_c)
    part_c = None
    for iteration in range(ITERS):
        last = iteration == ITERS - 1
        low_a = gather_cols(local_a.astype(BF16))
        b_parts, summed_c = gather_rows(local_b.astype(BF16), part_c)
        if summed_c is not None:
            shared_c = shared_c - rate_c * summed_c
        pieces_a, pieces_b = grads(counts, low_a, b_parts, shared_c, last)
        rows_a, rows_b = local_a.shape[0], local_b.shape[0]
        if last:
            total_b = exchange(pieces_b, "rows")
            low_c = jnp.broadcast_to(
                total_b[None, rows_b:].astype(BF16), (pieces_a.shape[0], depth, start_c.shape[1])
            )
            total_a = exchange(jnp.concatenate([pieces_a, low_c], axis=1), "cols")
            local_b = local_b - rate_b * total_b[:rows_b]
            shared_c = shared_c - rate_c * total_a[rows_a:]
        else:
            total_a = exchange(pieces_a, "cols")
            local_b = local_b - rate_b * scatter_rows(pieces_b)
            part_c = total_a[rows_a:]
        local_a = local_a - rate_a * total_a[:rows_a]
    return (local_a, local_b, shared_c)


def solution(mesh):
    placed = (P("rows", "cols"), P(("rows", "cols"), None), P(("cols", "rows"), None), P())
    return jax.shard_map(
        local,
        mesh=mesh,
        in_specs=placed,
        out_specs=(P(("rows", "cols"), None), P(("cols", "rows"), None), P()),
        check_vma=False,
    )
```

time: 143 us -> 127 us (0.89)
  blocking collectives: 39.2 us -> 8.19 us
  starting transfers between devices: 25.9 us -> 52.2 us
  waiting for transfers between devices: 47.2 us -> 40 us
  local copies, waits for them, and re-layouts: 8.9 us -> 2.14 us
  Pallas kernels: 14.2 us -> 19.4 us
  other arithmetic: 5.77 us -> 3.68 us
    all_to_all x2 -> x1, blocking collectives: 39.2 us -> 8.19 us  [exchange(): return jnp.sum(lax.all_to_all(pieces, axis, 0, 0).astype(F32), axis=0)]
    all_to_all x6 -> x4, waiting for transfers between devices: 47.2 us -> 25.6 us  [the longest x2 18.3 us: exchange(): return jnp.sum(lax.all_to_all(pieces, axis, 0, 0).astype(F32), axis=0)]
    ppermute x0 -> x12, starting transfers between devices: none -> 14.5 us  [swap(): return lax.ppermute(piece, 'rows', [(i, i ^ bit) for i in range(n)])]
    ppermute x0 -> x12, waiting for transfers between devices: none -> 14.4 us  [swap(): return lax.ppermute(piece, 'rows', [(i, i ^ bit) for i in range(n)])]
    all_to_all x6 -> x4, starting transfers between devices: 25.9 us -> 37.7 us  [the longest x2 19.5 us: gather_cols(): lax.all_to_all(jnp.broadcast_to(piece[None], (n, *piece.shape)), 'cols',...]
    unnamed x12 -> x8, local copies, waits for them, and re-layouts: 7.48 us -> 0.71 us
    pallas_call x2, Pallas kernels: 14.2 us -> 19.4 us  [grads(): pl.pallas_call(functools.partial(grads_body, last), in_specs=[pl.BlockSpe...]
    concatenate x4 -> x5, other arithmetic: 2.8 us -> 0.75 us  [the longest x1 0.73 us: local(): total_a = exchange(jnp.concatenate([pieces_a, low_c], axis=1), 'cols')]
  transfers between devices with their start and end apart: 6 -> 16, of which waited for: 6 -> 11; matrix products, arithmetic and copies ran while one was open for 1% -> 2% of each run, Pallas kernels for 0% -> 0%
where the time goes in v2:
time: 127 us; the launch traced here: 126 us
  starting transfers between devices  52.2 us (41%)
  waiting for transfers between devices  40 us (31%)
  Pallas kernels  19.4 us (15%)
  blocking collectives  8.19 us (6%)
  other arithmetic  3.68 us (3%)
  local copies, waits for them, and re-layouts  2.14 us (2%)
    all_to_all x2, starting transfers between devices, gather_cols(): lax.all_to_all(jnp.broadcast_to(piece[None], (n, *piece.shape)), 'cols',...  19.5 us
    pallas_call x2, Pallas kernels, grads(): pl.pallas_call(functools.partial(grads_body, last), in_specs=[pl.BlockSpe...  19.4 us
    all_to_all x2, waiting for transfers between devices, exchange(): return jnp.sum(lax.all_to_all(pieces, axis, 0, 0).astype(F32), axis=0)  18.3 us
    all_to_all x2, starting transfers between devices, exchange(): return jnp.sum(lax.all_to_all(pieces, axis, 0, 0).astype(F32), axis=0)  18.2 us
    ppermute x12, starting transfers between devices, swap(): return lax.ppermute(piece, 'rows', [(i, i ^ bit) for i in range(n)])  14.5 us
    ppermute x12, waiting for transfers between devices, swap(): return lax.ppermute(piece, 'rows', [(i, i ^ bit) for i in range(n)])  14.4 us
    all_to_all x1, blocking collectives, exchange(): return jnp.sum(lax.all_to_all(pieces, axis, 0, 0).astype(F32), axis=0)  8.19 us
    all_to_all x2, waiting for transfers between devices, gather_cols(): lax.all_to_all(jnp.broadcast_to(piece[None], (n, *piece.shape)), 'cols',...  7.32 us
  transfers between devices with their start and end apart: 16, of which 11 were waited for; matrix products, arithmetic and copies ran while one was open for 2% of the time, Pallas kernels for 0%

profile of v2, /device:TPU:1, one launch (start us, length us, event | category | flops | bytes accessed | tf_op | source)
XLA Modules:
  0.0 126.5 jit_solution(10837508495607281791)
XLA Ops:
  0.6 0.0 copy-start.2
  0.6 0.0 copy-start.3
  0.7 0.0 copy-start.1
  0.7 0.8 convert_element_type.73.refs_0_
  1.5 2.0 %collective-permute-start = (bf16[64,128]{1,0:T(8,128)(2,1)S(1)}, bf16[64,128]{1,0:T(8,128)(2,1)S(1)}, u32[]{:S(2)}, u32[]{:S(2)}) collective-permute-start(bf16[64,128]{1,0:T(8,128)(2,1)S(1)} %convert_element_type.73.refs_0_), channel_id=1, source_target_pairs={{0,32},{32,0},{64,96},{96,64},{128,160},{160,128},{192,224},{224,1... | collective-permute-start | bytes 49160 | tf_op jit(solution)/shard_map/ppermute | solution.py:97
  3.5 0.7 convert_element_type.72
  4.2 0.7 broadcast_in_dim.6
  4.9 11.7 %all-to-all-start = ((bf16[32,16,128]{2,1,0:T(8,128)(2,1)}), bf16[32,16,128]{2,1,0:T(8,128)(2,1)S(1)}, u32[]{:S(2)}, u32[]{:S(2)}) async-start(bf16[32,16,128]{2,1,0:T(8,128)(2,1)} %broadcast_in_dim.6), calls=%async_computation | async-start | bytes 262144 | tf_op jit(solution)/shard_map/all_to_all | solution.py:102
  16.6 0.0 collective-permute-done.refs_1_
  16.7 1.4 %collective-permute-start.1 = (bf16[128,128]{1,0:T(8,128)(2,1)S(1)}, bf16[128,128]{1,0:T(8,128)(2,1)S(1)}, u32[]{:S(2)}, u32[]{:S(2)}) collective-permute-start(bf16[128,128]{1,0:T(8,128)(2,1)S(1)} %pad_maximum_fusion.3), channel_id=1, source_target_pairs={{0,64},{32,96},{64,0},{96,32},{128,192},{160,224},{192,128},{224,1... | collective-permute-start | bytes 98312 | tf_op jit(solution)/shard_map/ppermute | solution.py:97
  18.1 1.5 %collective-permute-done.1.refs_2_ = bf16[128,128]{1,0:T(8,128)(2,1)S(1)} collective-permute-done((bf16[128,128]{1,0:T(8,128)(2,1)S(1)}, bf16[128,128]{1,0:T(8,128)(2,1)S(1)}, u32[]{:S(2)}, u32[]{:S(2)}) %collective-permute-start.1) | collective-permute-done | bytes 32800 | tf_op jit(solution)/shard_map/ppermute | solution.py:97
  19.6 2.9 %collective-permute-start.2 = (bf16[256,128]{1,0:T(8,128)(2,1)S(1)}, bf16[256,128]{1,0:T(8,128)(2,1)S(1)}, u32[]{:S(2)}, u32[]{:S(2)}) collective-permute-start(bf16[256,128]{1,0:T(8,128)(2,1)S(1)} %pad_maximum_fusion.1), channel_id=1, source_target_pairs={{0,128},{32,160},{64,192},{96,224},{128,0},{160,32},{192,64},{224,... | collective-permute-start | bytes 196616 | tf_op jit(solution)/shard_map/ppermute | solution.py:97
  22.5 2.0 %collective-permute-done.2.refs_3_ = bf16[256,128]{1,0:T(8,128)(2,1)S(1)} collective-permute-done((bf16[256,128]{1,0:T(8,128)(2,1)S(1)}, bf16[256,128]{1,0:T(8,128)(2,1)S(1)}, u32[]{:S(2)}, u32[]{:S(2)}) %collective-permute-start.2) | collective-permute-done | bytes 65568 | tf_op jit(solution)/shard_map/ppermute | solution.py:97
  24.5 2.9 %all-to-all-done = bf16[32,16,128]{2,1,0:T(8,128)(2,1)S(1)} async-done(((bf16[32,16,128]{2,1,0:T(8,128)(2,1)}), bf16[32,16,128]{2,1,0:T(8,128)(2,1)S(1)}, u32[]{:S(2)}, u32[]{:S(2)}) %all-to-all-start) | async-done | bytes 131104 | tf_op jit(solution)/shard_map/all_to_all | solution.py:102
  27.4 0.0 copy-start
  27.4 0.7 copy-done
  28.1 10.0 %shard_map.67 = (bf16[32,32,128]{2,1,0:T(8,128)(2,1)}, bf16[512,128]{1,0:T(8,128)(2,1)S(1)}) custom-call(bf16[512,8192]{1,0:T(8,128)(2,1)} %n_ref.3, bf16[512,128]{1,0:T(8,128)(2,1)S(1)} %bitcast.3, bf16[64,128]{1,0:T(8,128)(2,1)S(1)} %convert_element_type.73.refs_0_, bf16[64,128]{1,0:T(8,128)(2,1)S(1)} %collective-permute-done.refs_1_, ...), custom_call_target="tpu_custom_call" | custom-call | flops 3221225472 | bytes 8388608 | tf_op jit(solution)/shard_map/pallas_call | solution.py:73
  38.2 3.0 %collective-permute-start.3 = (bf16[256,128]{1,0:T(8,128)(2,1)S(1)}, bf16[256,128]{1,0:T(8,128)(2,1)S(1)}, u32[]{:S(2)}, u32[]{:S(2)}) collective-permute-start(bf16[256,128]{1,0:T(8,128)(2,1)S(1)} %slice.40), channel_id=1, source_target_pairs={{0,128},{32,160},{64,192},{96,224},{128,0},{160,32},{192,64},{224,... | collective-permute-start | bytes 196616 | tf_op jit(solution)/shard_map/ppermute | solution.py:97
  41.2 9.1 %all-to-all-start.1 = ((bf16[32,32,128]{2,1,0:T(8,128)(2,1)}), bf16[32,32,128]{2,1,0:T(8,128)(2,1)S(1)}, u32[]{:S(2)}, u32[]{:S(2)}) async-start(bf16[32,32,128]{2,1,0:T(8,128)(2,1)} %get-tuple-element.7), calls=%async_computation.1 | async-start | bytes 524288 | tf_op jit(solution)/shard_map/all_to_all | solution.py:107
  50.3 0.0 collective-permute-done.3
  50.3 0.7 collective-permute-start.4
  51.0 2.7 %collective-permute-done.4 = bf16[128,128]{1,0:T(8,128)(2,1)S(1)} collective-permute-done((bf16[128,128]{1,0:T(8,128)(2,1)S(1)}, bf16[128,128]{1,0:T(8,128)(2,1)S(1)}, u32[]{:S(2)}, u32[]{:S(2)}) %collective-permute-start.4) | collective-permute-done | bytes 32800 | tf_op jit(solution)/shard_map/ppermute | solution.py:97
  53.7 0.1 collective-permute-start.5
  53.8 3.3 %collective-permute-done.5 = bf16[64,128]{1,0:T(8,128)(2,1)S(1)} collective-permute-done((bf16[64,128]{1,0:T(8,128)(2,1)S(1)}, bf16[64,128]{1,0:T(8,128)(2,1)S(1)}, u32[]{:S(2)}, u32[]{:S(2)}) %collective-permute-start.5) | collective-permute-done | bytes 16416 | tf_op jit(solution)/shard_map/ppermute | solution.py:97
  57.1 0.0 copy-done.2
  57.1 0.1 collective-permute-start.6
  57.2 6.0 %all-to-all-done.1 = bf16[32,32,128]{2,1,0:T(8,128)(2,1)S(1)} async-done(((bf16[32,32,128]{2,1,0:T(8,128)(2,1)}), bf16[32,32,128]{2,1,0:T(8,128)(2,1)S(1)}, u32[]{:S(2)}, u32[]{:S(2)}) %all-to-all-start.1) | async-done | bytes 262176 | tf_op jit(solution)/shard_map/all_to_all | solution.py:107
  63.3 0.1 collective-permute-start.9
  63.4 0.0 collective-permute-done.6.refs_1_
  63.4 0.5 collective-permute-start.7
  63.9 1.9 %collective-permute-done.9 = bf16[16,128]{1,0:T(8,128)(2,1)S(1)} collective-permute-done((bf16[16,128]{1,0:T(8,128)(2,1)S(1)}, bf16[16,128]{1,0:T(8,128)(2,1)S(1)}, u32[]{:S(2)}, u32[]{:S(2)}) %collective-permute-start.9) | collective-permute-done | bytes 4128 | tf_op jit(solution)/shard_map/ppermute | solution.py:97
  65.8 0.4 collective-permute-start.10
  66.2 0.0 copy-done.3
  66.2 0.7 broadcast_in_dim.7
  66.9 7.8 %all-to-all-start.2 = ((bf16[32,16,128]{2,1,0:T(8,128)(2,1)}), bf16[32,16,128]{2,1,0:T(8,128)(2,1)S(1)}, u32[]{:S(2)}, u32[]{:S(2)}) async-start(bf16[32,16,128]{2,1,0:T(8,128)(2,1)} %broadcast_in_dim.7), calls=%async_computation.2 | async-start | bytes 262144 | tf_op jit(solution)/shard_map/all_to_all | solution.py:102
  74.7 0.0 collective-permute-done.10
  74.7 1.1 collective-permute-start.11
  75.9 0.0 collective-permute-done.7.refs_2_
  75.9 2.2 %collective-permute-start.8 = (bf16[256,128]{1,0:T(8,128)(2,1)S(1)}, bf16[256,128]{1,0:T(8,128)(2,1)S(1)}, u32[]{:S(2)}, u32[]{:S(2)}) collective-permute-start(bf16[256,128]{1,0:T(8,128)(2,1)S(1)} %pad_maximum_fusion.2), channel_id=1, source_target_pairs={{0,128},{32,160},{64,192},{96,224},{128,0},{160,32},{192,64},{224,... | collective-permute-start | bytes 196616 | tf_op jit(solution)/shard_map/ppermute | solution.py:97
  78.1 0.9 collective-permute-done.11
  79.0 0.0 copy-done.1
  79.0 2.1 %collective-permute-done.8.refs_3_ = bf16[256,128]{1,0:T(8,128)(2,1)S(1)} collective-permute-done((bf16[256,128]{1,0:T(8,128)(2,1)S(1)}, bf16[256,128]{1,0:T(8,128)(2,1)S(1)}, u32[]{:S(2)}, u32[]{:S(2)}) %collective-permute-start.8) | collective-permute-done | bytes 65568 | tf_op jit(solution)/shard_map/ppermute | solution.py:97
  81.1 4.4 %all-to-all-done.2 = bf16[32,16,128]{2,1,0:T(8,128)(2,1)S(1)} async-done(((bf16[32,16,128]{2,1,0:T(8,128)(2,1)}), bf16[32,16,128]{2,1,0:T(8,128)(2,1)S(1)}, u32[]{:S(2)}, u32[]{:S(2)}) %all-to-all-start.2) | async-done | bytes 131104 | tf_op jit(solution)/shard_map/all_to_all | solution.py:102
  85.5 9.3 %shard_map.68 = (bf16[32,16,128]{2,1,0:T(8,128)(2,1)S(1)}, bf16[8,80,128]{2,1,0:T(8,128)(2,1)S(1)}) custom-call(bf16[512,8192]{1,0:T(8,128)(2,1)} %n_ref.3, bf16[512,128]{1,0:T(8,128)(2,1)S(1)} %bitcast.2, bf16[64,128]{1,0:T(8,128)(2,1)S(1)} %fusion.1.refs_0_, bf16[64,128]{1,0:T(8,128)(2,1)S(1)} %collective-permute-done.6.refs_1_, ...), custom_call_target="tpu_custom_call" | custom-call | flops 3221225472 | bytes 8388608 | tf_op jit(solution)/shard_map/pallas_call | solution.py:73
  94.8 8.2 %all_to_all.25 = bf16[8,80,128]{2,1,0:T(8,128)(2,1)S(1)} all-to-all(bf16[8,80,128]{2,1,0:T(8,128)(2,1)S(1)} %get-tuple-element.10), channel_id=1, replica_groups=mesh['rows'=8,'cols'=32] {'rows'}, dimensions={0} | all-to-all | bytes 327680 | tf_op jit(solution)/shard_map/all_to_all | solution.py:107
  103.1 0.7 pad_maximum_fusion
  103.8 9.1 %all-to-all-start.4 = ((bf16[32,32,128]{2,1,0:T(8,128)(2,1)}), bf16[32,32,128]{2,1,0:T(8,128)(2,1)S(1)}, u32[]{:S(2)}, u32[]{:S(2)}) async-start(bf16[32,32,128]{2,1,0:T(8,128)(2,1)} %pad_maximum_fusion), calls=%async_computation.4 | async-start | bytes 524288 | tf_op jit(solution)/shard_map/all_to_all | solution.py:107
  112.9 0.6 fusion
  113.5 12.3 %all-to-all-done.4 = bf16[32,32,128]{2,1,0:T(8,128)(2,1)S(1)} async-done(((bf16[32,32,128]{2,1,0:T(8,128)(2,1)}), bf16[32,32,128]{2,1,0:T(8,128)(2,1)S(1)}, u32[]{:S(2)}, u32[]{:S(2)}) %all-to-all-start.4) | async-done | bytes 262176 | tf_op jit(solution)/shard_map/all_to_all | solution.py:107
  125.9 0.6 fusion.2
  (20 shorter events, 0.3 us)
Async XLA Ops:
  0.6 56.4 %copy-start.2 = (f32[64,128]{1,0:T(8,128)S(1)}, f32[64,128]{1,0:T(8,128)}, u32[]{:S(2)}) copy-start(f32[64,128]{1,0:T(8,128)} %param.6) | copy-start | bytes 98308
  0.6 65.6 %copy-start.3 = (f32[16,128]{1,0:T(8,128)S(1)}, f32[16,128]{1,0:T(8,128)}, u32[]{:S(2)}) copy-start(f32[16,128]{1,0:T(8,128)} %param.5) | copy-start | bytes 24580
  0.7 78.3 %copy-start.1 = (f32[16,128]{1,0:T(8,128)S(1)}, f32[16,128]{1,0:T(8,128)}, u32[]{:S(2)}) copy-start(f32[16,128]{1,0:T(8,128)} %refs_4_.1) | copy-start | bytes 24580
  1.5 15.2 %collective-permute-start = (bf16[64,128]{1,0:T(8,128)(2,1)S(1)}, bf16[64,128]{1,0:T(8,128)(2,1)S(1)}, u32[]{:S(2)}, u32[]{:S(2)}) collective-permute-start(bf16[64,128]{1,0:T(8,128)(2,1)S(1)} %convert_element_type.73.refs_0_), channel_id=1, source_target_pairs={{0,32},{32,0},{64,96},{96,64},{128,160},{160,128},{192,224},{224,1... | collective-permute-start | bytes 49160 | tf_op jit(solution)/shard_map/ppermute | solution.py:97
  4.9 22.5 %all-to-all-start = ((bf16[32,16,128]{2,1,0:T(8,128)(2,1)}), bf16[32,16,128]{2,1,0:T(8,128)(2,1)S(1)}, u32[]{:S(2)}, u32[]{:S(2)}) async-start(bf16[32,16,128]{2,1,0:T(8,128)(2,1)} %broadcast_in_dim.6), calls=%async_computation | async-start | bytes 262144 | tf_op jit(solution)/shard_map/all_to_all | solution.py:102
  16.7 2.9 %collective-permute-start.1 = (bf16[128,128]{1,0:T(8,128)(2,1)S(1)}, bf16[128,128]{1,0:T(8,128)(2,1)S(1)}, u32[]{:S(2)}, u32[]{:S(2)}) collective-permute-start(bf16[128,128]{1,0:T(8,128)(2,1)S(1)} %pad_maximum_fusion.3), channel_id=1, source_target_pairs={{0,64},{32,96},{64,0},{96,32},{128,192},{160,224},{192,128},{224,1... | collective-permute-start | bytes 98312 | tf_op jit(solution)/shard_map/ppermute | solution.py:97
  19.6 4.9 %collective-permute-start.2 = (bf16[256,128]{1,0:T(8,128)(2,1)S(1)}, bf16[256,128]{1,0:T(8,128)(2,1)S(1)}, u32[]{:S(2)}, u32[]{:S(2)}) collective-permute-start(bf16[256,128]{1,0:T(8,128)(2,1)S(1)} %pad_maximum_fusion.1), channel_id=1, source_target_pairs={{0,128},{32,160},{64,192},{96,224},{128,0},{160,32},{192,64},{224,... | collective-permute-start | bytes 196616 | tf_op jit(solution)/shard_map/ppermute | solution.py:97
  27.4 0.7 copy-start
  38.2 12.1 %collective-permute-start.3 = (bf16[256,128]{1,0:T(8,128)(2,1)S(1)}, bf16[256,128]{1,0:T(8,128)(2,1)S(1)}, u32[]{:S(2)}, u32[]{:S(2)}) collective-permute-start(bf16[256,128]{1,0:T(8,128)(2,1)S(1)} %slice.40), channel_id=1, source_target_pairs={{0,128},{32,160},{64,192},{96,224},{128,0},{160,32},{192,64},{224,... | collective-permute-start | bytes 196616 | tf_op jit(solution)/shard_map/ppermute | solution.py:97
  41.2 22.0 %all-to-all-start.1 = ((bf16[32,32,128]{2,1,0:T(8,128)(2,1)}), bf16[32,32,128]{2,1,0:T(8,128)(2,1)S(1)}, u32[]{:S(2)}, u32[]{:S(2)}) async-start(bf16[32,32,128]{2,1,0:T(8,128)(2,1)} %get-tuple-element.7), calls=%async_computation.1 | async-start | bytes 524288 | tf_op jit(solution)/shard_map/all_to_all | solution.py:107
  50.3 3.3 %collective-permute-start.4 = (bf16[128,128]{1,0:T(8,128)(2,1)S(1)}, bf16[128,128]{1,0:T(8,128)(2,1)S(1)}, u32[]{:S(2)}, u32[]{:S(2)}) collective-permute-start(bf16[128,128]{1,0:T(8,128)(2,1)S(1)} %slice.52), channel_id=1, source_target_pairs={{0,64},{32,96},{64,0},{96,32},{128,192},{160,224},{192,128},{224,1... | collective-permute-start | bytes 98312 | tf_op jit(solution)/shard_map/ppermute | solution.py:97
  53.7 3.4 %collective-permute-start.5 = (bf16[64,128]{1,0:T(8,128)(2,1)S(1)}, bf16[64,128]{1,0:T(8,128)(2,1)S(1)}, u32[]{:S(2)}, u32[]{:S(2)}) collective-permute-start(bf16[64,128]{1,0:T(8,128)(2,1)S(1)} %slice.54), channel_id=1, source_target_pairs={{0,32},{32,0},{64,96},{96,64},{128,160},{160,128},{192,224},{224,1... | collective-permute-start | bytes 49160 | tf_op jit(solution)/shard_map/ppermute | solution.py:97
  57.1 6.3 %collective-permute-start.6 = (bf16[64,128]{1,0:T(8,128)(2,1)S(1)}, bf16[64,128]{1,0:T(8,128)(2,1)S(1)}, u32[]{:S(2)}, u32[]{:S(2)}) collective-permute-start(bf16[64,128]{1,0:T(8,128)(2,1)S(1)} %fusion.1.refs_0_), channel_id=1, source_target_pairs={{0,32},{32,0},{64,96},{96,64},{128,160},{160,128},{192,224},{224,1... | collective-permute-start | bytes 49160 | tf_op jit(solution)/shard_map/ppermute | solution.py:97
  63.3 2.5 %collective-permute-start.9 = (bf16[16,128]{1,0:T(8,128)(2,1)S(1)}, bf16[16,128]{1,0:T(8,128)(2,1)S(1)}, u32[]{:S(2)}, u32[]{:S(2)}) collective-permute-start(bf16[16,128]{1,0:T(8,128)(2,1)S(1)} %slice.86), channel_id=1, source_target_pairs={{0,32},{32,0},{64,96},{96,64},{128,160},{160,128},{192,224},{224,1... | collective-permute-start | bytes 12296 | tf_op jit(solution)/shard_map/ppermute | solution.py:97
  63.4 12.5 %collective-permute-start.7 = (bf16[128,128]{1,0:T(8,128)(2,1)S(1)}, bf16[128,128]{1,0:T(8,128)(2,1)S(1)}, u32[]{:S(2)}, u32[]{:S(2)}) collective-permute-start(bf16[128,128]{1,0:T(8,128)(2,1)S(1)} %pad_maximum_fusion.4), channel_id=1, source_target_pairs={{0,64},{32,96},{64,0},{96,32},{128,192},{160,224},{192,128},{224,1... | collective-permute-start | bytes 98312 | tf_op jit(solution)/shard_map/ppermute | solution.py:97
  65.8 8.9 %collective-permute-start.10 = (bf16[16,128]{1,0:T(8,128)(2,1)S(1)}, bf16[16,128]{1,0:T(8,128)(2,1)S(1)}, u32[]{:S(2)}, u32[]{:S(2)}) collective-permute-start(bf16[16,128]{1,0:T(8,128)(2,1)S(1)} %add_convert_fusion.3), channel_id=1, source_target_pairs={{0,64},{32,96},{64,0},{96,32},{128,192},{160,224},{192,128},{224,1... | collective-permute-start | bytes 12296 | tf_op jit(solution)/shard_map/ppermute | solution.py:97
  66.9 18.6 %all-to-all-start.2 = ((bf16[32,16,128]{2,1,0:T(8,128)(2,1)}), bf16[32,16,128]{2,1,0:T(8,128)(2,1)S(1)}, u32[]{:S(2)}, u32[]{:S(2)}) async-start(bf16[32,16,128]{2,1,0:T(8,128)(2,1)} %broadcast_in_dim.7), calls=%async_computation.2 | async-start | bytes 262144 | tf_op jit(solution)/shard_map/all_to_all | solution.py:102
  74.7 4.2 %collective-permute-start.11 = (bf16[16,128]{1,0:T(8,128)(2,1)S(1)}, bf16[16,128]{1,0:T(8,128)(2,1)S(1)}, u32[]{:S(2)}, u32[]{:S(2)}) collective-permute-start(bf16[16,128]{1,0:T(8,128)(2,1)S(1)} %add_convert_fusion.2), channel_id=1, source_target_pairs={{0,128},{32,160},{64,192},{96,224},{128,0},{160,32},{192,64},{224,... | collective-permute-start | bytes 12296 | tf_op jit(solution)/shard_map/ppermute | solution.py:97
  75.9 5.2 %collective-permute-start.8 = (bf16[256,128]{1,0:T(8,128)(2,1)S(1)}, bf16[256,128]{1,0:T(8,128)(2,1)S(1)}, u32[]{:S(2)}, u32[]{:S(2)}) collective-permute-start(bf16[256,128]{1,0:T(8,128)(2,1)S(1)} %pad_maximum_fusion.2), channel_id=1, source_target_pairs={{0,128},{32,160},{64,192},{96,224},{128,0},{160,32},{192,64},{224,... | collective-permute-start | bytes 196616 | tf_op jit(solution)/shard_map/ppermute | solution.py:97
  103.8 22.0 %all-to-all-start.4 = ((bf16[32,32,128]{2,1,0:T(8,128)(2,1)}), bf16[32,32,128]{2,1,0:T(8,128)(2,1)S(1)}, u32[]{:S(2)}, u32[]{:S(2)}) async-start(bf16[32,32,128]{2,1,0:T(8,128)(2,1)} %pad_maximum_fusion), calls=%async_computation.4 | async-start | bytes 524288 | tf_op jit(solution)/shard_map/all_to_all | solution.py:107

commit v3 on v0

v3 whole, which is shorter than its diff:
```python
import functools
import math

import jax
import jax.numpy as jnp
from jax import lax
from jax.experimental import pallas as pl
from jax.experimental.pallas import tpu as pltpu
from jax.sharding import PartitionSpec as P

ITERS = 2
BF16 = jnp.bfloat16
F32 = jnp.float32
IN_FLIGHT = 3
WHOLE = pl.BlockSpec(memory_space=pltpu.VMEM)


def prepare_body(a_ref, b_ref, c_ref, copies_ref, low_b_ref, held_c_ref, a_buf, b_buf, sems):
    into = ((a_ref, a_buf), (b_ref, b_buf), (c_ref, held_c_ref))
    moves = [pltpu.make_async_copy(src, dst, sems.at[k]) for k, (src, dst) in enumerate(into)]
    for move in moves:
        move.start()
    moves[1].wait()
    low_b_ref[...] = b_buf[...].astype(BF16)
    moves[0].wait()
    copies_ref[...] = jnp.broadcast_to(a_buf[...].astype(BF16)[None], copies_ref.shape)
    moves[2].wait()


def prepare(a, b, c):
    operands = [pltpu.with_memory_space_constraint(x, pltpu.HBM) for x in (a, b, c)]
    return pl.pallas_call(
        prepare_body,
        in_specs=[pl.BlockSpec(memory_space=pltpu.HBM)] * 3,
        out_specs=[WHOLE] * 3,
        out_shape=[
            jax.ShapeDtypeStruct((lax.axis_size("cols"), *a.shape), BF16),
            jax.ShapeDtypeStruct(b.shape, BF16),
            jax.ShapeDtypeStruct(c.shape, F32),
        ],
        scratch_shapes=[
            pltpu.VMEM(a.shape, F32),
            pltpu.VMEM(b.shape, F32),
            pltpu.SemaphoreType.DMA((3,)),
        ],
        compiler_params=pltpu.CompilerParams(vmem_limit_bytes=2 << 20),
    )(*operands)


def visit_blocks(order, n_ref, held_ref, sems, low_a, b_of, c, put_b, acc_ref, grad_c):
    depth, rank = c.shape
    blocks = lax.axis_size("rows")
    me = lax.axis_index("rows")
    tile = n_ref.shape[1] // blocks
    wide = tile // depth

    def fetch(k):
        columns = pl.ds(pl.multiple_of((me ^ order[k]) * tile, tile), tile)
        return pltpu.make_async_copy(n_ref.at[:, columns], held_ref.at[k], sems.at[k])

    for k in range(min(IN_FLIGHT, len(order))):
        fetch(k).start()
    for k, p in enumerate(order):
        low_b = b_of(p).astype(F32)
        scaled = (low_b[:, None, :] * c[None]).astype(BF16).reshape(tile, rank)
        log_rate = lax.dot_general(
            low_a, scaled, (((1,), (1,)), ((), ())), preferred_element_type=F32
        )
        fetch(k).wait()
        if k + IN_FLIGHT < len(order):
            fetch(k + IN_FLIGHT).start()
        residual = (jnp.exp(log_rate) - held_ref[k].astype(F32)).astype(BF16)
        mixed = lax.dot_general(
            residual, low_a, (((0,), (0,)), ((), ())), preferred_element_type=F32
        ).reshape(wide, depth, rank)
        put_b(p, jnp.sum(mixed * c[None], axis=1).astype(BF16))
        grad_c = grad_c + jnp.sum(mixed * low_b[:, None, :], axis=0)
        acc_ref[...] += jnp.dot(residual, scaled, preferred_element_type=F32)
    return grad_c


def parts_of(b_refs, wide):
    def b_of(p):
        level = p.bit_length()
        start = (p - (1 << level >> 1)) * wide
        return b_refs[level][start : start + wide]

    return b_of


def first_body(n_ref, a_ref, *refs):
    b_refs, (c_ref, xa_ref, near_ref, far_ref, acc_ref, held_ref, sems) = refs[:-7], refs[-7:]
    blocks = lax.axis_size("rows")
    half = near_ref.shape[0]
    wide = 2 * half // blocks

    def put_b(p, value):
        at = p * wide % half
        (near_ref if p < blocks // 2 else far_ref)[at : at + wide] = value

    low_a = a_ref[...].reshape(acc_ref.shape)
    acc_ref[...] = jnp.zeros_like(acc_ref)
    b_of = parts_of(b_refs, wide)
    grad_c = jnp.zeros(c_ref.shape, F32)
    grad_c = visit_blocks(
        range(blocks), n_ref, held_ref, sems, low_a, b_of, c_ref[...], put_b, acc_ref, grad_c
    )
    xa_ref[...] = acc_ref[...].astype(BF16).reshape(xa_ref.shape)
    far_ref[half:] = grad_c.astype(BF16)


def last_body(rate_c, n_ref, a_ref, *refs):
    b_refs, (c_ref, xa_ref, xb_ref, new_c_ref, acc_ref, held_ref, sems) = refs[:-7], refs[-7:]
    depth, rank = c_ref.shape
    blocks = lax.axis_size("rows")
    me = lax.axis_index("rows")
    wide = xb_ref.shape[1] - depth
    parts, rows, _ = xa_ref.shape

    def put_b(p, value):
        xb_ref[me ^ p, :wide] = value

    acc_ref[...] = jnp.zeros_like(acc_ref)
    low_a = a_ref[:, :rows].reshape(acc_ref.shape)
    c = c_ref[...] - rate_c * jnp.sum(a_ref[:, rows:].astype(F32), axis=0)
    new_c_ref[...] = c
    b_of = parts_of(b_refs, wide)
    grad_c = jnp.zeros(c.shape, F32)
    grad_c = visit_blocks(
        range(blocks), n_ref, held_ref, sems, low_a, b_of, c, put_b, acc_ref, grad_c
    )
    xa_ref[...] = acc_ref[...].astype(BF16).reshape(xa_ref.shape)
    xb_ref[:, wide:] = jnp.broadcast_to(grad_c.astype(BF16)[None], (blocks, depth, rank))


def call(body, counts, operands, outs):
    rows, flat = counts.shape
    rank = operands[0].shape[-1]
    blocks = lax.axis_size("rows")
    return pl.pallas_call(
        body,
        in_specs=[pl.BlockSpec(memory_space=pltpu.HBM)] + [WHOLE] * len(operands),
        out_specs=[WHOLE] * len(outs),
        out_shape=[jax.ShapeDtypeStruct(shape, dtype) for shape, dtype in outs],
        scratch_shapes=[
            pltpu.VMEM((rows, rank), F32),
            pltpu.VMEM((blocks, rows, flat // blocks), BF16),
            pltpu.SemaphoreType.DMA((blocks,)),
        ],
        compiler_params=pltpu.CompilerParams(vmem_limit_bytes=32 << 20),
        cost_estimate=pl.CostEstimate(
            flops=6 * rows * flat * rank,
            transcendentals=rows * flat,
            bytes_accessed=2 * rows * flat,
        ),
    )(counts, *operands)


def swap(piece, bit):
    n = lax.axis_size("rows")
    return lax.ppermute(piece, "rows", [(i, i ^ bit) for i in range(n)])


def copies_of(piece):
    return jnp.broadcast_to(piece[None], (lax.axis_size("cols"), *piece.shape))


def total(pieces):
    return jnp.sum(pieces.astype(F32), axis=0)


def gather_rows(piece):
    held = [piece]
    bit = 1
    while bit < lax.axis_size("rows"):
        held.append(swap(jnp.concatenate(held), bit))
        bit *= 2
    return held


def reduce_rows(near, far):
    bit = lax.axis_size("rows") // 2
    half = near.shape[0]
    got = swap(far, bit).astype(F32)
    kept = near.astype(F32) + got[:half]
    extra = far[half:].astype(F32) + got[half:]
    while bit > 1:
        bit //= 2
        kept, extra = kept.astype(BF16), extra.astype(BF16)
        half //= 2
        got_extra = swap(extra, bit)
        kept = kept[:half].astype(F32) + swap(kept[half:], bit).astype(F32)
        extra = extra.astype(F32) + got_extra.astype(F32)
    return kept, extra.astype(BF16)


def local(counts, start_a, start_b, start_c):
    rows_here, flat_width = counts.shape
    depth, rank = start_c.shape
    cols_here = flat_width // depth
    n_rows, n_cols = lax.axis_size("rows"), lax.axis_size("cols")
    total_i = rows_here * n_rows
    total_j = cols_here * n_cols
    rate_a = 0.3 / math.sqrt(total_j * depth)
    rate_b = 0.3 / math.sqrt(total_i * depth)
    rate_c = 0.3 / math.sqrt(total_i * total_j)
    counts = pltpu.with_memory_space_constraint(counts, pltpu.HBM)
    local_a, local_b = start_a, start_b
    rows_a, rows_b = start_a.shape[0], start_b.shape[0]
    shape_a = (n_cols, rows_a, rank)
    copies, low_b, c = prepare(start_a, start_b, start_c)
    for _ in range(ITERS - 1):
        got = lax.all_to_all(copies, "cols", 0, 0)
        assert got.shape == shape_a
        half = cols_here // 2
        pieces_a, near_b, far_b = call(
            first_body, counts, [got, *gather_rows(low_b), c],
            [(shape_a, BF16), ((half, rank), BF16), ((half + depth, rank), BF16)],
        )
        part_b, low_c = reduce_rows(near_b, far_b)
        local_b = local_b - rate_b * part_b
        low_b = local_b.astype(BF16)
        local_a = local_a - rate_a * total(lax.all_to_all(pieces_a, "cols", 0, 0))
        copies = copies_of(jnp.concatenate([local_a.astype(BF16), low_c]))
        copies, low_b = lax.optimization_barrier((copies, low_b))
    got = lax.all_to_all(copies, "cols", 0, 0)
    b_parts = gather_rows(low_b)
    pieces_a, pieces_b, c = call(
        functools.partial(last_body, rate_c), counts, [got, *b_parts, c],
        [(shape_a, BF16), ((n_rows, rows_b + depth, rank), BF16), (c.shape, F32)],
    )
    part_b = total(lax.all_to_all(pieces_b, "rows", 0, 0))
    part_c = copies_of(part_b[rows_b:].astype(BF16))
    sums = total(lax.all_to_all(jnp.concatenate([pieces_a, part_c], axis=1), "cols", 0, 0))
    return (
        local_a - rate_a * sums[:rows_a],
        local_b - rate_b * part_b[:rows_b],
        c - rate_c * sums[rows_a:],
    )


def solution(mesh):
    placed = (P("rows", "cols"), P(("rows", "cols"), None), P(("cols", "rows"), None), P())
    return jax.shard_map(
        local,
        mesh=mesh,
        in_specs=placed,
        out_specs=(P(("rows", "cols"), None), P(("cols", "rows"), None), P()),
        check_vma=False,
    )
```

time: 456 us -> 126 us (0.28)
  blocking collectives: 296 us -> 8.34 us
  starting transfers between devices: 0.16 us -> 55.6 us
  waiting for transfers between devices: 79 us -> 37.1 us
  matrix products: 33 us -> 0 us
  Pallas kernels: 0 us -> 20.8 us
  local copies, waits for them, and re-layouts: 18.4 us -> 0.77 us
  between operations: 13.9 us -> 0.83 us
  other arithmetic: 11.1 us -> 2.17 us
    psum x2 -> x0, blocking collectives: 153 us -> none  [local(): summed_c = lax.psum(grad_c, ('rows', 'cols'))]
    all_gather x4 -> x0, blocking collectives: 142 us -> none  [the longest x2 96.4 us: local(): lax.all_gather(local_a.astype(jnp.bfloat16), 'cols', axis=0, tiled=True)]
    reduce_scatter x4 -> x0, waiting for transfers between devices: 78.9 us -> none  [the longest x2 39.5 us: local(): summed_b = lax.psum_scatter(grad_b, 'rows', scatter_dimension=0, tiled=True)]
    all_to_all x0 -> x4, starting transfers between devices: none -> 41 us  [the longest x2 19.7 us: local(): got = lax.all_to_all(copies, 'cols', 0, 0)]
    dot_general x6 -> x0, matrix products: 33 us -> none  [the longest x2 16.8 us: local(): lax.dot_general(residual, low_a, (((0,), (0,)), ((), ())), preferred_elem...]
    all_to_all x0 -> x4, waiting for transfers between devices: none -> 21.3 us  [the longest x1 12.3 us: local(): lax.all_to_all(jnp.concatenate([pieces_a, part_c], axis=1), 'cols', 0, 0)]
    pallas_call x0 -> x3, Pallas kernels: none -> 20.8 us  [the longest x2 19.3 us: call(): pl.pallas_call(body, in_specs=[pl.BlockSpec(memory_space=pltpu.HBM)] + [W...]
    unnamed x15 -> x4, local copies, waits for them, and re-layouts: 18.4 us -> 0.01 us
  transfers between devices with their start and end apart: 4 -> 15, of which waited for: 3 -> 13; matrix products, arithmetic and copies ran while one was open for 6% -> 1% of each run, Pallas kernels for 0% -> 0%
where the time goes in v3:
time: 126 us
  starting transfers between devices  55.6 us (44%)
  waiting for transfers between devices  37.1 us (29%)
  Pallas kernels  20.8 us (17%)
  blocking collectives  8.34 us (7%)
  other arithmetic  2.17 us (2%)
    all_to_all x2, starting transfers between devices, local(): got = lax.all_to_all(copies, 'cols', 0, 0)  19.7 us
    pallas_call x2, Pallas kernels, call(): pl.pallas_call(body, in_specs=[pl.BlockSpec(memory_space=pltpu.HBM)] + [W...  19.3 us
    ppermute x11, waiting for transfers between devices, swap(): return lax.ppermute(piece, 'rows', [(i, i ^ bit) for i in range(n)])  15.8 us
    ppermute x11, starting transfers between devices, swap(): return lax.ppermute(piece, 'rows', [(i, i ^ bit) for i in range(n)])  14.6 us
    all_to_all x1, waiting for transfers between devices, local(): lax.all_to_all(jnp.concatenate([pieces_a, part_c], axis=1), 'cols', 0, 0)  12.3 us
    all_to_all x1, starting transfers between devices, local(): lax.all_to_all(jnp.concatenate([pieces_a, part_c], axis=1), 'cols', 0, 0)  12.3 us
    all_to_all x1, starting transfers between devices, local(): local_a = local_a - rate_a * total(lax.all_to_all(pieces_a, 'cols', 0, 0))  9.09 us
    all_to_all x1, blocking collectives, local(): part_b = total(lax.all_to_all(pieces_b, 'rows', 0, 0))  8.34 us
  transfers between devices with their start and end apart: 15, of which 13 were waited for; matrix products, arithmetic and copies ran while one was open for 1% of the time, Pallas kernels for 0%

profile of v3, /device:TPU:1, one launch (start us, length us, event | category | flops | bytes accessed | tf_op | source)
XLA Modules:
  0.0 125.7 jit_solution(6724481167211131848)
XLA Ops:
  0.6 0.0 copy-start
  0.6 0.0 copy-start.1
  0.7 1.5 %shard_map.67 = (bf16[32,16,128]{2,1,0:T(8,128)(2,1)}, bf16[64,128]{1,0:T(8,128)(2,1)S(1)}, f32[16,128]{1,0:T(8,128)S(1)}) custom-call(f32[16,128]{1,0:T(8,128)} %a_ref.1, f32[64,128]{1,0:T(8,128)} %b_ref.1, f32[16,128]{1,0:T(8,128)} %c_ref.1), custom_call_target="tpu_custom_call" | custom-call | tf_op jit(solution)/shard_map/pallas_call | solution.py:32
  2.2 2.1 %collective-permute-start = (bf16[64,128]{1,0:T(8,128)(2,1)S(1)}, bf16[64,128]{1,0:T(8,128)(2,1)S(1)}, u32[]{:S(2)}, u32[]{:S(2)}) collective-permute-start(bf16[64,128]{1,0:T(8,128)(2,1)S(1)} %get-tuple-element.15.refs_0_), channel_id=1, source_target_pairs={{0,32},{32,0},{64,96},{96,64},{128,160},{160,128},{192,224},{224,1... | collective-permute-start | bytes 49160 | tf_op jit(solution)/shard_map/ppermute | solution.py:161
  4.3 11.7 %all-to-all-start = ((bf16[32,16,128]{2,1,0:T(8,128)(2,1)}), bf16[32,16,128]{2,1,0:T(8,128)(2,1)S(1)}, u32[]{:S(2)}, u32[]{:S(2)}) async-start(bf16[32,16,128]{2,1,0:T(8,128)(2,1)} %get-tuple-element.14), calls=%async_computation | async-start | bytes 262144 | tf_op jit(solution)/shard_map/all_to_all | solution.py:213
  16.0 0.0 collective-permute-done.refs_1_
  16.1 1.4 %collective-permute-start.1 = (bf16[128,128]{1,0:T(8,128)(2,1)S(1)}, bf16[128,128]{1,0:T(8,128)(2,1)S(1)}, u32[]{:S(2)}, u32[]{:S(2)}) collective-permute-start(bf16[128,128]{1,0:T(8,128)(2,1)S(1)} %pad_maximum_fusion.3), channel_id=1, source_target_pairs={{0,64},{32,96},{64,0},{96,32},{128,192},{160,224},{192,128},{224,1... | collective-permute-start | bytes 98312 | tf_op jit(solution)/shard_map/ppermute | solution.py:161
  17.4 1.5 %collective-permute-done.1.refs_2_ = bf16[128,128]{1,0:T(8,128)(2,1)S(1)} collective-permute-done((bf16[128,128]{1,0:T(8,128)(2,1)S(1)}, bf16[128,128]{1,0:T(8,128)(2,1)S(1)}, u32[]{:S(2)}, u32[]{:S(2)}) %collective-permute-start.1) | collective-permute-done | bytes 32800 | tf_op jit(solution)/shard_map/ppermute | solution.py:161
  18.9 2.9 %collective-permute-start.2 = (bf16[256,128]{1,0:T(8,128)(2,1)S(1)}, bf16[256,128]{1,0:T(8,128)(2,1)S(1)}, u32[]{:S(2)}, u32[]{:S(2)}) collective-permute-start(bf16[256,128]{1,0:T(8,128)(2,1)S(1)} %pad_maximum_fusion.1), channel_id=1, source_target_pairs={{0,128},{32,160},{64,192},{96,224},{128,0},{160,32},{192,64},{224,... | collective-permute-start | bytes 196616 | tf_op jit(solution)/shard_map/ppermute | solution.py:161
  21.9 2.0 %collective-permute-done.2.refs_3_ = bf16[256,128]{1,0:T(8,128)(2,1)S(1)} collective-permute-done((bf16[256,128]{1,0:T(8,128)(2,1)S(1)}, bf16[256,128]{1,0:T(8,128)(2,1)S(1)}, u32[]{:S(2)}, u32[]{:S(2)}) %collective-permute-start.2) | collective-permute-done | bytes 65568 | tf_op jit(solution)/shard_map/ppermute | solution.py:161
  23.9 2.9 %all-to-all-done.a_ref = bf16[32,16,128]{2,1,0:T(8,128)(2,1)S(1)} async-done(((bf16[32,16,128]{2,1,0:T(8,128)(2,1)}), bf16[32,16,128]{2,1,0:T(8,128)(2,1)S(1)}, u32[]{:S(2)}, u32[]{:S(2)}) %all-to-all-start) | async-done | bytes 131104 | tf_op jit(solution)/shard_map/all_to_all | solution.py:213
  26.8 10.0 %shard_map.68 = (bf16[32,16,128]{2,1,0:T(8,128)(2,1)}, bf16[256,128]{1,0:T(8,128)(2,1)S(1)}, bf16[272,128]{1,0:T(8,128)(2,1)S(1)}) custom-call(bf16[512,8192]{1,0:T(8,128)(2,1)} %n_ref.3, bf16[32,16,128]{2,1,0:T(8,128)(2,1)S(1)} %all-to-all-done.a_ref, bf16[64,128]{1,0:T(8,128)(2,1)S(1)} %get-tuple-element.15.refs_0_, ...), custom_call_target="tpu_custom_call" | custom-call | flops 3221225472 | bytes 8388608 | tf_op jit(solution)/shard_map/pallas_call | solution.py:140
  36.8 3.0 %collective-permute-start.3 = (bf16[272,128]{1,0:T(8,128)(2,1)S(1)}, bf16[272,128]{1,0:T(8,128)(2,1)S(1)}, u32[]{:S(2)}, u32[]{:S(2)}) collective-permute-start(bf16[272,128]{1,0:T(8,128)(2,1)S(1)} %get-tuple-element.18), channel_id=1, source_target_pairs={{0,128},{32,160},{64,192},{96,224},{128,0},{160,32},{192,64},{224,... | collective-permute-start | bytes 208904 | tf_op jit(solution)/shard_map/ppermute | solution.py:161
  39.8 9.1 %all-to-all-start.1 = ((bf16[32,16,128]{2,1,0:T(8,128)(2,1)}), bf16[32,16,128]{2,1,0:T(8,128)(2,1)S(1)}, u32[]{:S(2)}, u32[]{:S(2)}) async-start(bf16[32,16,128]{2,1,0:T(8,128)(2,1)} %get-tuple-element.17), calls=%async_computation.1 | async-start | bytes 262144 | tf_op jit(solution)/shard_map/all_to_all | solution.py:223
  48.9 0.0 collective-permute-done.3
  48.9 0.7 collective-permute-start.4
  49.6 1.2 collective-permute-start.6
  50.8 1.0 collective-permute-done.4
  51.8 0.0 collective-permute-start.5
  51.8 1.0 collective-permute-done.6
  52.8 0.5 collective-permute-start.7
  53.4 1.2 collective-permute-done.5
  54.6 1.3 %collective-permute-done.7 = bf16[64,128]{1,0:T(8,128)(2,1)S(1)} collective-permute-done((bf16[64,128]{1,0:T(8,128)(2,1)S(1)}, bf16[64,128]{1,0:T(8,128)(2,1)S(1)}, u32[]{:S(2)}, u32[]{:S(2)}) %collective-permute-start.7) | collective-permute-done | bytes 16416 | tf_op jit(solution)/shard_map/ppermute | solution.py:161
  55.8 0.0 copy-done
  55.8 3.8 %all-to-all-done.1 = bf16[32,16,128]{2,1,0:T(8,128)(2,1)S(1)} async-done(((bf16[32,16,128]{2,1,0:T(8,128)(2,1)}), bf16[32,16,128]{2,1,0:T(8,128)(2,1)S(1)}, u32[]{:S(2)}, u32[]{:S(2)}) %all-to-all-start.1) | async-done | bytes 131104 | tf_op jit(solution)/shard_map/all_to_all | solution.py:223
  59.7 0.0 copy-done.1
  59.7 0.7 broadcast_in_dim.4
  60.5 7.9 %all-to-all-start.2 = ((bf16[32,32,128]{2,1,0:T(8,128)(2,1)}), bf16[32,32,128]{2,1,0:T(8,128)(2,1)S(1)}, u32[]{:S(2)}, u32[]{:S(2)}) async-start(bf16[32,32,128]{2,1,0:T(8,128)(2,1)} %broadcast_in_dim.4), calls=%async_computation.2 | async-start | bytes 524288 | tf_op jit(solution)/shard_map/all_to_all | solution.py:226
  68.4 0.2 collective-permute-start.8
  68.6 2.5 %collective-permute-done.8.refs_1_ = bf16[64,128]{1,0:T(8,128)(2,1)S(1)} collective-permute-done((bf16[64,128]{1,0:T(8,128)(2,1)S(1)}, bf16[64,128]{1,0:T(8,128)(2,1)S(1)}, u32[]{:S(2)}, u32[]{:S(2)}) %collective-permute-start.8) | collective-permute-done | bytes 16416 | tf_op jit(solution)/shard_map/ppermute | solution.py:161
  71.1 1.1 collective-permute-start.9
  72.1 2.0 %collective-permute-done.9.refs_2_ = bf16[128,128]{1,0:T(8,128)(2,1)S(1)} collective-permute-done((bf16[128,128]{1,0:T(8,128)(2,1)S(1)}, bf16[128,128]{1,0:T(8,128)(2,1)S(1)}, u32[]{:S(2)}, u32[]{:S(2)}) %collective-permute-start.9) | collective-permute-done | bytes 32800 | tf_op jit(solution)/shard_map/ppermute | solution.py:161
  74.1 1.6 %collective-permute-start.10 = (bf16[256,128]{1,0:T(8,128)(2,1)S(1)}, bf16[256,128]{1,0:T(8,128)(2,1)S(1)}, u32[]{:S(2)}, u32[]{:S(2)}) collective-permute-start(bf16[256,128]{1,0:T(8,128)(2,1)S(1)} %pad_maximum_fusion.2), channel_id=1, source_target_pairs={{0,128},{32,160},{64,192},{96,224},{128,0},{160,32},{192,64},{224,... | collective-permute-start | bytes 196616 | tf_op jit(solution)/shard_map/ppermute | solution.py:161
  75.7 3.3 %collective-permute-done.10.refs_3_ = bf16[256,128]{1,0:T(8,128)(2,1)S(1)} collective-permute-done((bf16[256,128]{1,0:T(8,128)(2,1)S(1)}, bf16[256,128]{1,0:T(8,128)(2,1)S(1)}, u32[]{:S(2)}, u32[]{:S(2)}) %collective-permute-start.10) | collective-permute-done | bytes 65568 | tf_op jit(solution)/shard_map/ppermute | solution.py:161
  79.1 2.3 %all-to-all-done.2.a_ref = bf16[32,32,128]{2,1,0:T(8,128)(2,1)S(1)} async-done(((bf16[32,32,128]{2,1,0:T(8,128)(2,1)}), bf16[32,32,128]{2,1,0:T(8,128)(2,1)S(1)}, u32[]{:S(2)}, u32[]{:S(2)}) %all-to-all-start.2) | async-done | bytes 262176 | tf_op jit(solution)/shard_map/all_to_all | solution.py:226
  81.3 9.4 %shard_map.69 = (bf16[32,16,128]{2,1,0:T(8,128)(2,1)S(1)}, bf16[8,80,128]{2,1,0:T(8,128)(2,1)S(1)}, f32[16,128]{1,0:T(8,128)S(1)}) custom-call(bf16[512,8192]{1,0:T(8,128)(2,1)} %n_ref.3, bf16[32,32,128]{2,1,0:T(8,128)(2,1)S(1)} %all-to-all-done.2.a_ref, bf16[64,128]{1,0:T(8,128)(2,1)S(1)} %fusion.2.refs_0_, ...), custom_call_target="tpu_custom_call" | custom-call | flops 3221225472 | bytes 8388608 | tf_op jit(solution)/shard_map/pallas_call | solution.py:140
  90.7 8.3 %all_to_all.25 = bf16[8,80,128]{2,1,0:T(8,128)(2,1)S(1)} all-to-all(bf16[8,80,128]{2,1,0:T(8,128)(2,1)S(1)} %get-tuple-element.23), channel_id=1, replica_groups=mesh['rows'=8,'cols'=32] {'rows'}, dimensions={0} | all-to-all | bytes 327680 | tf_op jit(solution)/shard_map/all_to_all | solution.py:232
  99.1 0.7 pad_maximum_fusion
  99.8 12.3 %all-to-all-start.4 = ((bf16[32,32,128]{2,1,0:T(8,128)(2,1)}), bf16[32,32,128]{2,1,0:T(8,128)(2,1)S(1)}, u32[]{:S(2)}, u32[]{:S(2)}) async-start(bf16[32,32,128]{2,1,0:T(8,128)(2,1)} %pad_maximum_fusion), calls=%async_computation.4 | async-start | bytes 524288 | tf_op jit(solution)/shard_map/all_to_all | solution.py:234
  112.1 0.6 fusion.1
  112.7 12.3 %all-to-all-done.4 = bf16[32,32,128]{2,1,0:T(8,128)(2,1)S(1)} async-done(((bf16[32,32,128]{2,1,0:T(8,128)(2,1)}), bf16[32,32,128]{2,1,0:T(8,128)(2,1)S(1)}, u32[]{:S(2)}, u32[]{:S(2)}) %all-to-all-start.4) | async-done | bytes 262176 | tf_op jit(solution)/shard_map/all_to_all | solution.py:234
  125.1 0.6 fusion.3
  (20 shorter events, 0.2 us)
Async XLA Ops:
  0.6 55.2 %copy-start = (f32[64,128]{1,0:T(8,128)S(1)}, f32[64,128]{1,0:T(8,128)}, u32[]{:S(2)}) copy-start(f32[64,128]{1,0:T(8,128)} %b_ref.1) | copy-start | bytes 98308
  0.6 59.1 %copy-start.1 = (f32[16,128]{1,0:T(8,128)S(1)}, f32[16,128]{1,0:T(8,128)}, u32[]{:S(2)}) copy-start(f32[16,128]{1,0:T(8,128)} %a_ref.1) | copy-start | bytes 24580
  2.2 13.9 %collective-permute-start = (bf16[64,128]{1,0:T(8,128)(2,1)S(1)}, bf16[64,128]{1,0:T(8,128)(2,1)S(1)}, u32[]{:S(2)}, u32[]{:S(2)}) collective-permute-start(bf16[64,128]{1,0:T(8,128)(2,1)S(1)} %get-tuple-element.15.refs_0_), channel_id=1, source_target_pairs={{0,32},{32,0},{64,96},{96,64},{128,160},{160,128},{192,224},{224,1... | collective-permute-start | bytes 49160 | tf_op jit(solution)/shard_map/ppermute | solution.py:161
  4.3 22.5 %all-to-all-start = ((bf16[32,16,128]{2,1,0:T(8,128)(2,1)}), bf16[32,16,128]{2,1,0:T(8,128)(2,1)S(1)}, u32[]{:S(2)}, u32[]{:S(2)}) async-start(bf16[32,16,128]{2,1,0:T(8,128)(2,1)} %get-tuple-element.14), calls=%async_computation | async-start | bytes 262144 | tf_op jit(solution)/shard_map/all_to_all | solution.py:213
  16.1 2.9 %collective-permute-start.1 = (bf16[128,128]{1,0:T(8,128)(2,1)S(1)}, bf16[128,128]{1,0:T(8,128)(2,1)S(1)}, u32[]{:S(2)}, u32[]{:S(2)}) collective-permute-start(bf16[128,128]{1,0:T(8,128)(2,1)S(1)} %pad_maximum_fusion.3), channel_id=1, source_target_pairs={{0,64},{32,96},{64,0},{96,32},{128,192},{160,224},{192,128},{224,1... | collective-permute-start | bytes 98312 | tf_op jit(solution)/shard_map/ppermute | solution.py:161
  18.9 4.9 %collective-permute-start.2 = (bf16[256,128]{1,0:T(8,128)(2,1)S(1)}, bf16[256,128]{1,0:T(8,128)(2,1)S(1)}, u32[]{:S(2)}, u32[]{:S(2)}) collective-permute-start(bf16[256,128]{1,0:T(8,128)(2,1)S(1)} %pad_maximum_fusion.1), channel_id=1, source_target_pairs={{0,128},{32,160},{64,192},{96,224},{128,0},{160,32},{192,64},{224,... | collective-permute-start | bytes 196616 | tf_op jit(solution)/shard_map/ppermute | solution.py:161
  36.8 12.1 %collective-permute-start.3 = (bf16[272,128]{1,0:T(8,128)(2,1)S(1)}, bf16[272,128]{1,0:T(8,128)(2,1)S(1)}, u32[]{:S(2)}, u32[]{:S(2)}) collective-permute-start(bf16[272,128]{1,0:T(8,128)(2,1)S(1)} %get-tuple-element.18), channel_id=1, source_target_pairs={{0,128},{32,160},{64,192},{96,224},{128,0},{160,32},{192,64},{224,... | collective-permute-start | bytes 208904 | tf_op jit(solution)/shard_map/ppermute | solution.py:161
  39.8 19.9 %all-to-all-start.1 = ((bf16[32,16,128]{2,1,0:T(8,128)(2,1)}), bf16[32,16,128]{2,1,0:T(8,128)(2,1)S(1)}, u32[]{:S(2)}, u32[]{:S(2)}) async-start(bf16[32,16,128]{2,1,0:T(8,128)(2,1)} %get-tuple-element.17), calls=%async_computation.1 | async-start | bytes 262144 | tf_op jit(solution)/shard_map/all_to_all | solution.py:223
  48.9 2.9 %collective-permute-start.4 = (bf16[16,128]{1,0:T(8,128)(2,1)S(1)}, bf16[16,128]{1,0:T(8,128)(2,1)S(1)}, u32[]{:S(2)}, u32[]{:S(2)}) collective-permute-start(bf16[16,128]{1,0:T(8,128)(2,1)S(1)} %fusion.5), channel_id=1, source_target_pairs={{0,64},{32,96},{64,0},{96,32},{128,192},{160,224},{192,128},{224,1... | collective-permute-start | bytes 12296 | tf_op jit(solution)/shard_map/ppermute | solution.py:161
  49.6 3.2 %collective-permute-start.6 = (bf16[128,128]{1,0:T(8,128)(2,1)S(1)}, bf16[128,128]{1,0:T(8,128)(2,1)S(1)}, u32[]{:S(2)}, u32[]{:S(2)}) collective-permute-start(bf16[128,128]{1,0:T(8,128)(2,1)S(1)} %slice.48), channel_id=1, source_target_pairs={{0,64},{32,96},{64,0},{96,32},{128,192},{160,224},{192,128},{224,1... | collective-permute-start | bytes 98312 | tf_op jit(solution)/shard_map/ppermute | solution.py:161
  51.8 2.8 %collective-permute-start.5 = (bf16[16,128]{1,0:T(8,128)(2,1)S(1)}, bf16[16,128]{1,0:T(8,128)(2,1)S(1)}, u32[]{:S(2)}, u32[]{:S(2)}) collective-permute-start(bf16[16,128]{1,0:T(8,128)(2,1)S(1)} %add_convert_fusion.2), channel_id=1, source_target_pairs={{0,32},{32,0},{64,96},{96,64},{128,160},{160,128},{192,224},{224,1... | collective-permute-start | bytes 12296 | tf_op jit(solution)/shard_map/ppermute | solution.py:161
  52.8 3.0 %collective-permute-start.7 = (bf16[64,128]{1,0:T(8,128)(2,1)S(1)}, bf16[64,128]{1,0:T(8,128)(2,1)S(1)}, u32[]{:S(2)}, u32[]{:S(2)}) collective-permute-start(bf16[64,128]{1,0:T(8,128)(2,1)S(1)} %slice.50), channel_id=1, source_target_pairs={{0,32},{32,0},{64,96},{96,64},{128,160},{160,128},{192,224},{224,1... | collective-permute-start | bytes 49160 | tf_op jit(solution)/shard_map/ppermute | solution.py:161
  60.5 20.9 %all-to-all-start.2 = ((bf16[32,32,128]{2,1,0:T(8,128)(2,1)}), bf16[32,32,128]{2,1,0:T(8,128)(2,1)S(1)}, u32[]{:S(2)}, u32[]{:S(2)}) async-start(bf16[32,32,128]{2,1,0:T(8,128)(2,1)} %broadcast_in_dim.4), calls=%async_computation.2 | async-start | bytes 524288 | tf_op jit(solution)/shard_map/all_to_all | solution.py:226
  68.4 2.7 %collective-permute-start.8 = (bf16[64,128]{1,0:T(8,128)(2,1)S(1)}, bf16[64,128]{1,0:T(8,128)(2,1)S(1)}, u32[]{:S(2)}, u32[]{:S(2)}) collective-permute-start(bf16[64,128]{1,0:T(8,128)(2,1)S(1)} %fusion.2.refs_0_), channel_id=1, source_target_pairs={{0,32},{32,0},{64,96},{96,64},{128,160},{160,128},{192,224},{224,1... | collective-permute-start | bytes 49160 | tf_op jit(solution)/shard_map/ppermute | solution.py:161
  71.1 3.1 %collective-permute-start.9 = (bf16[128,128]{1,0:T(8,128)(2,1)S(1)}, bf16[128,128]{1,0:T(8,128)(2,1)S(1)}, u32[]{:S(2)}, u32[]{:S(2)}) collective-permute-start(bf16[128,128]{1,0:T(8,128)(2,1)S(1)} %pad_maximum_fusion.4), channel_id=1, source_target_pairs={{0,64},{32,96},{64,0},{96,32},{128,192},{160,224},{192,128},{224,1... | collective-permute-start | bytes 98312 | tf_op jit(solution)/shard_map/ppermute | solution.py:161
  74.1 4.9 %collective-permute-start.10 = (bf16[256,128]{1,0:T(8,128)(2,1)S(1)}, bf16[256,128]{1,0:T(8,128)(2,1)S(1)}, u32[]{:S(2)}, u32[]{:S(2)}) collective-permute-start(bf16[256,128]{1,0:T(8,128)(2,1)S(1)} %pad_maximum_fusion.2), channel_id=1, source_target_pairs={{0,128},{32,160},{64,192},{96,224},{128,0},{160,32},{192,64},{224,... | collective-permute-start | bytes 196616 | tf_op jit(solution)/shard_map/ppermute | solution.py:161
  99.8 25.2 %all-to-all-start.4 = ((bf16[32,32,128]{2,1,0:T(8,128)(2,1)}), bf16[32,32,128]{2,1,0:T(8,128)(2,1)S(1)}, u32[]{:S(2)}, u32[]{:S(2)}) async-start(bf16[32,32,128]{2,1,0:T(8,128)(2,1)} %pad_maximum_fusion), calls=%async_computation.4 | async-start | bytes 524288 | tf_op jit(solution)/shard_map/all_to_all | solution.py:234

commit v4 on v3

--- a/solution.py
+++ b/solution.py
@@ -11,7 +11,8 @@
 ITERS = 2
 BF16 = jnp.bfloat16
 F32 = jnp.float32
-IN_FLIGHT = 3
+WAITS = {0: (0,), 1: (1, 2), 4: (3,)}
+JOIN_WEIGHT = 3_000_000_000
 WHOLE = pl.BlockSpec(memory_space=pltpu.VMEM)
 
 
@@ -47,29 +48,61 @@
     )(*operands)
 
 
-def visit_blocks(order, n_ref, held_ref, sems, low_a, b_of, c, put_b, acc_ref, grad_c):
+def update_body(rate_a, rate_b, got_ref, a_ref, sum_b_ref, b_ref, low_c_ref, *outs):
+    copies_ref, low_b_ref, new_a_ref, new_b_ref = outs
+    new_b = b_ref[...] - rate_b * sum_b_ref[...]
+    new_b_ref[...] = new_b
+    low_b_ref[...] = new_b.astype(BF16)
+    new_a = a_ref[...] - rate_a * total(got_ref[...])
+    new_a_ref[...] = new_a
+    parts, height, rank = copies_ref.shape
+    rows = new_a.shape[0]
+    copies_ref[:, :rows] = jnp.broadcast_to(new_a.astype(BF16)[None], (parts, rows, rank))
+    copies_ref[:, rows:] = jnp.broadcast_to(low_c_ref[...][None], (parts, height - rows, rank))
+
+
+def update(got, a, sum_b, b, low_c, rate_a, rate_b):
+    parts, rows, rank = got.shape
+    return pl.pallas_call(
+        functools.partial(update_body, rate_a, rate_b),
+        in_specs=[WHOLE] * 5,
+        out_specs=[WHOLE] * 4,
+        out_shape=[
+            jax.ShapeDtypeStruct((parts, rows + low_c.shape[0], rank), BF16),
+            jax.ShapeDtypeStruct(b.shape, BF16),
+            jax.ShapeDtypeStruct(a.shape, F32),
+            jax.ShapeDtypeStruct(b.shape, F32),
+        ],
+        compiler_params=pltpu.CompilerParams(vmem_limit_bytes=2 << 20),
+    )(got, a, sum_b, b, low_c)
+
+
+def visit_blocks(n_ref, held_ref, sems, low_a, b_of, c, put_b, acc_ref, grad_c):
     depth, rank = c.shape
     blocks = lax.axis_size("rows")
     me = lax.axis_index("rows")
     tile = n_ref.shape[1] // blocks
     wide = tile // depth
 
-    def fetch(k):
-        columns = pl.ds(pl.multiple_of((me ^ order[k]) * tile, tile), tile)
-        return pltpu.make_async_copy(n_ref.at[:, columns], held_ref.at[k], sems.at[k])
-
-    for k in range(min(IN_FLIGHT, len(order))):
-        fetch(k).start()
-    for k, p in enumerate(order):
+    def fetch(level):
+        count = max(1 << level >> 1, 1)
+        first = (me ^ (1 << level >> 1)) // count * count
+        columns = pl.ds(pl.multiple_of(first * tile, tile), count * tile)
+        return pltpu.make_async_copy(n_ref.at[:, columns], held_ref.at[:, columns], sems.at[level])
+
+    levels = blocks.bit_length()
+    for level in range(levels):
+        fetch(level).start()
+    for p in range(blocks):
+        columns = pl.ds(pl.multiple_of((me ^ p) * tile, tile), tile)
         low_b = b_of(p).astype(F32)
         scaled = (low_b[:, None, :] * c[None]).astype(BF16).reshape(tile, rank)
         log_rate = lax.dot_general(
             low_a, scaled, (((1,), (1,)), ((), ())), preferred_element_type=F32
         )
-        fetch(k).wait()
-        if k + IN_FLIGHT < len(order):
-            fetch(k + IN_FLIGHT).start()
-        residual = (jnp.exp(log_rate) - held_ref[k].astype(F32)).astype(BF16)
+        for level in WAITS.get(p, ()):
+            fetch(level).wait()
+        residual = (jnp.exp(log_rate) - held_ref[:, columns].astype(F32)).astype(BF16)
         mixed = lax.dot_general(
             residual, low_a, (((0,), (0,)), ((), ())), preferred_element_type=F32
         ).reshape(wide, depth, rank)
@@ -80,10 +113,12 @@
 
 
 def parts_of(b_refs, wide):
-    def b_of(p):
-        level = p.bit_length()
-        start = (p - (1 << level >> 1)) * wide
-        return b_refs[level][start : start + wide]
+    def b_of(x):
+        steps = len(b_refs) - 1
+        p = sum((x >> k & 1) << (steps - 1 - k) for k in range(steps))
+        step = p.bit_length()
+        start = (p - (1 << step >> 1)) * wide
+        return b_refs[step][start : start + wide]
 
     return b_of
 
@@ -103,7 +138,7 @@
     b_of = parts_of(b_refs, wide)
     grad_c = jnp.zeros(c_ref.shape, F32)
     grad_c = visit_blocks(
-        range(blocks), n_ref, held_ref, sems, low_a, b_of, c_ref[...], put_b, acc_ref, grad_c
+        n_ref, held_ref, sems, low_a, b_of, c_ref[...], put_b, acc_ref, grad_c
     )
     xa_ref[...] = acc_ref[...].astype(BF16).reshape(xa_ref.shape)
     far_ref[half:] = grad_c.astype(BF16)
@@ -127,7 +162,7 @@
     b_of = parts_of(b_refs, wide)
     grad_c = jnp.zeros(c.shape, F32)
     grad_c = visit_blocks(
-        range(blocks), n_ref, held_ref, sems, low_a, b_of, c, put_b, acc_ref, grad_c
+        n_ref, held_ref, sems, low_a, b_of, c, put_b, acc_ref, grad_c
     )
     xa_ref[...] = acc_ref[...].astype(BF16).reshape(xa_ref.shape)
     xb_ref[:, wide:] = jnp.broadcast_to(grad_c.astype(BF16)[None], (blocks, depth, rank))
@@ -136,7 +171,6 @@
 def call(body, counts, operands, outs):
     rows, flat = counts.shape
     rank = operands[0].shape[-1]
-    blocks = lax.axis_size("rows")
     return pl.pallas_call(
         body,
         in_specs=[pl.BlockSpec(memory_space=pltpu.HBM)] + [WHOLE] * len(operands),
@@ -144,8 +178,8 @@
         out_shape=[jax.ShapeDtypeStruct(shape, dtype) for shape, dtype in outs],
         scratch_shapes=[
             pltpu.VMEM((rows, rank), F32),
-            pltpu.VMEM((blocks, rows, flat // blocks), BF16),
-            pltpu.SemaphoreType.DMA((blocks,)),
+            pltpu.VMEM((rows, flat), BF16),
+            pltpu.SemaphoreType.DMA((lax.axis_size("rows").bit_length(),)),
         ],
         compiler_params=pltpu.CompilerParams(vmem_limit_bytes=32 << 20),
         cost_estimate=pl.CostEstimate(
@@ -169,12 +203,33 @@
     return jnp.sum(pieces.astype(F32), axis=0)
 
 
-def gather_rows(piece):
+def join_body(*refs):
+    *pieces, out_ref = refs
+    at = 0
+    for piece in pieces:
+        out_ref[at : at + piece.shape[0]] = piece[...]
+        at += piece.shape[0]
+
+
+def join(pieces, weight):
+    rows = sum(piece.shape[0] for piece in pieces)
+    return pl.pallas_call(
+        join_body,
+        in_specs=[WHOLE] * len(pieces),
+        out_specs=WHOLE,
+        out_shape=jax.ShapeDtypeStruct((rows, pieces[0].shape[1]), pieces[0].dtype),
+        compiler_params=pltpu.CompilerParams(vmem_limit_bytes=2 << 20),
+        cost_estimate=pl.CostEstimate(flops=weight, transcendentals=0, bytes_accessed=0),
+    )(*pieces)
+
+
+def gather_rows(piece, weight=0):
     held = [piece]
-    bit = 1
-    while bit < lax.axis_size("rows"):
-        held.append(swap(jnp.concatenate(held), bit))
-        bit *= 2
+    bit = lax.axis_size("rows") // 2
+    while bit:
+        whole = join(held, weight) if weight and bit == 1 else jnp.concatenate(held)
+        held.append(swap(whole, bit))
+        bit //= 2
     return held
 
 
@@ -218,20 +273,21 @@
             [(shape_a, BF16), ((half, rank), BF16), ((half + depth, rank), BF16)],
         )
         part_b, low_c = reduce_rows(near_b, far_b)
-        local_b = local_b - rate_b * part_b
-        low_b = local_b.astype(BF16)
-        local_a = local_a - rate_a * total(lax.all_to_all(pieces_a, "cols", 0, 0))
-        copies = copies_of(jnp.concatenate([local_a.astype(BF16), low_c]))
-        copies, low_b = lax.optimization_barrier((copies, low_b))
+        got = lax.all_to_all(pieces_a, "cols", 0, 0)
+        copies, low_b, local_a, local_b = update(
+            got, local_a, part_b, local_b, low_c, rate_a, rate_b
+        )
     got = lax.all_to_all(copies, "cols", 0, 0)
-    b_parts = gather_rows(low_b)
+    b_parts = gather_rows(low_b, JOIN_WEIGHT)
     pieces_a, pieces_b, c = call(
         functools.partial(last_body, rate_c), counts, [got, *b_parts, c],
         [(shape_a, BF16), ((n_rows, rows_b + depth, rank), BF16), (c.shape, F32)],
     )
     part_b = total(lax.all_to_all(pieces_b, "rows", 0, 0))
     part_c = copies_of(part_b[rows_b:].astype(BF16))
-    sums = total(lax.all_to_all(jnp.concatenate([pieces_a, part_c], axis=1), "cols", 0, 0))
+    sums = lax.all_to_all(jnp.concatenate([pieces_a, part_c], axis=1), "cols", 0, 0)
+    sums, part_b = lax.optimization_barrier((sums, part_b))
+    sums = total(sums)
     return (
         local_a - rate_a * sums[:rows_a],
         local_b - rate_b * part_b[:rows_b],

time: 126 us -> 119 us (0.944)
  blocking collectives: 8.34 us -> 27.3 us
  starting transfers between devices: 55.6 us -> 38.7 us
  waiting for transfers between devices: 37.1 us -> 30.7 us
    all_to_all x0 -> x1, blocking collectives: none -> 18.9 us  [local(): lax.all_to_all(jnp.concatenate([pieces_a, part_c], axis=1), 'cols', 0, 0)]
    all_to_all x2 -> x1, starting transfers between devices: 21.4 us -> 7.76 us  [local(): got = lax.all_to_all(pieces_a, 'cols', 0, 0)]
    all_to_all x2 -> x1, waiting for transfers between devices: 16.1 us -> 3.31 us  [local(): got = lax.all_to_all(pieces_a, 'cols', 0, 0)]
    all_to_all x2, waiting for transfers between devices: 5.22 us -> 10.1 us  [local(): got = lax.all_to_all(copies, 'cols', 0, 0)]
    ppermute x11, starting transfers between devices: 14.6 us -> 10.3 us  [swap(): return lax.ppermute(piece, 'rows', [(i, i ^ bit) for i in range(n)])]
    pallas_call x2, Pallas kernels: 19.3 us -> 17.7 us  [call(): pl.pallas_call(body, in_specs=[pl.BlockSpec(memory_space=pltpu.HBM)] + [W...]
    ppermute x11, waiting for transfers between devices: 15.8 us -> 17.3 us  [swap(): return lax.ppermute(piece, 'rows', [(i, i ^ bit) for i in range(n)])]
  transfers between devices with their start and end apart: 15 -> 14, of which waited for: 13 -> 11; matrix products, arithmetic and copies ran while one was open for 1% -> 0% of each run, Pallas kernels for 0% -> 0%
where the time goes in v4:
time: 119 us
  starting transfers between devices  38.7 us (33%)
  waiting for transfers between devices  30.7 us (26%)
  blocking collectives  27.3 us (23%)
  Pallas kernels  20 us (17%)
  other arithmetic  1.41 us (1%)
    all_to_all x2, starting transfers between devices, local(): got = lax.all_to_all(copies, 'cols', 0, 0)  20.7 us
    all_to_all x1, blocking collectives, local(): lax.all_to_all(jnp.concatenate([pieces_a, part_c], axis=1), 'cols', 0, 0)  18.9 us
    pallas_call x2, Pallas kernels, call(): pl.pallas_call(body, in_specs=[pl.BlockSpec(memory_space=pltpu.HBM)] + [W...  17.7 us
    ppermute x11, waiting for transfers between devices, swap(): return lax.ppermute(piece, 'rows', [(i, i ^ bit) for i in range(n)])  17.3 us
    ppermute x11, starting transfers between devices, swap(): return lax.ppermute(piece, 'rows', [(i, i ^ bit) for i in range(n)])  10.3 us
    all_to_all x2, waiting for transfers between devices, local(): got = lax.all_to_all(copies, 'cols', 0, 0)  10.1 us
    all_to_all x1, blocking collectives, local(): part_b = total(lax.all_to_all(pieces_b, 'rows', 0, 0))  8.32 us
    all_to_all x1, starting transfers between devices, local(): got = lax.all_to_all(pieces_a, 'cols', 0, 0)  7.76 us
  transfers between devices with their start and end apart: 14, of which 11 were waited for; matrix products, arithmetic and copies ran while one was open for 0% of the time, Pallas kernels for 0%

profile of v4, /device:TPU:1, one launch (start us, length us, event | category | flops | bytes accessed | tf_op | source)
XLA Modules:
  0.0 118.9 jit_solution(13349818669596026680)
XLA Ops:
  0.6 0.0 copy-start
  0.6 0.0 copy-start.1
  0.7 1.5 %shard_map.67 = (bf16[32,16,128]{2,1,0:T(8,128)(2,1)}, bf16[64,128]{1,0:T(8,128)(2,1)S(1)}, f32[16,128]{1,0:T(8,128)S(1)}) custom-call(f32[16,128]{1,0:T(8,128)} %a_ref.3, f32[64,128]{1,0:T(8,128)} %b_ref.3, f32[16,128]{1,0:T(8,128)} %c_ref.1), custom_call_target="tpu_custom_call" | custom-call | tf_op jit(solution)/shard_map/pallas_call | solution.py:33
  2.2 3.8 %collective-permute-start = (bf16[64,128]{1,0:T(8,128)(2,1)S(1)}, bf16[64,128]{1,0:T(8,128)(2,1)S(1)}, u32[]{:S(2)}, u32[]{:S(2)}) collective-permute-start(bf16[64,128]{1,0:T(8,128)(2,1)S(1)} %get-tuple-element.19.refs_0_), channel_id=1, source_target_pairs={{0,128},{32,160},{64,192},{96,224},{128,0},{160,32},{192,64},{224,... | collective-permute-start | bytes 49160 | tf_op jit(solution)/shard_map/ppermute | solution.py:195
  6.0 12.0 %all-to-all-start = ((bf16[32,16,128]{2,1,0:T(8,128)(2,1)}), bf16[32,16,128]{2,1,0:T(8,128)(2,1)S(1)}, u32[]{:S(2)}, u32[]{:S(2)}) async-start(bf16[32,16,128]{2,1,0:T(8,128)(2,1)} %get-tuple-element.18), calls=%async_computation | async-start | bytes 262144 | tf_op jit(solution)/shard_map/all_to_all | solution.py:268
  18.1 0.0 collective-permute-done.refs_1_
  18.1 0.5 collective-permute-start.1
  18.6 2.4 %collective-permute-done.1.refs_2_ = bf16[128,128]{1,0:T(8,128)(2,1)S(1)} collective-permute-done((bf16[128,128]{1,0:T(8,128)(2,1)S(1)}, bf16[128,128]{1,0:T(8,128)(2,1)S(1)}, u32[]{:S(2)}, u32[]{:S(2)}) %collective-permute-start.1) | collective-permute-done | bytes 32800 | tf_op jit(solution)/shard_map/ppermute | solution.py:195
  21.0 0.3 collective-permute-start.2
  21.3 3.3 %collective-permute-done.2.refs_3_ = bf16[256,128]{1,0:T(8,128)(2,1)S(1)} collective-permute-done((bf16[256,128]{1,0:T(8,128)(2,1)S(1)}, bf16[256,128]{1,0:T(8,128)(2,1)S(1)}, u32[]{:S(2)}, u32[]{:S(2)}) %collective-permute-start.2) | collective-permute-done | bytes 65568 | tf_op jit(solution)/shard_map/ppermute | solution.py:195
  24.5 4.3 %all-to-all-done.a_ref = bf16[32,16,128]{2,1,0:T(8,128)(2,1)S(1)} async-done(((bf16[32,16,128]{2,1,0:T(8,128)(2,1)}), bf16[32,16,128]{2,1,0:T(8,128)(2,1)S(1)}, u32[]{:S(2)}, u32[]{:S(2)}) %all-to-all-start) | async-done | bytes 131104 | tf_op jit(solution)/shard_map/all_to_all | solution.py:268
  28.8 9.1 %shard_map.68 = (bf16[32,16,128]{2,1,0:T(8,128)(2,1)}, bf16[256,128]{1,0:T(8,128)(2,1)S(1)}, bf16[272,128]{1,0:T(8,128)(2,1)S(1)}) custom-call(bf16[512,8192]{1,0:T(8,128)(2,1)} %n_ref.3, bf16[32,16,128]{2,1,0:T(8,128)(2,1)S(1)} %all-to-all-done.a_ref, bf16[64,128]{1,0:T(8,128)(2,1)S(1)} %get-tuple-element.19.refs_0_, ...), custom_call_target="tpu_custom_call" | custom-call | flops 3221225472 | bytes 8388608 | tf_op jit(solution)/shard_map/pallas_call | solution.py:174
  38.0 0.1 collective-permute-start.3
  38.1 7.8 %all-to-all-start.1 = ((bf16[32,16,128]{2,1,0:T(8,128)(2,1)}), bf16[32,16,128]{2,1,0:T(8,128)(2,1)S(1)}, u32[]{:S(2)}, u32[]{:S(2)}) async-start(bf16[32,16,128]{2,1,0:T(8,128)(2,1)} %get-tuple-element.21), calls=%async_computation.1 | async-start | bytes 262144 | tf_op jit(solution)/shard_map/all_to_all | solution.py:276
  45.9 0.0 collective-permute-done.3
  45.9 1.2 %collective-permute-start.6 = (bf16[16,128]{1,0:T(8,128)(2,1)S(1)}, bf16[16,128]{1,0:T(8,128)(2,1)S(1)}, u32[]{:S(2)}, u32[]{:S(2)}) collective-permute-start(bf16[16,128]{1,0:T(8,128)(2,1)S(1)} %fusion.3), channel_id=1, source_target_pairs={{0,64},{32,96},{64,0},{96,32},{128,192},{160,224},{192,128},{224,1... | collective-permute-start | bytes 12296 | tf_op jit(solution)/shard_map/ppermute | solution.py:195
  47.2 0.4 collective-permute-start.4
  47.6 1.2 collective-permute-done.6
  48.7 0.3 collective-permute-start.7
  49.1 1.2 %collective-permute-done.4 = bf16[128,128]{1,0:T(8,128)(2,1)S(1)} collective-permute-done((bf16[128,128]{1,0:T(8,128)(2,1)S(1)}, bf16[128,128]{1,0:T(8,128)(2,1)S(1)}, u32[]{:S(2)}, u32[]{:S(2)}) %collective-permute-start.4) | collective-permute-done | bytes 32800 | tf_op jit(solution)/shard_map/ppermute | solution.py:195
  50.3 0.4 collective-permute-start.5
  50.7 0.8 collective-permute-done.7
  51.5 1.8 %collective-permute-done.5 = bf16[64,128]{1,0:T(8,128)(2,1)S(1)} collective-permute-done((bf16[64,128]{1,0:T(8,128)(2,1)S(1)}, bf16[64,128]{1,0:T(8,128)(2,1)S(1)}, u32[]{:S(2)}, u32[]{:S(2)}) %collective-permute-start.5) | collective-permute-done | bytes 16416 | tf_op jit(solution)/shard_map/ppermute | solution.py:195
  53.3 3.3 %all-to-all-done.1.got_ref = bf16[32,16,128]{2,1,0:T(8,128)(2,1)S(1)} async-done(((bf16[32,16,128]{2,1,0:T(8,128)(2,1)}), bf16[32,16,128]{2,1,0:T(8,128)(2,1)S(1)}, u32[]{:S(2)}, u32[]{:S(2)}) %all-to-all-start.1) | async-done | bytes 131104 | tf_op jit(solution)/shard_map/all_to_all | solution.py:276
  56.6 0.0 copy-done
  56.6 0.0 copy-done.1
  56.6 0.8 shard_map.69
  57.4 2.8 %collective-permute-start.8 = (bf16[64,128]{1,0:T(8,128)(2,1)S(1)}, bf16[64,128]{1,0:T(8,128)(2,1)S(1)}, u32[]{:S(2)}, u32[]{:S(2)}) collective-permute-start(bf16[64,128]{1,0:T(8,128)(2,1)S(1)} %get-tuple-element.26.refs_0_), channel_id=1, source_target_pairs={{0,128},{32,160},{64,192},{96,224},{128,0},{160,32},{192,64},{224,... | collective-permute-start | bytes 49160 | tf_op jit(solution)/shard_map/ppermute | solution.py:195
  60.1 8.6 %all-to-all-start.2 = ((bf16[32,32,128]{2,1,0:T(8,128)(2,1)}), bf16[32,32,128]{2,1,0:T(8,128)(2,1)S(1)}, u32[]{:S(2)}, u32[]{:S(2)}) async-start(bf16[32,32,128]{2,1,0:T(8,128)(2,1)} %get-tuple-element.25), calls=%async_computation.2 | async-start | bytes 524288 | tf_op jit(solution)/shard_map/all_to_all | solution.py:280
  68.8 0.0 collective-permute-done.8.refs_1_
  68.8 0.1 collective-permute-start.9
  68.9 3.0 %collective-permute-done.9.refs_2_ = bf16[128,128]{1,0:T(8,128)(2,1)S(1)} collective-permute-done((bf16[128,128]{1,0:T(8,128)(2,1)S(1)}, bf16[128,128]{1,0:T(8,128)(2,1)S(1)}, u32[]{:S(2)}, u32[]{:S(2)}) %collective-permute-start.9) | collective-permute-done | bytes 32800 | tf_op jit(solution)/shard_map/ppermute | solution.py:195
  71.9 0.3 collective-permute-start.10
  72.2 3.7 %collective-permute-done.10.refs_3_ = bf16[256,128]{1,0:T(8,128)(2,1)S(1)} collective-permute-done((bf16[256,128]{1,0:T(8,128)(2,1)S(1)}, bf16[256,128]{1,0:T(8,128)(2,1)S(1)}, u32[]{:S(2)}, u32[]{:S(2)}) %collective-permute-start.10) | collective-permute-done | bytes 65568 | tf_op jit(solution)/shard_map/ppermute | solution.py:195
  75.9 5.8 %all-to-all-done.2.a_ref = bf16[32,32,128]{2,1,0:T(8,128)(2,1)S(1)} async-done(((bf16[32,32,128]{2,1,0:T(8,128)(2,1)}), bf16[32,32,128]{2,1,0:T(8,128)(2,1)S(1)}, u32[]{:S(2)}, u32[]{:S(2)}) %all-to-all-start.2) | async-done | bytes 262176 | tf_op jit(solution)/shard_map/all_to_all | solution.py:280
  81.7 8.5 %shard_map.71 = (bf16[32,16,128]{2,1,0:T(8,128)(2,1)S(1)}, bf16[8,80,128]{2,1,0:T(8,128)(2,1)S(1)}, f32[16,128]{1,0:T(8,128)S(1)}) custom-call(bf16[512,8192]{1,0:T(8,128)(2,1)} %n_ref.3, bf16[32,32,128]{2,1,0:T(8,128)(2,1)S(1)} %all-to-all-done.2.a_ref, bf16[64,128]{1,0:T(8,128)(2,1)S(1)} %get-tuple-element.26.refs_0_, ...), custom_call_target="tpu_custom_call" | custom-call | flops 3221225472 | bytes 8388608 | tf_op jit(solution)/shard_map/pallas_call | solution.py:174
  90.3 8.3 %all_to_all.25 = bf16[8,80,128]{2,1,0:T(8,128)(2,1)S(1)} all-to-all(bf16[8,80,128]{2,1,0:T(8,128)(2,1)S(1)} %get-tuple-element.28), channel_id=1, replica_groups=mesh['rows'=8,'cols'=32] {'rows'}, dimensions={0} | all-to-all | bytes 327680 | tf_op jit(solution)/shard_map/all_to_all | solution.py:286
  98.7 18.9 %all_to_all.26 = bf16[32,32,128]{2,1,0:T(8,128)(2,1)S(1)} all-to-all(bf16[32,32,128]{2,1,0:T(8,128)(2,1)S(1)} %pad_maximum_fusion), channel_id=1, replica_groups=mesh['rows'=8,'cols'=32] {'cols'}, dimensions={0} | all-to-all | bytes 524288 | tf_op jit(solution)/shard_map/all_to_all | solution.py:288
  117.7 0.6 multiply_subtract_fusion
  118.3 0.6 fusion.1
  (18 shorter events, 0.2 us)
Async XLA Ops:
  0.6 56.0 %copy-start = (f32[64,128]{1,0:T(8,128)S(1)}, f32[64,128]{1,0:T(8,128)}, u32[]{:S(2)}) copy-start(f32[64,128]{1,0:T(8,128)} %b_ref.3) | copy-start | bytes 98308
  0.6 56.0 %copy-start.1 = (f32[16,128]{1,0:T(8,128)S(1)}, f32[16,128]{1,0:T(8,128)}, u32[]{:S(2)}) copy-start(f32[16,128]{1,0:T(8,128)} %a_ref.3) | copy-start | bytes 24580
  2.2 15.9 %collective-permute-start = (bf16[64,128]{1,0:T(8,128)(2,1)S(1)}, bf16[64,128]{1,0:T(8,128)(2,1)S(1)}, u32[]{:S(2)}, u32[]{:S(2)}) collective-permute-start(bf16[64,128]{1,0:T(8,128)(2,1)S(1)} %get-tuple-element.19.refs_0_), channel_id=1, source_target_pairs={{0,128},{32,160},{64,192},{96,224},{128,0},{160,32},{192,64},{224,... | collective-permute-start | bytes 49160 | tf_op jit(solution)/shard_map/ppermute | solution.py:195
  6.0 22.8 %all-to-all-start = ((bf16[32,16,128]{2,1,0:T(8,128)(2,1)}), bf16[32,16,128]{2,1,0:T(8,128)(2,1)S(1)}, u32[]{:S(2)}, u32[]{:S(2)}) async-start(bf16[32,16,128]{2,1,0:T(8,128)(2,1)} %get-tuple-element.18), calls=%async_computation | async-start | bytes 262144 | tf_op jit(solution)/shard_map/all_to_all | solution.py:268
  18.1 2.9 %collective-permute-start.1 = (bf16[128,128]{1,0:T(8,128)(2,1)S(1)}, bf16[128,128]{1,0:T(8,128)(2,1)S(1)}, u32[]{:S(2)}, u32[]{:S(2)}) collective-permute-start(bf16[128,128]{1,0:T(8,128)(2,1)S(1)} %pad_maximum_fusion.2), channel_id=1, source_target_pairs={{0,64},{32,96},{64,0},{96,32},{128,192},{160,224},{192,128},{224,1... | collective-permute-start | bytes 98312 | tf_op jit(solution)/shard_map/ppermute | solution.py:195
  21.0 3.6 %collective-permute-start.2 = (bf16[256,128]{1,0:T(8,128)(2,1)S(1)}, bf16[256,128]{1,0:T(8,128)(2,1)S(1)}, u32[]{:S(2)}, u32[]{:S(2)}) collective-permute-start(bf16[256,128]{1,0:T(8,128)(2,1)S(1)} %pad_maximum_fusion.1), channel_id=1, source_target_pairs={{0,32},{32,0},{64,96},{96,64},{128,160},{160,128},{192,224},{224,1... | collective-permute-start | bytes 196616 | tf_op jit(solution)/shard_map/ppermute | solution.py:195
  38.0 7.9 %collective-permute-start.3 = (bf16[272,128]{1,0:T(8,128)(2,1)S(1)}, bf16[272,128]{1,0:T(8,128)(2,1)S(1)}, u32[]{:S(2)}, u32[]{:S(2)}) collective-permute-start(bf16[272,128]{1,0:T(8,128)(2,1)S(1)} %get-tuple-element.23), channel_id=1, source_target_pairs={{0,128},{32,160},{64,192},{96,224},{128,0},{160,32},{192,64},{224,... | collective-permute-start | bytes 208904 | tf_op jit(solution)/shard_map/ppermute | solution.py:195
  38.1 18.5 %all-to-all-start.1 = ((bf16[32,16,128]{2,1,0:T(8,128)(2,1)}), bf16[32,16,128]{2,1,0:T(8,128)(2,1)S(1)}, u32[]{:S(2)}, u32[]{:S(2)}) async-start(bf16[32,16,128]{2,1,0:T(8,128)(2,1)} %get-tuple-element.21), calls=%async_computation.1 | async-start | bytes 262144 | tf_op jit(solution)/shard_map/all_to_all | solution.py:276
  45.9 2.8 %collective-permute-start.6 = (bf16[16,128]{1,0:T(8,128)(2,1)S(1)}, bf16[16,128]{1,0:T(8,128)(2,1)S(1)}, u32[]{:S(2)}, u32[]{:S(2)}) collective-permute-start(bf16[16,128]{1,0:T(8,128)(2,1)S(1)} %fusion.3), channel_id=1, source_target_pairs={{0,64},{32,96},{64,0},{96,32},{128,192},{160,224},{192,128},{224,1... | collective-permute-start | bytes 12296 | tf_op jit(solution)/shard_map/ppermute | solution.py:195
  47.2 3.1 %collective-permute-start.4 = (bf16[128,128]{1,0:T(8,128)(2,1)S(1)}, bf16[128,128]{1,0:T(8,128)(2,1)S(1)}, u32[]{:S(2)}, u32[]{:S(2)}) collective-permute-start(bf16[128,128]{1,0:T(8,128)(2,1)S(1)} %slice.47), channel_id=1, source_target_pairs={{0,64},{32,96},{64,0},{96,32},{128,192},{160,224},{192,128},{224,1... | collective-permute-start | bytes 98312 | tf_op jit(solution)/shard_map/ppermute | solution.py:195
  48.7 2.8 %collective-permute-start.7 = (bf16[16,128]{1,0:T(8,128)(2,1)S(1)}, bf16[16,128]{1,0:T(8,128)(2,1)S(1)}, u32[]{:S(2)}, u32[]{:S(2)}) collective-permute-start(bf16[16,128]{1,0:T(8,128)(2,1)S(1)} %add_convert_fusion.2), channel_id=1, source_target_pairs={{0,32},{32,0},{64,96},{96,64},{128,160},{160,128},{192,224},{224,1... | collective-permute-start | bytes 12296 | tf_op jit(solution)/shard_map/ppermute | solution.py:195
  50.3 3.0 %collective-permute-start.5 = (bf16[64,128]{1,0:T(8,128)(2,1)S(1)}, bf16[64,128]{1,0:T(8,128)(2,1)S(1)}, u32[]{:S(2)}, u32[]{:S(2)}) collective-permute-start(bf16[64,128]{1,0:T(8,128)(2,1)S(1)} %slice.49), channel_id=1, source_target_pairs={{0,32},{32,0},{64,96},{96,64},{128,160},{160,128},{192,224},{224,1... | collective-permute-start | bytes 49160 | tf_op jit(solution)/shard_map/ppermute | solution.py:195
  57.4 11.4 %collective-permute-start.8 = (bf16[64,128]{1,0:T(8,128)(2,1)S(1)}, bf16[64,128]{1,0:T(8,128)(2,1)S(1)}, u32[]{:S(2)}, u32[]{:S(2)}) collective-permute-start(bf16[64,128]{1,0:T(8,128)(2,1)S(1)} %get-tuple-element.26.refs_0_), channel_id=1, source_target_pairs={{0,128},{32,160},{64,192},{96,224},{128,0},{160,32},{192,64},{224,... | collective-permute-start | bytes 49160 | tf_op jit(solution)/shard_map/ppermute | solution.py:195
  60.1 21.6 %all-to-all-start.2 = ((bf16[32,32,128]{2,1,0:T(8,128)(2,1)}), bf16[32,32,128]{2,1,0:T(8,128)(2,1)S(1)}, u32[]{:S(2)}, u32[]{:S(2)}) async-start(bf16[32,32,128]{2,1,0:T(8,128)(2,1)} %get-tuple-element.25), calls=%async_computation.2 | async-start | bytes 524288 | tf_op jit(solution)/shard_map/all_to_all | solution.py:280
  68.8 3.1 %collective-permute-start.9 = (bf16[128,128]{1,0:T(8,128)(2,1)S(1)}, bf16[128,128]{1,0:T(8,128)(2,1)S(1)}, u32[]{:S(2)}, u32[]{:S(2)}) collective-permute-start(bf16[128,128]{1,0:T(8,128)(2,1)S(1)} %pad_maximum_fusion.3), channel_id=1, source_target_pairs={{0,64},{32,96},{64,0},{96,32},{128,192},{160,224},{192,128},{224,1... | collective-permute-start | bytes 98312 | tf_op jit(solution)/shard_map/ppermute | solution.py:195
  71.9 4.1 %collective-permute-start.10 = (bf16[256,128]{1,0:T(8,128)(2,1)S(1)}, bf16[256,128]{1,0:T(8,128)(2,1)S(1)}, u32[]{:S(2)}, u32[]{:S(2)}) collective-permute-start(bf16[256,128]{1,0:T(8,128)(2,1)S(1)} %shard_map.70), channel_id=1, source_target_pairs={{0,32},{32,0},{64,96},{96,64},{128,160},{160,128},{192,224},{224,1... | collective-permute-start | bytes 196616 | tf_op jit(solution)/shard_map/ppermute | solution.py:195

commit v5 on v4

--- a/solution.py
+++ b/solution.py
@@ -145,12 +145,14 @@
 
 
 def last_body(rate_c, n_ref, a_ref, *refs):
-    b_refs, (c_ref, xa_ref, xb_ref, new_c_ref, acc_ref, held_ref, sems) = refs[:-7], refs[-7:]
+    b_refs, rest = refs[:-8], refs[-8:]
+    c_ref, own_ref, other_ref, xb_ref, new_c_ref, acc_ref, held_ref, sems = rest
     depth, rank = c_ref.shape
     blocks = lax.axis_size("rows")
     me = lax.axis_index("rows")
     wide = xb_ref.shape[1] - depth
-    parts, rows, _ = xa_ref.shape
+    chips, rows, _ = own_ref.shape
+    core = lax.axis_index("cols") % 2
 
     def put_b(p, value):
         xb_ref[me ^ p, :wide] = value
@@ -164,7 +166,10 @@
     grad_c = visit_blocks(
         n_ref, held_ref, sems, low_a, b_of, c, put_b, acc_ref, grad_c
     )
-    xa_ref[...] = acc_ref[...].astype(BF16).reshape(xa_ref.shape)
+    for chip in range(chips):
+        for piece_ref, which in ((own_ref, core), (other_ref, 1 - core)):
+            at = pl.multiple_of((2 * chip + which) * rows, rows)
+            piece_ref[chip] = acc_ref[pl.ds(at, rows)].astype(BF16)
     xb_ref[:, wide:] = jnp.broadcast_to(grad_c.astype(BF16)[None], (blocks, depth, rank))
 
 
@@ -197,6 +202,10 @@
 
 def copies_of(piece):
     return jnp.broadcast_to(piece[None], (lax.axis_size("cols"), *piece.shape))
+
+
+def swap_cores(piece):
+    return lax.ppermute(piece, "cols", [(i, i ^ 1) for i in range(lax.axis_size("cols"))])
 
 
 def total(pieces):
@@ -279,19 +288,27 @@
         )
     got = lax.all_to_all(copies, "cols", 0, 0)
     b_parts = gather_rows(low_b, JOIN_WEIGHT)
-    pieces_a, pieces_b, c = call(
+    shape_half = (n_cols // 2, rows_a, rank)
+    own_a, other_a, pieces_b, c = call(
         functools.partial(last_body, rate_c), counts, [got, *b_parts, c],
-        [(shape_a, BF16), ((n_rows, rows_b + depth, rank), BF16), (c.shape, F32)],
-    )
+        [(shape_half, BF16)] * 2
+        + [((n_rows, rows_b + depth, rank), BF16), (c.shape, F32)],
+    )
+    half_a = (own_a.astype(F32) + swap_cores(other_a).astype(F32)).astype(BF16)
+    pieces_b, half_a = lax.optimization_barrier((pieces_b, half_a))
     part_b = total(lax.all_to_all(pieces_b, "rows", 0, 0))
-    part_c = copies_of(part_b[rows_b:].astype(BF16))
-    sums = lax.all_to_all(jnp.concatenate([pieces_a, part_c], axis=1), "cols", 0, 0)
+    part_c = jnp.broadcast_to(part_b[None, rows_b:].astype(BF16), (n_cols // 2, depth, rank))
+    same_core = [list(range(core, n_cols, 2)) for core in range(2)]
+    sums = lax.all_to_all(
+        jnp.concatenate([half_a, part_c], axis=1), "cols", 0, 0, axis_index_groups=same_core
+    )
     sums, part_b = lax.optimization_barrier((sums, part_b))
     sums = total(sums)
+    part_c = sums[rows_a:] + swap_cores(sums[rows_a:])
     return (
         local_a - rate_a * sums[:rows_a],
         local_b - rate_b * part_b[:rows_b],
-        c - rate_c * sums[rows_a:],
+        c - rate_c * part_c,
     )
 
 

time: 119 us -> 119 us (level)
  blocking collectives: 27.3 us -> 22.7 us
  starting transfers between devices: 38.7 us -> 42 us
    all_to_all x1, blocking collectives: 18.9 us -> 14.4 us  [local(): lax.all_to_all(jnp.concatenate([half_a, part_c], axis=1), 'cols', 0, 0, a...]
    ppermute x0 -> x2, starting transfers between devices: none -> 3.31 us  [swap_cores(): lax.ppermute(piece, 'cols', [(i, i ^ 1) for i in range(lax.axis_size('col...]
  transfers between devices with their start and end apart: 14 -> 16, of which waited for: 11 -> 13; matrix products, arithmetic and copies ran while one was open for 0% -> 1% of each run, Pallas kernels for 0% -> 0%
where the time goes in v5:
time: 119 us
  starting transfers between devices  42 us (35%)
  waiting for transfers between devices  31.8 us (27%)
  blocking collectives  22.7 us (19%)
  Pallas kernels  19.9 us (17%)
  other arithmetic  1.4 us (1%)
    all_to_all x2, starting transfers between devices, local(): got = lax.all_to_all(copies, 'cols', 0, 0)  20.7 us
    pallas_call x2, Pallas kernels, call(): pl.pallas_call(body, in_specs=[pl.BlockSpec(memory_space=pltpu.HBM)] + [W...  17.6 us
    ppermute x11, waiting for transfers between devices, swap(): return lax.ppermute(piece, 'rows', [(i, i ^ bit) for i in range(n)])  17.3 us
    all_to_all x1, blocking collectives, local(): lax.all_to_all(jnp.concatenate([half_a, part_c], axis=1), 'cols', 0, 0, a...  14.4 us
    ppermute x11, starting transfers between devices, swap(): return lax.ppermute(piece, 'rows', [(i, i ^ bit) for i in range(n)])  10.3 us
    all_to_all x2, waiting for transfers between devices, local(): got = lax.all_to_all(copies, 'cols', 0, 0)  10.1 us
    all_to_all x1, blocking collectives, local(): part_b = total(lax.all_to_all(pieces_b, 'rows', 0, 0))  8.28 us
    all_to_all x1, starting transfers between devices, local(): got = lax.all_to_all(pieces_a, 'cols', 0, 0)  7.76 us
  transfers between devices with their start and end apart: 16, of which 13 were waited for; matrix products, arithmetic and copies ran while one was open for 1% of the time, Pallas kernels for 0%

profile of v5, /device:TPU:1, one launch (start us, length us, event | category | flops | bytes accessed | tf_op | source)
XLA Modules:
  0.0 118.7 jit_solution(15951987425657694253)
XLA Ops:
  0.6 0.0 copy-start
  0.6 0.0 copy-start.1
  0.7 1.5 %shard_map.67 = (bf16[32,16,128]{2,1,0:T(8,128)(2,1)}, bf16[64,128]{1,0:T(8,128)(2,1)S(1)}, f32[16,128]{1,0:T(8,128)S(1)}) custom-call(f32[16,128]{1,0:T(8,128)} %a_ref.3, f32[64,128]{1,0:T(8,128)} %b_ref.3, f32[16,128]{1,0:T(8,128)} %c_ref.1), custom_call_target="tpu_custom_call" | custom-call | tf_op jit(solution)/shard_map/pallas_call | solution.py:33
  2.2 3.8 %collective-permute-start = (bf16[64,128]{1,0:T(8,128)(2,1)S(1)}, bf16[64,128]{1,0:T(8,128)(2,1)S(1)}, u32[]{:S(2)}, u32[]{:S(2)}) collective-permute-start(bf16[64,128]{1,0:T(8,128)(2,1)S(1)} %get-tuple-element.22.refs_0_), channel_id=1, source_target_pairs={{0,128},{32,160},{64,192},{96,224},{128,0},{160,32},{192,64},{224,... | collective-permute-start | bytes 49160 | tf_op jit(solution)/shard_map/ppermute | solution.py:200
  6.0 12.0 %all-to-all-start = ((bf16[32,16,128]{2,1,0:T(8,128)(2,1)}), bf16[32,16,128]{2,1,0:T(8,128)(2,1)S(1)}, u32[]{:S(2)}, u32[]{:S(2)}) async-start(bf16[32,16,128]{2,1,0:T(8,128)(2,1)} %get-tuple-element.21), calls=%async_computation | async-start | bytes 262144 | tf_op jit(solution)/shard_map/all_to_all | solution.py:277
  18.0 0.0 collective-permute-done.refs_1_
  18.1 0.5 collective-permute-start.1
  18.5 2.4 %collective-permute-done.1.refs_2_ = bf16[128,128]{1,0:T(8,128)(2,1)S(1)} collective-permute-done((bf16[128,128]{1,0:T(8,128)(2,1)S(1)}, bf16[128,128]{1,0:T(8,128)(2,1)S(1)}, u32[]{:S(2)}, u32[]{:S(2)}) %collective-permute-start.1) | collective-permute-done | bytes 32800 | tf_op jit(solution)/shard_map/ppermute | solution.py:200
  20.9 0.3 collective-permute-start.2
  21.3 3.3 %collective-permute-done.2.refs_3_ = bf16[256,128]{1,0:T(8,128)(2,1)S(1)} collective-permute-done((bf16[256,128]{1,0:T(8,128)(2,1)S(1)}, bf16[256,128]{1,0:T(8,128)(2,1)S(1)}, u32[]{:S(2)}, u32[]{:S(2)}) %collective-permute-start.2) | collective-permute-done | bytes 65568 | tf_op jit(solution)/shard_map/ppermute | solution.py:200
  24.5 4.3 %all-to-all-done.a_ref = bf16[32,16,128]{2,1,0:T(8,128)(2,1)S(1)} async-done(((bf16[32,16,128]{2,1,0:T(8,128)(2,1)}), bf16[32,16,128]{2,1,0:T(8,128)(2,1)S(1)}, u32[]{:S(2)}, u32[]{:S(2)}) %all-to-all-start) | async-done | bytes 131104 | tf_op jit(solution)/shard_map/all_to_all | solution.py:277
  28.8 9.1 %shard_map.68 = (bf16[32,16,128]{2,1,0:T(8,128)(2,1)}, bf16[256,128]{1,0:T(8,128)(2,1)S(1)}, bf16[272,128]{1,0:T(8,128)(2,1)S(1)}) custom-call(bf16[512,8192]{1,0:T(8,128)(2,1)} %n_ref.3, bf16[32,16,128]{2,1,0:T(8,128)(2,1)S(1)} %all-to-all-done.a_ref, bf16[64,128]{1,0:T(8,128)(2,1)S(1)} %get-tuple-element.22.refs_0_, ...), custom_call_target="tpu_custom_call" | custom-call | flops 3221225472 | bytes 8388608 | tf_op jit(solution)/shard_map/pallas_call | solution.py:179
  37.9 0.1 collective-permute-start.3
  38.0 7.8 %all-to-all-start.1 = ((bf16[32,16,128]{2,1,0:T(8,128)(2,1)}), bf16[32,16,128]{2,1,0:T(8,128)(2,1)S(1)}, u32[]{:S(2)}, u32[]{:S(2)}) async-start(bf16[32,16,128]{2,1,0:T(8,128)(2,1)} %get-tuple-element.24), calls=%async_computation.1 | async-start | bytes 262144 | tf_op jit(solution)/shard_map/all_to_all | solution.py:285
  45.8 0.0 collective-permute-done.3
  45.9 1.2 %collective-permute-start.6 = (bf16[16,128]{1,0:T(8,128)(2,1)S(1)}, bf16[16,128]{1,0:T(8,128)(2,1)S(1)}, u32[]{:S(2)}, u32[]{:S(2)}) collective-permute-start(bf16[16,128]{1,0:T(8,128)(2,1)S(1)} %fusion.2), channel_id=1, source_target_pairs={{0,64},{32,96},{64,0},{96,32},{128,192},{160,224},{192,128},{224,1... | collective-permute-start | bytes 12296 | tf_op jit(solution)/shard_map/ppermute | solution.py:200
  47.1 0.4 collective-permute-start.4
  47.5 1.2 collective-permute-done.6
  48.7 0.3 collective-permute-start.7
  49.0 1.2 %collective-permute-done.4 = bf16[128,128]{1,0:T(8,128)(2,1)S(1)} collective-permute-done((bf16[128,128]{1,0:T(8,128)(2,1)S(1)}, bf16[128,128]{1,0:T(8,128)(2,1)S(1)}, u32[]{:S(2)}, u32[]{:S(2)}) %collective-permute-start.4) | collective-permute-done | bytes 32800 | tf_op jit(solution)/shard_map/ppermute | solution.py:200
  50.3 0.4 collective-permute-start.5
  50.7 0.8 collective-permute-done.7
  51.5 1.8 %collective-permute-done.5 = bf16[64,128]{1,0:T(8,128)(2,1)S(1)} collective-permute-done((bf16[64,128]{1,0:T(8,128)(2,1)S(1)}, bf16[64,128]{1,0:T(8,128)(2,1)S(1)}, u32[]{:S(2)}, u32[]{:S(2)}) %collective-permute-start.5) | collective-permute-done | bytes 16416 | tf_op jit(solution)/shard_map/ppermute | solution.py:200
  53.3 3.3 %all-to-all-done.1.got_ref = bf16[32,16,128]{2,1,0:T(8,128)(2,1)S(1)} async-done(((bf16[32,16,128]{2,1,0:T(8,128)(2,1)}), bf16[32,16,128]{2,1,0:T(8,128)(2,1)S(1)}, u32[]{:S(2)}, u32[]{:S(2)}) %all-to-all-start.1) | async-done | bytes 131104 | tf_op jit(solution)/shard_map/all_to_all | solution.py:285
  56.6 0.0 copy-done
  56.6 0.0 copy-done.1
  56.6 0.8 shard_map.69
  57.3 2.8 %collective-permute-start.8 = (bf16[64,128]{1,0:T(8,128)(2,1)S(1)}, bf16[64,128]{1,0:T(8,128)(2,1)S(1)}, u32[]{:S(2)}, u32[]{:S(2)}) collective-permute-start(bf16[64,128]{1,0:T(8,128)(2,1)S(1)} %get-tuple-element.29.refs_0_), channel_id=1, source_target_pairs={{0,128},{32,160},{64,192},{96,224},{128,0},{160,32},{192,64},{224,... | collective-permute-start | bytes 49160 | tf_op jit(solution)/shard_map/ppermute | solution.py:200
  60.1 8.6 %all-to-all-start.2 = ((bf16[32,32,128]{2,1,0:T(8,128)(2,1)}), bf16[32,32,128]{2,1,0:T(8,128)(2,1)S(1)}, u32[]{:S(2)}, u32[]{:S(2)}) async-start(bf16[32,32,128]{2,1,0:T(8,128)(2,1)} %get-tuple-element.28), calls=%async_computation.2 | async-start | bytes 524288 | tf_op jit(solution)/shard_map/all_to_all | solution.py:289
  68.7 0.0 collective-permute-done.8.refs_1_
  68.8 0.1 collective-permute-start.9
  68.9 3.0 %collective-permute-done.9.refs_2_ = bf16[128,128]{1,0:T(8,128)(2,1)S(1)} collective-permute-done((bf16[128,128]{1,0:T(8,128)(2,1)S(1)}, bf16[128,128]{1,0:T(8,128)(2,1)S(1)}, u32[]{:S(2)}, u32[]{:S(2)}) %collective-permute-start.9) | collective-permute-done | bytes 32800 | tf_op jit(solution)/shard_map/ppermute | solution.py:200
  71.8 0.3 collective-permute-start.10
  72.1 3.7 %collective-permute-done.10.refs_3_ = bf16[256,128]{1,0:T(8,128)(2,1)S(1)} collective-permute-done((bf16[256,128]{1,0:T(8,128)(2,1)S(1)}, bf16[256,128]{1,0:T(8,128)(2,1)S(1)}, u32[]{:S(2)}, u32[]{:S(2)}) %collective-permute-start.10) | collective-permute-done | bytes 65568 | tf_op jit(solution)/shard_map/ppermute | solution.py:200
  75.9 5.8 %all-to-all-done.2.a_ref = bf16[32,32,128]{2,1,0:T(8,128)(2,1)S(1)} async-done(((bf16[32,32,128]{2,1,0:T(8,128)(2,1)}), bf16[32,32,128]{2,1,0:T(8,128)(2,1)S(1)}, u32[]{:S(2)}, u32[]{:S(2)}) %all-to-all-start.2) | async-done | bytes 262176 | tf_op jit(solution)/shard_map/all_to_all | solution.py:289
  81.7 8.5 %shard_map.71 = (bf16[16,16,128]{2,1,0:T(8,128)(2,1)S(1)}, bf16[16,16,128]{2,1,0:T(8,128)(2,1)S(1)}, bf16[8,80,128]{2,1,0:T(8,128)(2,1)S(1)}, f32[16,128]{1,0:T(8,128)S(1)}) custom-call(bf16[512,8192]{1,0:T(8,128)(2,1)} %n_ref.3, bf16[32,32,128]{2,1,0:T(8,128)(2,1)S(1)} %all-to-all-done.2.a_ref, bf16[64,128]{1,0:T(8,128)(2,1)S(1)} %get-tuple-element.29.refs_0_, ...), custom_call_target="tpu_custom_call" | custom-call | flops 3221225472 | bytes 8388608 | tf_op jit(solution)/shard_map/pallas_call | solution.py:179
  90.2 0.5 collective-permute-start.11
  90.7 0.9 collective-permute-done.11
  91.6 8.3 %all_to_all.25 = bf16[8,80,128]{2,1,0:T(8,128)(2,1)S(1)} all-to-all(bf16[8,80,128]{2,1,0:T(8,128)(2,1)S(1)} %get-tuple-element.34), channel_id=1, replica_groups=mesh['rows'=8,'cols'=32] {'rows'}, dimensions={0} | all-to-all | bytes 327680 | tf_op jit(solution)/shard_map/all_to_all | solution.py:299
  100.0 14.4 %all_to_all.26 = bf16[16,32,128]{2,1,0:T(8,128)(2,1)S(1)} all-to-all(bf16[16,32,128]{2,1,0:T(8,128)(2,1)S(1)} %pad_maximum_fusion), channel_id=1, replica_groups={{0,2,4,6,8,10,12,14,16,18,20,22,24,26,28,30},{1,3,5,7,9,11,13,15,17,19,..., dimensions={0} | all-to-all | bytes 262144 | tf_op jit(solution)/shard_map/all_to_all | solution.py:302
  114.4 2.8 %collective-permute-start.12 = (f32[16,128]{1,0:T(8,128)S(1)}, f32[16,128]{1,0:T(8,128)S(1)}, u32[]{:S(2)}, u32[]{:S(2)}) collective-permute-start(f32[16,128]{1,0:T(8,128)S(1)} %slice.54), channel_id=1, source_target_pairs={{0,1},{1,0},{2,3},{3,2},{4,5},{5,4},{6,7},{7,6},{8,9},{9,8},{10,11... | collective-permute-start | bytes 24584 | tf_op jit(solution)/shard_map/ppermute | solution.py:208
  117.2 0.6 multiply_subtract_fusion
  117.9 0.2 collective-permute-done.12
  118.1 0.6 multiply_subtract_fusion.1
  (20 shorter events, 0.2 us)
Async XLA Ops:
  0.6 55.9 %copy-start = (f32[64,128]{1,0:T(8,128)S(1)}, f32[64,128]{1,0:T(8,128)}, u32[]{:S(2)}) copy-start(f32[64,128]{1,0:T(8,128)} %b_ref.3) | copy-start | bytes 98308
  0.6 55.9 %copy-start.1 = (f32[16,128]{1,0:T(8,128)S(1)}, f32[16,128]{1,0:T(8,128)}, u32[]{:S(2)}) copy-start(f32[16,128]{1,0:T(8,128)} %a_ref.3) | copy-start | bytes 24580
  2.2 15.9 %collective-permute-start = (bf16[64,128]{1,0:T(8,128)(2,1)S(1)}, bf16[64,128]{1,0:T(8,128)(2,1)S(1)}, u32[]{:S(2)}, u32[]{:S(2)}) collective-permute-start(bf16[64,128]{1,0:T(8,128)(2,1)S(1)} %get-tuple-element.22.refs_0_), channel_id=1, source_target_pairs={{0,128},{32,160},{64,192},{96,224},{128,0},{160,32},{192,64},{224,... | collective-permute-start | bytes 49160 | tf_op jit(solution)/shard_map/ppermute | solution.py:200
  6.0 22.8 %all-to-all-start = ((bf16[32,16,128]{2,1,0:T(8,128)(2,1)}), bf16[32,16,128]{2,1,0:T(8,128)(2,1)S(1)}, u32[]{:S(2)}, u32[]{:S(2)}) async-start(bf16[32,16,128]{2,1,0:T(8,128)(2,1)} %get-tuple-element.21), calls=%async_computation | async-start | bytes 262144 | tf_op jit(solution)/shard_map/all_to_all | solution.py:277
  18.1 2.9 %collective-permute-start.1 = (bf16[128,128]{1,0:T(8,128)(2,1)S(1)}, bf16[128,128]{1,0:T(8,128)(2,1)S(1)}, u32[]{:S(2)}, u32[]{:S(2)}) collective-permute-start(bf16[128,128]{1,0:T(8,128)(2,1)S(1)} %pad_maximum_fusion.2), channel_id=1, source_target_pairs={{0,64},{32,96},{64,0},{96,32},{128,192},{160,224},{192,128},{224,1... | collective-permute-start | bytes 98312 | tf_op jit(solution)/shard_map/ppermute | solution.py:200
  20.9 3.6 %collective-permute-start.2 = (bf16[256,128]{1,0:T(8,128)(2,1)S(1)}, bf16[256,128]{1,0:T(8,128)(2,1)S(1)}, u32[]{:S(2)}, u32[]{:S(2)}) collective-permute-start(bf16[256,128]{1,0:T(8,128)(2,1)S(1)} %pad_maximum_fusion.1), channel_id=1, source_target_pairs={{0,32},{32,0},{64,96},{96,64},{128,160},{160,128},{192,224},{224,1... | collective-permute-start | bytes 196616 | tf_op jit(solution)/shard_map/ppermute | solution.py:200
  37.9 7.9 %collective-permute-start.3 = (bf16[272,128]{1,0:T(8,128)(2,1)S(1)}, bf16[272,128]{1,0:T(8,128)(2,1)S(1)}, u32[]{:S(2)}, u32[]{:S(2)}) collective-permute-start(bf16[272,128]{1,0:T(8,128)(2,1)S(1)} %get-tuple-element.26), channel_id=1, source_target_pairs={{0,128},{32,160},{64,192},{96,224},{128,0},{160,32},{192,64},{224,... | collective-permute-start | bytes 208904 | tf_op jit(solution)/shard_map/ppermute | solution.py:200
  38.0 18.5 %all-to-all-start.1 = ((bf16[32,16,128]{2,1,0:T(8,128)(2,1)}), bf16[32,16,128]{2,1,0:T(8,128)(2,1)S(1)}, u32[]{:S(2)}, u32[]{:S(2)}) async-start(bf16[32,16,128]{2,1,0:T(8,128)(2,1)} %get-tuple-element.24), calls=%async_computation.1 | async-start | bytes 262144 | tf_op jit(solution)/shard_map/all_to_all | solution.py:285
  45.9 2.8 %collective-permute-start.6 = (bf16[16,128]{1,0:T(8,128)(2,1)S(1)}, bf16[16,128]{1,0:T(8,128)(2,1)S(1)}, u32[]{:S(2)}, u32[]{:S(2)}) collective-permute-start(bf16[16,128]{1,0:T(8,128)(2,1)S(1)} %fusion.2), channel_id=1, source_target_pairs={{0,64},{32,96},{64,0},{96,32},{128,192},{160,224},{192,128},{224,1... | collective-permute-start | bytes 12296 | tf_op jit(solution)/shard_map/ppermute | solution.py:200
  47.1 3.1 %collective-permute-start.4 = (bf16[128,128]{1,0:T(8,128)(2,1)S(1)}, bf16[128,128]{1,0:T(8,128)(2,1)S(1)}, u32[]{:S(2)}, u32[]{:S(2)}) collective-permute-start(bf16[128,128]{1,0:T(8,128)(2,1)S(1)} %slice.48), channel_id=1, source_target_pairs={{0,64},{32,96},{64,0},{96,32},{128,192},{160,224},{192,128},{224,1... | collective-permute-start | bytes 98312 | tf_op jit(solution)/shard_map/ppermute | solution.py:200
  48.7 2.8 %collective-permute-start.7 = (bf16[16,128]{1,0:T(8,128)(2,1)S(1)}, bf16[16,128]{1,0:T(8,128)(2,1)S(1)}, u32[]{:S(2)}, u32[]{:S(2)}) collective-permute-start(bf16[16,128]{1,0:T(8,128)(2,1)S(1)} %add_convert_fusion.3), channel_id=1, source_target_pairs={{0,32},{32,0},{64,96},{96,64},{128,160},{160,128},{192,224},{224,1... | collective-permute-start | bytes 12296 | tf_op jit(solution)/shard_map/ppermute | solution.py:200
  50.3 3.0 %collective-permute-start.5 = (bf16[64,128]{1,0:T(8,128)(2,1)S(1)}, bf16[64,128]{1,0:T(8,128)(2,1)S(1)}, u32[]{:S(2)}, u32[]{:S(2)}) collective-permute-start(bf16[64,128]{1,0:T(8,128)(2,1)S(1)} %slice.50), channel_id=1, source_target_pairs={{0,32},{32,0},{64,96},{96,64},{128,160},{160,128},{192,224},{224,1... | collective-permute-start | bytes 49160 | tf_op jit(solution)/shard_map/ppermute | solution.py:200
  57.3 11.4 %collective-permute-start.8 = (bf16[64,128]{1,0:T(8,128)(2,1)S(1)}, bf16[64,128]{1,0:T(8,128)(2,1)S(1)}, u32[]{:S(2)}, u32[]{:S(2)}) collective-permute-start(bf16[64,128]{1,0:T(8,128)(2,1)S(1)} %get-tuple-element.29.refs_0_), channel_id=1, source_target_pairs={{0,128},{32,160},{64,192},{96,224},{128,0},{160,32},{192,64},{224,... | collective-permute-start | bytes 49160 | tf_op jit(solution)/shard_map/ppermute | solution.py:200
  60.1 21.6 %all-to-all-start.2 = ((bf16[32,32,128]{2,1,0:T(8,128)(2,1)}), bf16[32,32,128]{2,1,0:T(8,128)(2,1)S(1)}, u32[]{:S(2)}, u32[]{:S(2)}) async-start(bf16[32,32,128]{2,1,0:T(8,128)(2,1)} %get-tuple-element.28), calls=%async_computation.2 | async-start | bytes 524288 | tf_op jit(solution)/shard_map/all_to_all | solution.py:289
  68.8 3.1 %collective-permute-start.9 = (bf16[128,128]{1,0:T(8,128)(2,1)S(1)}, bf16[128,128]{1,0:T(8,128)(2,1)S(1)}, u32[]{:S(2)}, u32[]{:S(2)}) collective-permute-start(bf16[128,128]{1,0:T(8,128)(2,1)S(1)} %pad_maximum_fusion.3), channel_id=1, source_target_pairs={{0,64},{32,96},{64,0},{96,32},{128,192},{160,224},{192,128},{224,1... | collective-permute-start | bytes 98312 | tf_op jit(solution)/shard_map/ppermute | solution.py:200
  71.8 4.1 %collective-permute-start.10 = (bf16[256,128]{1,0:T(8,128)(2,1)S(1)}, bf16[256,128]{1,0:T(8,128)(2,1)S(1)}, u32[]{:S(2)}, u32[]{:S(2)}) collective-permute-start(bf16[256,128]{1,0:T(8,128)(2,1)S(1)} %shard_map.70), channel_id=1, source_target_pairs={{0,32},{32,0},{64,96},{96,64},{128,160},{160,128},{192,224},{224,1... | collective-permute-start | bytes 196616 | tf_op jit(solution)/shard_map/ppermute | solution.py:200
  90.2 1.4 %collective-permute-start.11 = (bf16[16,16,128]{2,1,0:T(8,128)(2,1)S(1)}, bf16[16,16,128]{2,1,0:T(8,128)(2,1)S(1)}, u32[]{:S(2)}, u32[]{:S(2)}) collective-permute-start(bf16[16,16,128]{2,1,0:T(8,128)(2,1)S(1)} %get-tuple-element.32), channel_id=1, source_target_pairs={{0,1},{1,0},{2,3},{3,2},{4,5},{5,4},{6,7},{7,6},{8,9},{9,8},{10,11... | collective-permute-start | bytes 196616 | tf_op jit(solution)/shard_map/ppermute | solution.py:208
  114.4 3.7 %collective-permute-start.12 = (f32[16,128]{1,0:T(8,128)S(1)}, f32[16,128]{1,0:T(8,128)S(1)}, u32[]{:S(2)}, u32[]{:S(2)}) collective-permute-start(f32[16,128]{1,0:T(8,128)S(1)} %slice.54), channel_id=1, source_target_pairs={{0,1},{1,0},{2,3},{3,2},{4,5},{5,4},{6,7},{7,6},{8,9},{9,8},{10,11... | collective-permute-start | bytes 24584 | tf_op jit(solution)/shard_map/ppermute | solution.py:208

commit v6 on v4

--- a/solution.py
+++ b/solution.py
@@ -144,28 +144,51 @@
     far_ref[half:] = grad_c.astype(BF16)
 
 
-def last_body(rate_c, n_ref, a_ref, *refs):
-    b_refs, (c_ref, xa_ref, xb_ref, new_c_ref, acc_ref, held_ref, sems) = refs[:-7], refs[-7:]
-    depth, rank = c_ref.shape
+def last_body(rate_c, n_ref, got_ref, *refs):
+    b_refs, rest = refs[:-8], refs[-8:]
+    c_ref, own_ref, other_ref, xb_ref, new_c_ref, acc_ref, held_ref, sems = rest
     blocks = lax.axis_size("rows")
     me = lax.axis_index("rows")
-    wide = xb_ref.shape[1] - depth
-    parts, rows, _ = xa_ref.shape
-
-    def put_b(p, value):
-        xb_ref[me ^ p, :wide] = value
+    core = lax.axis_index("cols") % 2
+    wide = xb_ref.shape[1]
+    chips, rows = got_ref.shape[0] // 2, own_ref.shape[1]
+
+    def put_b(x, value):
+        xb_ref[me ^ x] = value
 
     acc_ref[...] = jnp.zeros_like(acc_ref)
-    low_a = a_ref[:, :rows].reshape(acc_ref.shape)
-    c = c_ref[...] - rate_c * jnp.sum(a_ref[:, rows:].astype(F32), axis=0)
+    low_a = got_ref[:, :rows].reshape(acc_ref.shape)
+    c = c_ref[...] - rate_c * total(got_ref[:, rows:])
     new_c_ref[...] = c
     b_of = parts_of(b_refs, wide)
     grad_c = jnp.zeros(c.shape, F32)
     grad_c = visit_blocks(
         n_ref, held_ref, sems, low_a, b_of, c, put_b, acc_ref, grad_c
     )
-    xa_ref[...] = acc_ref[...].astype(BF16).reshape(xa_ref.shape)
-    xb_ref[:, wide:] = jnp.broadcast_to(grad_c.astype(BF16)[None], (blocks, depth, rank))
+    for chip in range(chips):
+        for piece_ref, which in ((own_ref, core), (other_ref, 1 - core)):
+            at = pl.multiple_of((2 * chip + which) * rows, rows)
+            piece_ref[chip] = acc_ref[pl.ds(at, rows)].astype(BF16)
+    for piece_ref in (own_ref, other_ref):
+        piece_ref[chips] = grad_c.astype(BF16)
+
+
+def finish_body(rates, got_ref, part_b_ref, a_ref, b_ref, c_ref, out_a_ref, out_b_ref, out_c_ref):
+    rows_a, rows_b = out_a_ref.shape[0], out_b_ref.shape[0]
+    sums = total(got_ref[...])
+    out_a_ref[...] = a_ref[...] - rates[0] * sums[:rows_a]
+    out_b_ref[...] = b_ref[...] - rates[1] * part_b_ref[:rows_b]
+    out_c_ref[...] = c_ref[...] - rates[2] * sums[rows_a:]
+
+
+def finish(rates, got, part_b, *factors):
+    return pl.pallas_call(
+        functools.partial(finish_body, rates),
+        in_specs=[WHOLE] * 5,
+        out_specs=[WHOLE] * 3,
+        out_shape=[jax.ShapeDtypeStruct(x.shape, F32) for x in factors],
+        compiler_params=pltpu.CompilerParams(vmem_limit_bytes=2 << 20),
+    )(got, part_b, *factors)
 
 
 def call(body, counts, operands, outs):
@@ -195,8 +218,14 @@
     return lax.ppermute(piece, "rows", [(i, i ^ bit) for i in range(n)])
 
 
-def copies_of(piece):
-    return jnp.broadcast_to(piece[None], (lax.axis_size("cols"), *piece.shape))
+def swap_cores(piece):
+    return lax.ppermute(piece, "cols", [(i, i ^ 1) for i in range(lax.axis_size("cols"))])
+
+
+def exchange_chips(pieces):
+    n = lax.axis_size("cols")
+    groups = [list(range(core, n, 2)) for core in range(2)]
+    return lax.all_to_all(pieces, "cols", 0, 0, axis_index_groups=groups)
 
 
 def total(pieces):
@@ -279,20 +308,19 @@
         )
     got = lax.all_to_all(copies, "cols", 0, 0)
     b_parts = gather_rows(low_b, JOIN_WEIGHT)
-    pieces_a, pieces_b, c = call(
+    shape_half = (n_cols // 2 + 1, rows_a, rank)
+    own, other, pieces_b, c = call(
         functools.partial(last_body, rate_c), counts, [got, *b_parts, c],
-        [(shape_a, BF16), ((n_rows, rows_b + depth, rank), BF16), (c.shape, F32)],
+        [(shape_half, BF16)] * 2 + [((n_rows, rows_b, rank), BF16), (c.shape, F32)],
     )
+    own = (own.astype(F32) + swap_cores(other).astype(F32)).astype(BF16)
+    low_c = jnp.broadcast_to(own[-1:], (n_rows, depth, rank))
+    pieces_b = jnp.concatenate([pieces_b, low_c], axis=1)
+    pieces_b, half_a = lax.optimization_barrier((pieces_b, own[:-1]))
     part_b = total(lax.all_to_all(pieces_b, "rows", 0, 0))
-    part_c = copies_of(part_b[rows_b:].astype(BF16))
-    sums = lax.all_to_all(jnp.concatenate([pieces_a, part_c], axis=1), "cols", 0, 0)
-    sums, part_b = lax.optimization_barrier((sums, part_b))
-    sums = total(sums)
-    return (
-        local_a - rate_a * sums[:rows_a],
-        local_b - rate_b * part_b[:rows_b],
-        c - rate_c * sums[rows_a:],
-    )
+    low_c = jnp.broadcast_to(part_b[None, rows_b:].astype(BF16), (n_cols // 2, depth, rank))
+    got = exchange_chips(jnp.concatenate([half_a, low_c], axis=1))
+    return tuple(finish((rate_a, rate_b, rate_c), got, part_b, local_a, local_b, c))
 
 
 def solution(mesh):

time: 119 us -> 116 us (0.975)
  blocking collectives: 27.3 us -> 22.7 us
  other arithmetic: 1.41 us -> 0.16 us
    all_to_all x1, blocking collectives: 18.9 us -> 14.4 us  [exchange_chips(): return lax.all_to_all(pieces, 'cols', 0, 0, axis_index_groups=groups)]
    sub x2 -> x0, other arithmetic: 1.23 us -> none  [the longest x1 0.62 us: local(): local_b - rate_b * part_b[:rows_b]]
  transfers between devices with their start and end apart: 14 -> 15, of which waited for: 11 -> 12; matrix products, arithmetic and copies ran while one was open for 0% -> 0% of each run, Pallas kernels for 0% -> 0%
where the time goes in v6:
time: 116 us; the launch traced here: 115 us
  starting transfers between devices  39.2 us (34%)
  waiting for transfers between devices  31.6 us (27%)
  blocking collectives  22.7 us (20%)
  Pallas kernels  20.5 us (18%)
    all_to_all x2, starting transfers between devices, local(): got = lax.all_to_all(copies, 'cols', 0, 0)  20.7 us
    pallas_call x2, Pallas kernels, call(): pl.pallas_call(body, in_specs=[pl.BlockSpec(memory_space=pltpu.HBM)] + [W...  17.6 us
    ppermute x11, waiting for transfers between devices, swap(): return lax.ppermute(piece, 'rows', [(i, i ^ bit) for i in range(n)])  17.3 us
    all_to_all x1, blocking collectives, exchange_chips(): return lax.all_to_all(pieces, 'cols', 0, 0, axis_index_groups=groups)  14.4 us
    ppermute x11, starting transfers between devices, swap(): return lax.ppermute(piece, 'rows', [(i, i ^ bit) for i in range(n)])  10.3 us
    all_to_all x2, waiting for transfers between devices, local(): got = lax.all_to_all(copies, 'cols', 0, 0)  10.1 us
    all_to_all x1, blocking collectives, local(): part_b = total(lax.all_to_all(pieces_b, 'rows', 0, 0))  8.28 us
    all_to_all x1, starting transfers between devices, local(): got = lax.all_to_all(pieces_a, 'cols', 0, 0)  7.75 us
  transfers between devices with their start and end apart: 15, of which 12 were waited for; matrix products, arithmetic and copies ran while one was open for 0% of the time, Pallas kernels for 0%

profile of v6, /device:TPU:1, one launch (start us, length us, event | category | flops | bytes accessed | tf_op | source)
XLA Modules:
  0.0 115.0 jit_solution(7573441550183058980)
XLA Ops:
  0.6 0.0 copy-start
  0.6 0.0 copy-start.1
  0.7 1.5 %shard_map.67 = (bf16[32,16,128]{2,1,0:T(8,128)(2,1)}, bf16[64,128]{1,0:T(8,128)(2,1)S(1)}, f32[16,128]{1,0:T(8,128)S(1)}) custom-call(f32[16,128]{1,0:T(8,128)} %a_ref.3, f32[64,128]{1,0:T(8,128)} %b_ref.3, f32[16,128]{1,0:T(8,128)} %c_ref.1), custom_call_target="tpu_custom_call" | custom-call | tf_op jit(solution)/shard_map/pallas_call | solution.py:33
  2.2 3.8 %collective-permute-start = (bf16[64,128]{1,0:T(8,128)(2,1)S(1)}, bf16[64,128]{1,0:T(8,128)(2,1)S(1)}, u32[]{:S(2)}, u32[]{:S(2)}) collective-permute-start(bf16[64,128]{1,0:T(8,128)(2,1)S(1)} %get-tuple-element.20.refs_0_), channel_id=1, source_target_pairs={{0,128},{32,160},{64,192},{96,224},{128,0},{160,32},{192,64},{224,... | collective-permute-start | bytes 49160 | tf_op jit(solution)/shard_map/ppermute | solution.py:218
  6.0 12.0 %all-to-all-start = ((bf16[32,16,128]{2,1,0:T(8,128)(2,1)}), bf16[32,16,128]{2,1,0:T(8,128)(2,1)S(1)}, u32[]{:S(2)}, u32[]{:S(2)}) async-start(bf16[32,16,128]{2,1,0:T(8,128)(2,1)} %get-tuple-element.19), calls=%async_computation | async-start | bytes 262144 | tf_op jit(solution)/shard_map/all_to_all | solution.py:297
  18.0 0.0 collective-permute-done.refs_1_
  18.0 0.5 collective-permute-start.1
  18.5 2.4 %collective-permute-done.1.refs_2_ = bf16[128,128]{1,0:T(8,128)(2,1)S(1)} collective-permute-done((bf16[128,128]{1,0:T(8,128)(2,1)S(1)}, bf16[128,128]{1,0:T(8,128)(2,1)S(1)}, u32[]{:S(2)}, u32[]{:S(2)}) %collective-permute-start.1) | collective-permute-done | bytes 32800 | tf_op jit(solution)/shard_map/ppermute | solution.py:218
  20.9 0.3 collective-permute-start.2
  21.2 3.3 %collective-permute-done.2.refs_3_ = bf16[256,128]{1,0:T(8,128)(2,1)S(1)} collective-permute-done((bf16[256,128]{1,0:T(8,128)(2,1)S(1)}, bf16[256,128]{1,0:T(8,128)(2,1)S(1)}, u32[]{:S(2)}, u32[]{:S(2)}) %collective-permute-start.2) | collective-permute-done | bytes 65568 | tf_op jit(solution)/shard_map/ppermute | solution.py:218
  24.5 4.3 %all-to-all-done.a_ref = bf16[32,16,128]{2,1,0:T(8,128)(2,1)S(1)} async-done(((bf16[32,16,128]{2,1,0:T(8,128)(2,1)}), bf16[32,16,128]{2,1,0:T(8,128)(2,1)S(1)}, u32[]{:S(2)}, u32[]{:S(2)}) %all-to-all-start) | async-done | bytes 131104 | tf_op jit(solution)/shard_map/all_to_all | solution.py:297
  28.8 9.1 %shard_map.68 = (bf16[32,16,128]{2,1,0:T(8,128)(2,1)}, bf16[256,128]{1,0:T(8,128)(2,1)S(1)}, bf16[272,128]{1,0:T(8,128)(2,1)S(1)}) custom-call(bf16[512,8192]{1,0:T(8,128)(2,1)} %n_ref.3, bf16[32,16,128]{2,1,0:T(8,128)(2,1)S(1)} %all-to-all-done.a_ref, bf16[64,128]{1,0:T(8,128)(2,1)S(1)} %get-tuple-element.20.refs_0_, ...), custom_call_target="tpu_custom_call" | custom-call | flops 3221225472 | bytes 8388608 | tf_op jit(solution)/shard_map/pallas_call | solution.py:197
  37.9 0.1 collective-permute-start.3
  38.0 7.8 %all-to-all-start.1 = ((bf16[32,16,128]{2,1,0:T(8,128)(2,1)}), bf16[32,16,128]{2,1,0:T(8,128)(2,1)S(1)}, u32[]{:S(2)}, u32[]{:S(2)}) async-start(bf16[32,16,128]{2,1,0:T(8,128)(2,1)} %get-tuple-element.22), calls=%async_computation.1 | async-start | bytes 262144 | tf_op jit(solution)/shard_map/all_to_all | solution.py:305
  45.8 0.0 collective-permute-done.3
  45.8 1.2 %collective-permute-start.6 = (bf16[16,128]{1,0:T(8,128)(2,1)S(1)}, bf16[16,128]{1,0:T(8,128)(2,1)S(1)}, u32[]{:S(2)}, u32[]{:S(2)}) collective-permute-start(bf16[16,128]{1,0:T(8,128)(2,1)S(1)} %fusion.1), channel_id=1, source_target_pairs={{0,64},{32,96},{64,0},{96,32},{128,192},{160,224},{192,128},{224,1... | collective-permute-start | bytes 12296 | tf_op jit(solution)/shard_map/ppermute | solution.py:218
  47.1 0.4 collective-permute-start.4
  47.5 1.2 %collective-permute-done.6 = bf16[16,128]{1,0:T(8,128)(2,1)S(1)} collective-permute-done((bf16[16,128]{1,0:T(8,128)(2,1)S(1)}, bf16[16,128]{1,0:T(8,128)(2,1)S(1)}, u32[]{:S(2)}, u32[]{:S(2)}) %collective-permute-start.6) | collective-permute-done | bytes 4128 | tf_op jit(solution)/shard_map/ppermute | solution.py:218
  48.7 0.3 collective-permute-start.7
  49.0 1.2 %collective-permute-done.4 = bf16[128,128]{1,0:T(8,128)(2,1)S(1)} collective-permute-done((bf16[128,128]{1,0:T(8,128)(2,1)S(1)}, bf16[128,128]{1,0:T(8,128)(2,1)S(1)}, u32[]{:S(2)}, u32[]{:S(2)}) %collective-permute-start.4) | collective-permute-done | bytes 32800 | tf_op jit(solution)/shard_map/ppermute | solution.py:218
  50.3 0.4 collective-permute-start.5
  50.7 0.8 collective-permute-done.7
  51.4 1.8 %collective-permute-done.5 = bf16[64,128]{1,0:T(8,128)(2,1)S(1)} collective-permute-done((bf16[64,128]{1,0:T(8,128)(2,1)S(1)}, bf16[64,128]{1,0:T(8,128)(2,1)S(1)}, u32[]{:S(2)}, u32[]{:S(2)}) %collective-permute-start.5) | collective-permute-done | bytes 16416 | tf_op jit(solution)/shard_map/ppermute | solution.py:218
  53.3 3.3 %all-to-all-done.1.got_ref = bf16[32,16,128]{2,1,0:T(8,128)(2,1)S(1)} async-done(((bf16[32,16,128]{2,1,0:T(8,128)(2,1)}), bf16[32,16,128]{2,1,0:T(8,128)(2,1)S(1)}, u32[]{:S(2)}, u32[]{:S(2)}) %all-to-all-start.1) | async-done | bytes 131104 | tf_op jit(solution)/shard_map/all_to_all | solution.py:305
  56.6 0.0 copy-done
  56.6 0.0 copy-done.1
  56.6 0.8 shard_map.69
  57.3 2.8 %collective-permute-start.8 = (bf16[64,128]{1,0:T(8,128)(2,1)S(1)}, bf16[64,128]{1,0:T(8,128)(2,1)S(1)}, u32[]{:S(2)}, u32[]{:S(2)}) collective-permute-start(bf16[64,128]{1,0:T(8,128)(2,1)S(1)} %get-tuple-element.26.refs_0_), channel_id=1, source_target_pairs={{0,128},{32,160},{64,192},{96,224},{128,0},{160,32},{192,64},{224,... | collective-permute-start | bytes 49160 | tf_op jit(solution)/shard_map/ppermute | solution.py:218
  60.1 8.6 %all-to-all-start.2 = ((bf16[32,32,128]{2,1,0:T(8,128)(2,1)}), bf16[32,32,128]{2,1,0:T(8,128)(2,1)S(1)}, u32[]{:S(2)}, u32[]{:S(2)}) async-start(bf16[32,32,128]{2,1,0:T(8,128)(2,1)} %get-tuple-element.25), calls=%async_computation.2 | async-start | bytes 524288 | tf_op jit(solution)/shard_map/all_to_all | solution.py:309
  68.7 0.0 collective-permute-done.8.refs_1_
  68.7 0.1 collective-permute-start.9
  68.8 3.0 %collective-permute-done.9.refs_2_ = bf16[128,128]{1,0:T(8,128)(2,1)S(1)} collective-permute-done((bf16[128,128]{1,0:T(8,128)(2,1)S(1)}, bf16[128,128]{1,0:T(8,128)(2,1)S(1)}, u32[]{:S(2)}, u32[]{:S(2)}) %collective-permute-start.9) | collective-permute-done | bytes 32800 | tf_op jit(solution)/shard_map/ppermute | solution.py:218
  71.8 0.3 collective-permute-start.10
  72.1 3.7 %collective-permute-done.10.refs_3_ = bf16[256,128]{1,0:T(8,128)(2,1)S(1)} collective-permute-done((bf16[256,128]{1,0:T(8,128)(2,1)S(1)}, bf16[256,128]{1,0:T(8,128)(2,1)S(1)}, u32[]{:S(2)}, u32[]{:S(2)}) %collective-permute-start.10) | collective-permute-done | bytes 65568 | tf_op jit(solution)/shard_map/ppermute | solution.py:218
  75.9 5.8 %all-to-all-done.2.got_ref = bf16[32,32,128]{2,1,0:T(8,128)(2,1)S(1)} async-done(((bf16[32,32,128]{2,1,0:T(8,128)(2,1)}), bf16[32,32,128]{2,1,0:T(8,128)(2,1)S(1)}, u32[]{:S(2)}, u32[]{:S(2)}) %all-to-all-start.2) | async-done | bytes 262176 | tf_op jit(solution)/shard_map/all_to_all | solution.py:309
  81.7 8.5 %shard_map.71 = (bf16[17,16,128]{2,1,0:T(8,128)(2,1)S(1)}, bf16[17,16,128]{2,1,0:T(8,128)(2,1)S(1)}, bf16[8,64,128]{2,1,0:T(8,128)(2,1)S(1)}, f32[16,128]{1,0:T(8,128)S(1)}) custom-call(bf16[512,8192]{1,0:T(8,128)(2,1)} %n_ref.3, bf16[32,32,128]{2,1,0:T(8,128)(2,1)S(1)} %all-to-all-done.2.got_ref, bf16[64,128]{1,0:T(8,128)(2,1)S(1)} %get-tuple-element.26.refs_0_, ...), custom_call_target="tpu_custom_call" | custom-call | flops 3221225472 | bytes 8388608 | tf_op jit(solution)/shard_map/pallas_call | solution.py:197
  90.2 0.5 collective-permute-start.11
  90.7 0.9 collective-permute-done.11
  91.7 8.3 %all_to_all.25 = bf16[8,80,128]{2,1,0:T(8,128)(2,1)S(1)} all-to-all(bf16[8,80,128]{2,1,0:T(8,128)(2,1)S(1)} %pad_maximum_fusion), channel_id=1, replica_groups=mesh['rows'=8,'cols'=32] {'rows'}, dimensions={0} | all-to-all | bytes 327680 | tf_op jit(solution)/shard_map/all_to_all | solution.py:320
  100.0 14.4 %all_to_all.26.got_ref = bf16[16,32,128]{2,1,0:T(8,128)(2,1)S(1)} all-to-all(bf16[16,32,128]{2,1,0:T(8,128)(2,1)S(1)} %pad_maximum_fusion.1), channel_id=1, replica_groups={{0,2,4,6,8,10,12,14,16,18,20,22,24,26,28,30},{1,3,5,7,9,11,13,15,17,19,..., dimensions={0} | all-to-all | bytes 262144 | tf_op jit(solution)/shard_map/all_to_all | solution.py:228
  114.4 0.6 shard_map.72
  (22 shorter events, 0.2 us)
Async XLA Ops:
  0.6 55.9 %copy-start = (f32[64,128]{1,0:T(8,128)S(1)}, f32[64,128]{1,0:T(8,128)}, u32[]{:S(2)}) copy-start(f32[64,128]{1,0:T(8,128)} %b_ref.3) | copy-start | bytes 98308
  0.6 55.9 %copy-start.1 = (f32[16,128]{1,0:T(8,128)S(1)}, f32[16,128]{1,0:T(8,128)}, u32[]{:S(2)}) copy-start(f32[16,128]{1,0:T(8,128)} %a_ref.3) | copy-start | bytes 24580
  2.2 15.9 %collective-permute-start = (bf16[64,128]{1,0:T(8,128)(2,1)S(1)}, bf16[64,128]{1,0:T(8,128)(2,1)S(1)}, u32[]{:S(2)}, u32[]{:S(2)}) collective-permute-start(bf16[64,128]{1,0:T(8,128)(2,1)S(1)} %get-tuple-element.20.refs_0_), channel_id=1, source_target_pairs={{0,128},{32,160},{64,192},{96,224},{128,0},{160,32},{192,64},{224,... | collective-permute-start | bytes 49160 | tf_op jit(solution)/shard_map/ppermute | solution.py:218
  6.0 22.8 %all-to-all-start = ((bf16[32,16,128]{2,1,0:T(8,128)(2,1)}), bf16[32,16,128]{2,1,0:T(8,128)(2,1)S(1)}, u32[]{:S(2)}, u32[]{:S(2)}) async-start(bf16[32,16,128]{2,1,0:T(8,128)(2,1)} %get-tuple-element.19), calls=%async_computation | async-start | bytes 262144 | tf_op jit(solution)/shard_map/all_to_all | solution.py:297
  18.0 2.9 %collective-permute-start.1 = (bf16[128,128]{1,0:T(8,128)(2,1)S(1)}, bf16[128,128]{1,0:T(8,128)(2,1)S(1)}, u32[]{:S(2)}, u32[]{:S(2)}) collective-permute-start(bf16[128,128]{1,0:T(8,128)(2,1)S(1)} %pad_maximum_fusion.3), channel_id=1, source_target_pairs={{0,64},{32,96},{64,0},{96,32},{128,192},{160,224},{192,128},{224,1... | collective-permute-start | bytes 98312 | tf_op jit(solution)/shard_map/ppermute | solution.py:218
  20.9 3.6 %collective-permute-start.2 = (bf16[256,128]{1,0:T(8,128)(2,1)S(1)}, bf16[256,128]{1,0:T(8,128)(2,1)S(1)}, u32[]{:S(2)}, u32[]{:S(2)}) collective-permute-start(bf16[256,128]{1,0:T(8,128)(2,1)S(1)} %pad_maximum_fusion.2), channel_id=1, source_target_pairs={{0,32},{32,0},{64,96},{96,64},{128,160},{160,128},{192,224},{224,1... | collective-permute-start | bytes 196616 | tf_op jit(solution)/shard_map/ppermute | solution.py:218
  37.9 7.9 %collective-permute-start.3 = (bf16[272,128]{1,0:T(8,128)(2,1)S(1)}, bf16[272,128]{1,0:T(8,128)(2,1)S(1)}, u32[]{:S(2)}, u32[]{:S(2)}) collective-permute-start(bf16[272,128]{1,0:T(8,128)(2,1)S(1)} %get-tuple-element.24), channel_id=1, source_target_pairs={{0,128},{32,160},{64,192},{96,224},{128,0},{160,32},{192,64},{224,... | collective-permute-start | bytes 208904 | tf_op jit(solution)/shard_map/ppermute | solution.py:218
  38.0 18.5 %all-to-all-start.1 = ((bf16[32,16,128]{2,1,0:T(8,128)(2,1)}), bf16[32,16,128]{2,1,0:T(8,128)(2,1)S(1)}, u32[]{:S(2)}, u32[]{:S(2)}) async-start(bf16[32,16,128]{2,1,0:T(8,128)(2,1)} %get-tuple-element.22), calls=%async_computation.1 | async-start | bytes 262144 | tf_op jit(solution)/shard_map/all_to_all | solution.py:305
  45.8 2.8 %collective-permute-start.6 = (bf16[16,128]{1,0:T(8,128)(2,1)S(1)}, bf16[16,128]{1,0:T(8,128)(2,1)S(1)}, u32[]{:S(2)}, u32[]{:S(2)}) collective-permute-start(bf16[16,128]{1,0:T(8,128)(2,1)S(1)} %fusion.1), channel_id=1, source_target_pairs={{0,64},{32,96},{64,0},{96,32},{128,192},{160,224},{192,128},{224,1... | collective-permute-start | bytes 12296 | tf_op jit(solution)/shard_map/ppermute | solution.py:218
  47.1 3.1 %collective-permute-start.4 = (bf16[128,128]{1,0:T(8,128)(2,1)S(1)}, bf16[128,128]{1,0:T(8,128)(2,1)S(1)}, u32[]{:S(2)}, u32[]{:S(2)}) collective-permute-start(bf16[128,128]{1,0:T(8,128)(2,1)S(1)} %slice.43), channel_id=1, source_target_pairs={{0,64},{32,96},{64,0},{96,32},{128,192},{160,224},{192,128},{224,1... | collective-permute-start | bytes 98312 | tf_op jit(solution)/shard_map/ppermute | solution.py:218
  48.7 2.8 %collective-permute-start.7 = (bf16[16,128]{1,0:T(8,128)(2,1)S(1)}, bf16[16,128]{1,0:T(8,128)(2,1)S(1)}, u32[]{:S(2)}, u32[]{:S(2)}) collective-permute-start(bf16[16,128]{1,0:T(8,128)(2,1)S(1)} %add_convert_fusion.3), channel_id=1, source_target_pairs={{0,32},{32,0},{64,96},{96,64},{128,160},{160,128},{192,224},{224,1... | collective-permute-start | bytes 12296 | tf_op jit(solution)/shard_map/ppermute | solution.py:218
  50.3 3.0 %collective-permute-start.5 = (bf16[64,128]{1,0:T(8,128)(2,1)S(1)}, bf16[64,128]{1,0:T(8,128)(2,1)S(1)}, u32[]{:S(2)}, u32[]{:S(2)}) collective-permute-start(bf16[64,128]{1,0:T(8,128)(2,1)S(1)} %slice.45), channel_id=1, source_target_pairs={{0,32},{32,0},{64,96},{96,64},{128,160},{160,128},{192,224},{224,1... | collective-permute-start | bytes 49160 | tf_op jit(solution)/shard_map/ppermute | solution.py:218
  57.3 11.4 %collective-permute-start.8 = (bf16[64,128]{1,0:T(8,128)(2,1)S(1)}, bf16[64,128]{1,0:T(8,128)(2,1)S(1)}, u32[]{:S(2)}, u32[]{:S(2)}) collective-permute-start(bf16[64,128]{1,0:T(8,128)(2,1)S(1)} %get-tuple-element.26.refs_0_), channel_id=1, source_target_pairs={{0,128},{32,160},{64,192},{96,224},{128,0},{160,32},{192,64},{224,... | collective-permute-start | bytes 49160 | tf_op jit(solution)/shard_map/ppermute | solution.py:218
  60.1 21.6 %all-to-all-start.2 = ((bf16[32,32,128]{2,1,0:T(8,128)(2,1)}), bf16[32,32,128]{2,1,0:T(8,128)(2,1)S(1)}, u32[]{:S(2)}, u32[]{:S(2)}) async-start(bf16[32,32,128]{2,1,0:T(8,128)(2,1)} %get-tuple-element.25), calls=%async_computation.2 | async-start | bytes 524288 | tf_op jit(solution)/shard_map/all_to_all | solution.py:309
  68.7 3.1 %collective-permute-start.9 = (bf16[128,128]{1,0:T(8,128)(2,1)S(1)}, bf16[128,128]{1,0:T(8,128)(2,1)S(1)}, u32[]{:S(2)}, u32[]{:S(2)}) collective-permute-start(bf16[128,128]{1,0:T(8,128)(2,1)S(1)} %pad_maximum_fusion.4), channel_id=1, source_target_pairs={{0,64},{32,96},{64,0},{96,32},{128,192},{160,224},{192,128},{224,1... | collective-permute-start | bytes 98312 | tf_op jit(solution)/shard_map/ppermute | solution.py:218
  71.8 4.1 %collective-permute-start.10 = (bf16[256,128]{1,0:T(8,128)(2,1)S(1)}, bf16[256,128]{1,0:T(8,128)(2,1)S(1)}, u32[]{:S(2)}, u32[]{:S(2)}) collective-permute-start(bf16[256,128]{1,0:T(8,128)(2,1)S(1)} %shard_map.70), channel_id=1, source_target_pairs={{0,32},{32,0},{64,96},{96,64},{128,160},{160,128},{192,224},{224,1... | collective-permute-start | bytes 196616 | tf_op jit(solution)/shard_map/ppermute | solution.py:218
  90.2 1.4 %collective-permute-start.11 = (bf16[17,16,128]{2,1,0:T(8,128)(2,1)S(1)}, bf16[17,16,128]{2,1,0:T(8,128)(2,1)S(1)}, u32[]{:S(2)}, u32[]{:S(2)}) collective-permute-start(bf16[17,16,128]{2,1,0:T(8,128)(2,1)S(1)} %get-tuple-element.29), channel_id=1, source_target_pairs={{0,1},{1,0},{2,3},{3,2},{4,5},{5,4},{6,7},{7,6},{8,9},{9,8},{10,11... | collective-permute-start | bytes 208904 | tf_op jit(solution)/shard_map/ppermute | solution.py:222

commit v7 on v6

--- a/solution.py
+++ b/solution.py
@@ -114,10 +114,8 @@
 
 def parts_of(b_refs, wide):
     def b_of(x):
-        steps = len(b_refs) - 1
-        p = sum((x >> k & 1) << (steps - 1 - k) for k in range(steps))
-        step = p.bit_length()
-        start = (p - (1 << step >> 1)) * wide
+        step = x.bit_length()
+        start = (x - (1 << step >> 1)) * wide
         return b_refs[step][start : start + wide]
 
     return b_of
@@ -253,12 +251,13 @@
 
 
 def gather_rows(piece, weight=0):
+    n = lax.axis_size("rows")
     held = [piece]
-    bit = lax.axis_size("rows") // 2
-    while bit:
-        whole = join(held, weight) if weight and bit == 1 else jnp.concatenate(held)
+    bit = 1
+    while bit < n:
+        whole = join(held, weight) if weight and 2 * bit == n else jnp.concatenate(held)
         held.append(swap(whole, bit))
-        bit //= 2
+        bit *= 2
     return held
 
 

time: 116 us -> 117 us (level)
  waiting for transfers between devices: 31.6 us -> 26.1 us
  starting transfers between devices: 39.2 us -> 44.2 us
  blocking collectives: 22.7 us -> 24.7 us
    ppermute x11, waiting for transfers between devices: 17.3 us -> 13.3 us  [swap(): return lax.ppermute(piece, 'rows', [(i, i ^ bit) for i in range(n)])]
    ppermute x11, starting transfers between devices: 10.3 us -> 14.2 us  [swap(): return lax.ppermute(piece, 'rows', [(i, i ^ bit) for i in range(n)])]
    all_to_all x2, waiting for transfers between devices: 10.1 us -> 7.88 us  [local(): got = lax.all_to_all(copies, 'cols', 0, 0)]
    all_to_all x1, blocking collectives: 14.4 us -> 16.4 us  [exchange_chips(): return lax.all_to_all(pieces, 'cols', 0, 0, axis_index_groups=groups)]
    all_to_all x1, starting transfers between devices: 7.75 us -> 9.1 us  [local(): got = lax.all_to_all(pieces_a, 'cols', 0, 0)]
where the time goes in v7:
time: 117 us
  starting transfers between devices  44.2 us (38%)
  waiting for transfers between devices  26.1 us (22%)
  blocking collectives  24.7 us (21%)
  Pallas kernels  20.5 us (18%)
    all_to_all x2, starting transfers between devices, local(): got = lax.all_to_all(copies, 'cols', 0, 0)  20.4 us
    pallas_call x2, Pallas kernels, call(): pl.pallas_call(body, in_specs=[pl.BlockSpec(memory_space=pltpu.HBM)] + [W...  17.6 us
    all_to_all x1, blocking collectives, exchange_chips(): return lax.all_to_all(pieces, 'cols', 0, 0, axis_index_groups=groups)  16.4 us
    ppermute x11, starting transfers between devices, swap(): return lax.ppermute(piece, 'rows', [(i, i ^ bit) for i in range(n)])  14.2 us
    ppermute x11, waiting for transfers between devices, swap(): return lax.ppermute(piece, 'rows', [(i, i ^ bit) for i in range(n)])  13.3 us
    all_to_all x1, starting transfers between devices, local(): got = lax.all_to_all(pieces_a, 'cols', 0, 0)  9.1 us
    all_to_all x1, blocking collectives, local(): part_b = total(lax.all_to_all(pieces_b, 'rows', 0, 0))  8.3 us
    all_to_all x2, waiting for transfers between devices, local(): got = lax.all_to_all(copies, 'cols', 0, 0)  7.88 us
  transfers between devices with their start and end apart: 15, of which 12 were waited for; matrix products, arithmetic and copies ran while one was open for 0% of the time, Pallas kernels for 0%

profile of v7, /device:TPU:1, one launch (start us, length us, event | category | flops | bytes accessed | tf_op | source)
XLA Modules:
  0.0 116.6 jit_solution(7568487152894792731)
XLA Ops:
  0.6 0.0 copy-start
  0.6 0.0 copy-start.1
  0.7 1.5 %shard_map.67 = (bf16[32,16,128]{2,1,0:T(8,128)(2,1)}, bf16[64,128]{1,0:T(8,128)(2,1)S(1)}, f32[16,128]{1,0:T(8,128)S(1)}) custom-call(f32[16,128]{1,0:T(8,128)} %a_ref.3, f32[64,128]{1,0:T(8,128)} %b_ref.3, f32[16,128]{1,0:T(8,128)} %c_ref.1), custom_call_target="tpu_custom_call" | custom-call | tf_op jit(solution)/shard_map/pallas_call | solution.py:33
  2.2 2.1 %collective-permute-start = (bf16[64,128]{1,0:T(8,128)(2,1)S(1)}, bf16[64,128]{1,0:T(8,128)(2,1)S(1)}, u32[]{:S(2)}, u32[]{:S(2)}) collective-permute-start(bf16[64,128]{1,0:T(8,128)(2,1)S(1)} %get-tuple-element.20.refs_0_), channel_id=1, source_target_pairs={{0,32},{32,0},{64,96},{96,64},{128,160},{160,128},{192,224},{224,1... | collective-permute-start | bytes 49160 | tf_op jit(solution)/shard_map/ppermute | solution.py:216
  4.3 11.7 %all-to-all-start = ((bf16[32,16,128]{2,1,0:T(8,128)(2,1)}), bf16[32,16,128]{2,1,0:T(8,128)(2,1)S(1)}, u32[]{:S(2)}, u32[]{:S(2)}) async-start(bf16[32,16,128]{2,1,0:T(8,128)(2,1)} %get-tuple-element.19), calls=%async_computation | async-start | bytes 262144 | tf_op jit(solution)/shard_map/all_to_all | solution.py:296
  16.0 0.0 collective-permute-done.refs_1_
  16.1 1.4 %collective-permute-start.1 = (bf16[128,128]{1,0:T(8,128)(2,1)S(1)}, bf16[128,128]{1,0:T(8,128)(2,1)S(1)}, u32[]{:S(2)}, u32[]{:S(2)}) collective-permute-start(bf16[128,128]{1,0:T(8,128)(2,1)S(1)} %pad_maximum_fusion.3), channel_id=1, source_target_pairs={{0,64},{32,96},{64,0},{96,32},{128,192},{160,224},{192,128},{224,1... | collective-permute-start | bytes 98312 | tf_op jit(solution)/shard_map/ppermute | solution.py:216
  17.4 1.5 %collective-permute-done.1.refs_2_ = bf16[128,128]{1,0:T(8,128)(2,1)S(1)} collective-permute-done((bf16[128,128]{1,0:T(8,128)(2,1)S(1)}, bf16[128,128]{1,0:T(8,128)(2,1)S(1)}, u32[]{:S(2)}, u32[]{:S(2)}) %collective-permute-start.1) | collective-permute-done | bytes 32800 | tf_op jit(solution)/shard_map/ppermute | solution.py:216
  18.9 2.9 %collective-permute-start.2 = (bf16[256,128]{1,0:T(8,128)(2,1)S(1)}, bf16[256,128]{1,0:T(8,128)(2,1)S(1)}, u32[]{:S(2)}, u32[]{:S(2)}) collective-permute-start(bf16[256,128]{1,0:T(8,128)(2,1)S(1)} %pad_maximum_fusion.2), channel_id=1, source_target_pairs={{0,128},{32,160},{64,192},{96,224},{128,0},{160,32},{192,64},{224,... | collective-permute-start | bytes 196616 | tf_op jit(solution)/shard_map/ppermute | solution.py:216
  21.9 2.0 %collective-permute-done.2.refs_3_ = bf16[256,128]{1,0:T(8,128)(2,1)S(1)} collective-permute-done((bf16[256,128]{1,0:T(8,128)(2,1)S(1)}, bf16[256,128]{1,0:T(8,128)(2,1)S(1)}, u32[]{:S(2)}, u32[]{:S(2)}) %collective-permute-start.2) | collective-permute-done | bytes 65568 | tf_op jit(solution)/shard_map/ppermute | solution.py:216
  23.9 2.9 %all-to-all-done.a_ref = bf16[32,16,128]{2,1,0:T(8,128)(2,1)S(1)} async-done(((bf16[32,16,128]{2,1,0:T(8,128)(2,1)}), bf16[32,16,128]{2,1,0:T(8,128)(2,1)S(1)}, u32[]{:S(2)}, u32[]{:S(2)}) %all-to-all-start) | async-done | bytes 131104 | tf_op jit(solution)/shard_map/all_to_all | solution.py:296
  26.8 9.1 %shard_map.68 = (bf16[32,16,128]{2,1,0:T(8,128)(2,1)}, bf16[256,128]{1,0:T(8,128)(2,1)S(1)}, bf16[272,128]{1,0:T(8,128)(2,1)S(1)}) custom-call(bf16[512,8192]{1,0:T(8,128)(2,1)} %n_ref.3, bf16[32,16,128]{2,1,0:T(8,128)(2,1)S(1)} %all-to-all-done.a_ref, bf16[64,128]{1,0:T(8,128)(2,1)S(1)} %get-tuple-element.20.refs_0_, ...), custom_call_target="tpu_custom_call" | custom-call | flops 3221225472 | bytes 8388608 | tf_op jit(solution)/shard_map/pallas_call | solution.py:195
  35.9 3.0 %collective-permute-start.3 = (bf16[272,128]{1,0:T(8,128)(2,1)S(1)}, bf16[272,128]{1,0:T(8,128)(2,1)S(1)}, u32[]{:S(2)}, u32[]{:S(2)}) collective-permute-start(bf16[272,128]{1,0:T(8,128)(2,1)S(1)} %get-tuple-element.24), channel_id=1, source_target_pairs={{0,128},{32,160},{64,192},{96,224},{128,0},{160,32},{192,64},{224,... | collective-permute-start | bytes 208904 | tf_op jit(solution)/shard_map/ppermute | solution.py:216
  38.9 9.1 %all-to-all-start.1 = ((bf16[32,16,128]{2,1,0:T(8,128)(2,1)}), bf16[32,16,128]{2,1,0:T(8,128)(2,1)S(1)}, u32[]{:S(2)}, u32[]{:S(2)}) async-start(bf16[32,16,128]{2,1,0:T(8,128)(2,1)} %get-tuple-element.22), calls=%async_computation.1 | async-start | bytes 262144 | tf_op jit(solution)/shard_map/all_to_all | solution.py:304
  48.0 0.0 collective-permute-done.3
  48.0 0.5 collective-permute-start.6
  48.6 1.2 collective-permute-start.4
  49.7 1.2 collective-permute-done.6
  50.9 0.0 collective-permute-start.7
  50.9 0.9 collective-permute-done.4
  51.8 0.7 collective-permute-start.5
  52.5 1.2 %collective-permute-done.7 = bf16[16,128]{1,0:T(8,128)(2,1)S(1)} collective-permute-done((bf16[16,128]{1,0:T(8,128)(2,1)S(1)}, bf16[16,128]{1,0:T(8,128)(2,1)S(1)}, u32[]{:S(2)}, u32[]{:S(2)}) %collective-permute-start.7) | collective-permute-done | bytes 4128 | tf_op jit(solution)/shard_map/ppermute | solution.py:216
  53.7 1.1 collective-permute-done.5
  54.8 4.0 %all-to-all-done.1.got_ref = bf16[32,16,128]{2,1,0:T(8,128)(2,1)S(1)} async-done(((bf16[32,16,128]{2,1,0:T(8,128)(2,1)}), bf16[32,16,128]{2,1,0:T(8,128)(2,1)S(1)}, u32[]{:S(2)}, u32[]{:S(2)}) %all-to-all-start.1) | async-done | bytes 131104 | tf_op jit(solution)/shard_map/all_to_all | solution.py:304
  58.8 0.0 copy-done
  58.8 0.0 copy-done.1
  58.8 0.8 shard_map.69
  59.5 0.0 collective-permute-start.8
  59.5 8.7 %all-to-all-start.2 = ((bf16[32,32,128]{2,1,0:T(8,128)(2,1)}), bf16[32,32,128]{2,1,0:T(8,128)(2,1)S(1)}, u32[]{:S(2)}, u32[]{:S(2)}) async-start(bf16[32,32,128]{2,1,0:T(8,128)(2,1)} %get-tuple-element.25), calls=%async_computation.2 | async-start | bytes 524288 | tf_op jit(solution)/shard_map/all_to_all | solution.py:308
  68.3 0.0 collective-permute-done.8.refs_1_
  68.3 1.0 collective-permute-start.9
  69.3 2.0 %collective-permute-done.9.refs_2_ = bf16[128,128]{1,0:T(8,128)(2,1)S(1)} collective-permute-done((bf16[128,128]{1,0:T(8,128)(2,1)S(1)}, bf16[128,128]{1,0:T(8,128)(2,1)S(1)}, u32[]{:S(2)}, u32[]{:S(2)}) %collective-permute-start.9) | collective-permute-done | bytes 32800 | tf_op jit(solution)/shard_map/ppermute | solution.py:216
  71.3 1.4 %collective-permute-start.10 = (bf16[256,128]{1,0:T(8,128)(2,1)S(1)}, bf16[256,128]{1,0:T(8,128)(2,1)S(1)}, u32[]{:S(2)}, u32[]{:S(2)}) collective-permute-start(bf16[256,128]{1,0:T(8,128)(2,1)S(1)} %shard_map.70), channel_id=1, source_target_pairs={{0,128},{32,160},{64,192},{96,224},{128,0},{160,32},{192,64},{224,... | collective-permute-start | bytes 196616 | tf_op jit(solution)/shard_map/ppermute | solution.py:216
  72.8 3.5 %collective-permute-done.10.refs_3_ = bf16[256,128]{1,0:T(8,128)(2,1)S(1)} collective-permute-done((bf16[256,128]{1,0:T(8,128)(2,1)S(1)}, bf16[256,128]{1,0:T(8,128)(2,1)S(1)}, u32[]{:S(2)}, u32[]{:S(2)}) %collective-permute-start.10) | collective-permute-done | bytes 65568 | tf_op jit(solution)/shard_map/ppermute | solution.py:216
  76.2 4.9 %all-to-all-done.2.got_ref = bf16[32,32,128]{2,1,0:T(8,128)(2,1)S(1)} async-done(((bf16[32,32,128]{2,1,0:T(8,128)(2,1)}), bf16[32,32,128]{2,1,0:T(8,128)(2,1)S(1)}, u32[]{:S(2)}, u32[]{:S(2)}) %all-to-all-start.2) | async-done | bytes 262176 | tf_op jit(solution)/shard_map/all_to_all | solution.py:308
  81.2 8.5 %shard_map.71 = (bf16[17,16,128]{2,1,0:T(8,128)(2,1)S(1)}, bf16[17,16,128]{2,1,0:T(8,128)(2,1)S(1)}, bf16[8,64,128]{2,1,0:T(8,128)(2,1)S(1)}, f32[16,128]{1,0:T(8,128)S(1)}) custom-call(bf16[512,8192]{1,0:T(8,128)(2,1)} %n_ref.3, bf16[32,32,128]{2,1,0:T(8,128)(2,1)S(1)} %all-to-all-done.2.got_ref, bf16[64,128]{1,0:T(8,128)(2,1)S(1)} %get-tuple-element.26.refs_0_, ...), custom_call_target="tpu_custom_call" | custom-call | flops 3221225472 | bytes 8388608 | tf_op jit(solution)/shard_map/pallas_call | solution.py:195
  89.7 0.5 collective-permute-start.11
  90.2 0.9 collective-permute-done.11
  91.2 8.3 %all_to_all.25 = bf16[8,80,128]{2,1,0:T(8,128)(2,1)S(1)} all-to-all(bf16[8,80,128]{2,1,0:T(8,128)(2,1)S(1)} %pad_maximum_fusion), channel_id=1, replica_groups=mesh['rows'=8,'cols'=32] {'rows'}, dimensions={0} | all-to-all | bytes 327680 | tf_op jit(solution)/shard_map/all_to_all | solution.py:319
  99.6 16.4 %all_to_all.26.got_ref = bf16[16,32,128]{2,1,0:T(8,128)(2,1)S(1)} all-to-all(bf16[16,32,128]{2,1,0:T(8,128)(2,1)S(1)} %pad_maximum_fusion.1), channel_id=1, replica_groups={{0,2,4,6,8,10,12,14,16,18,20,22,24,26,28,30},{1,3,5,7,9,11,13,15,17,19,..., dimensions={0} | all-to-all | bytes 262144 | tf_op jit(solution)/shard_map/all_to_all | solution.py:226
  115.9 0.6 shard_map.72
  (22 shorter events, 0.2 us)
Async XLA Ops:
  0.6 58.1 %copy-start = (f32[64,128]{1,0:T(8,128)S(1)}, f32[64,128]{1,0:T(8,128)}, u32[]{:S(2)}) copy-start(f32[64,128]{1,0:T(8,128)} %b_ref.3) | copy-start | bytes 98308
  0.6 58.1 %copy-start.1 = (f32[16,128]{1,0:T(8,128)S(1)}, f32[16,128]{1,0:T(8,128)}, u32[]{:S(2)}) copy-start(f32[16,128]{1,0:T(8,128)} %a_ref.3) | copy-start | bytes 24580
  2.2 13.9 %collective-permute-start = (bf16[64,128]{1,0:T(8,128)(2,1)S(1)}, bf16[64,128]{1,0:T(8,128)(2,1)S(1)}, u32[]{:S(2)}, u32[]{:S(2)}) collective-permute-start(bf16[64,128]{1,0:T(8,128)(2,1)S(1)} %get-tuple-element.20.refs_0_), channel_id=1, source_target_pairs={{0,32},{32,0},{64,96},{96,64},{128,160},{160,128},{192,224},{224,1... | collective-permute-start | bytes 49160 | tf_op jit(solution)/shard_map/ppermute | solution.py:216
  4.3 22.5 %all-to-all-start = ((bf16[32,16,128]{2,1,0:T(8,128)(2,1)}), bf16[32,16,128]{2,1,0:T(8,128)(2,1)S(1)}, u32[]{:S(2)}, u32[]{:S(2)}) async-start(bf16[32,16,128]{2,1,0:T(8,128)(2,1)} %get-tuple-element.19), calls=%async_computation | async-start | bytes 262144 | tf_op jit(solution)/shard_map/all_to_all | solution.py:296
  16.1 2.9 %collective-permute-start.1 = (bf16[128,128]{1,0:T(8,128)(2,1)S(1)}, bf16[128,128]{1,0:T(8,128)(2,1)S(1)}, u32[]{:S(2)}, u32[]{:S(2)}) collective-permute-start(bf16[128,128]{1,0:T(8,128)(2,1)S(1)} %pad_maximum_fusion.3), channel_id=1, source_target_pairs={{0,64},{32,96},{64,0},{96,32},{128,192},{160,224},{192,128},{224,1... | collective-permute-start | bytes 98312 | tf_op jit(solution)/shard_map/ppermute | solution.py:216
  18.9 4.9 %collective-permute-start.2 = (bf16[256,128]{1,0:T(8,128)(2,1)S(1)}, bf16[256,128]{1,0:T(8,128)(2,1)S(1)}, u32[]{:S(2)}, u32[]{:S(2)}) collective-permute-start(bf16[256,128]{1,0:T(8,128)(2,1)S(1)} %pad_maximum_fusion.2), channel_id=1, source_target_pairs={{0,128},{32,160},{64,192},{96,224},{128,0},{160,32},{192,64},{224,... | collective-permute-start | bytes 196616 | tf_op jit(solution)/shard_map/ppermute | solution.py:216
  35.9 12.1 %collective-permute-start.3 = (bf16[272,128]{1,0:T(8,128)(2,1)S(1)}, bf16[272,128]{1,0:T(8,128)(2,1)S(1)}, u32[]{:S(2)}, u32[]{:S(2)}) collective-permute-start(bf16[272,128]{1,0:T(8,128)(2,1)S(1)} %get-tuple-element.24), channel_id=1, source_target_pairs={{0,128},{32,160},{64,192},{96,224},{128,0},{160,32},{192,64},{224,... | collective-permute-start | bytes 208904 | tf_op jit(solution)/shard_map/ppermute | solution.py:216
  38.9 19.9 %all-to-all-start.1 = ((bf16[32,16,128]{2,1,0:T(8,128)(2,1)}), bf16[32,16,128]{2,1,0:T(8,128)(2,1)S(1)}, u32[]{:S(2)}, u32[]{:S(2)}) async-start(bf16[32,16,128]{2,1,0:T(8,128)(2,1)} %get-tuple-element.22), calls=%async_computation.1 | async-start | bytes 262144 | tf_op jit(solution)/shard_map/all_to_all | solution.py:304
  48.0 2.8 %collective-permute-start.6 = (bf16[16,128]{1,0:T(8,128)(2,1)S(1)}, bf16[16,128]{1,0:T(8,128)(2,1)S(1)}, u32[]{:S(2)}, u32[]{:S(2)}) collective-permute-start(bf16[16,128]{1,0:T(8,128)(2,1)S(1)} %fusion.1), channel_id=1, source_target_pairs={{0,64},{32,96},{64,0},{96,32},{128,192},{160,224},{192,128},{224,1... | collective-permute-start | bytes 12296 | tf_op jit(solution)/shard_map/ppermute | solution.py:216
  48.6 3.2 %collective-permute-start.4 = (bf16[128,128]{1,0:T(8,128)(2,1)S(1)}, bf16[128,128]{1,0:T(8,128)(2,1)S(1)}, u32[]{:S(2)}, u32[]{:S(2)}) collective-permute-start(bf16[128,128]{1,0:T(8,128)(2,1)S(1)} %slice.43), channel_id=1, source_target_pairs={{0,64},{32,96},{64,0},{96,32},{128,192},{160,224},{192,128},{224,1... | collective-permute-start | bytes 98312 | tf_op jit(solution)/shard_map/ppermute | solution.py:216
  50.9 2.8 %collective-permute-start.7 = (bf16[16,128]{1,0:T(8,128)(2,1)S(1)}, bf16[16,128]{1,0:T(8,128)(2,1)S(1)}, u32[]{:S(2)}, u32[]{:S(2)}) collective-permute-start(bf16[16,128]{1,0:T(8,128)(2,1)S(1)} %add_convert_fusion.3), channel_id=1, source_target_pairs={{0,32},{32,0},{64,96},{96,64},{128,160},{160,128},{192,224},{224,1... | collective-permute-start | bytes 12296 | tf_op jit(solution)/shard_map/ppermute | solution.py:216
  51.8 3.0 %collective-permute-start.5 = (bf16[64,128]{1,0:T(8,128)(2,1)S(1)}, bf16[64,128]{1,0:T(8,128)(2,1)S(1)}, u32[]{:S(2)}, u32[]{:S(2)}) collective-permute-start(bf16[64,128]{1,0:T(8,128)(2,1)S(1)} %slice.45), channel_id=1, source_target_pairs={{0,32},{32,0},{64,96},{96,64},{128,160},{160,128},{192,224},{224,1... | collective-permute-start | bytes 49160 | tf_op jit(solution)/shard_map/ppermute | solution.py:216
  59.5 8.7 %collective-permute-start.8 = (bf16[64,128]{1,0:T(8,128)(2,1)S(1)}, bf16[64,128]{1,0:T(8,128)(2,1)S(1)}, u32[]{:S(2)}, u32[]{:S(2)}) collective-permute-start(bf16[64,128]{1,0:T(8,128)(2,1)S(1)} %get-tuple-element.26.refs_0_), channel_id=1, source_target_pairs={{0,32},{32,0},{64,96},{96,64},{128,160},{160,128},{192,224},{224,1... | collective-permute-start | bytes 49160 | tf_op jit(solution)/shard_map/ppermute | solution.py:216
  59.5 21.7 %all-to-all-start.2 = ((bf16[32,32,128]{2,1,0:T(8,128)(2,1)}), bf16[32,32,128]{2,1,0:T(8,128)(2,1)S(1)}, u32[]{:S(2)}, u32[]{:S(2)}) async-start(bf16[32,32,128]{2,1,0:T(8,128)(2,1)} %get-tuple-element.25), calls=%async_computation.2 | async-start | bytes 524288 | tf_op jit(solution)/shard_map/all_to_all | solution.py:308
  68.3 3.1 %collective-permute-start.9 = (bf16[128,128]{1,0:T(8,128)(2,1)S(1)}, bf16[128,128]{1,0:T(8,128)(2,1)S(1)}, u32[]{:S(2)}, u32[]{:S(2)}) collective-permute-start(bf16[128,128]{1,0:T(8,128)(2,1)S(1)} %pad_maximum_fusion.4), channel_id=1, source_target_pairs={{0,64},{32,96},{64,0},{96,32},{128,192},{160,224},{192,128},{224,1... | collective-permute-start | bytes 98312 | tf_op jit(solution)/shard_map/ppermute | solution.py:216
  71.3 4.9 %collective-permute-start.10 = (bf16[256,128]{1,0:T(8,128)(2,1)S(1)}, bf16[256,128]{1,0:T(8,128)(2,1)S(1)}, u32[]{:S(2)}, u32[]{:S(2)}) collective-permute-start(bf16[256,128]{1,0:T(8,128)(2,1)S(1)} %shard_map.70), channel_id=1, source_target_pairs={{0,128},{32,160},{64,192},{96,224},{128,0},{160,32},{192,64},{224,... | collective-permute-start | bytes 196616 | tf_op jit(solution)/shard_map/ppermute | solution.py:216
  89.7 1.4 %collective-permute-start.11 = (bf16[17,16,128]{2,1,0:T(8,128)(2,1)S(1)}, bf16[17,16,128]{2,1,0:T(8,128)(2,1)S(1)}, u32[]{:S(2)}, u32[]{:S(2)}) collective-permute-start(bf16[17,16,128]{2,1,0:T(8,128)(2,1)S(1)} %get-tuple-element.29), channel_id=1, source_target_pairs={{0,1},{1,0},{2,3},{3,2},{4,5},{5,4},{6,7},{7,6},{8,9},{9,8},{10,11... | collective-permute-start | bytes 208904 | tf_op jit(solution)/shard_map/ppermute | solution.py:220

commit v8 on v6

--- a/solution.py
+++ b/solution.py
@@ -112,10 +112,10 @@
     return grad_c
 
 
-def parts_of(b_refs, wide):
+def parts_of(b_refs, wide, near):
     def b_of(x):
         steps = len(b_refs) - 1
-        p = sum((x >> k & 1) << (steps - 1 - k) for k in range(steps))
+        p = x if near else sum((x >> k & 1) << (steps - 1 - k) for k in range(steps))
         step = p.bit_length()
         start = (p - (1 << step >> 1)) * wide
         return b_refs[step][start : start + wide]
@@ -135,7 +135,7 @@
 
     low_a = a_ref[...].reshape(acc_ref.shape)
     acc_ref[...] = jnp.zeros_like(acc_ref)
-    b_of = parts_of(b_refs, wide)
+    b_of = parts_of(b_refs, wide, False)
     grad_c = jnp.zeros(c_ref.shape, F32)
     grad_c = visit_blocks(
         n_ref, held_ref, sems, low_a, b_of, c_ref[...], put_b, acc_ref, grad_c
@@ -160,7 +160,7 @@
     low_a = got_ref[:, :rows].reshape(acc_ref.shape)
     c = c_ref[...] - rate_c * total(got_ref[:, rows:])
     new_c_ref[...] = c
-    b_of = parts_of(b_refs, wide)
+    b_of = parts_of(b_refs, wide, True)
     grad_c = jnp.zeros(c.shape, F32)
     grad_c = visit_blocks(
         n_ref, held_ref, sems, low_a, b_of, c, put_b, acc_ref, grad_c
@@ -252,13 +252,12 @@
     )(*pieces)
 
 
-def gather_rows(piece, weight=0):
+def gather_rows(piece, near=False):
+    steps = lax.axis_size("rows").bit_length() - 1
     held = [piece]
-    bit = lax.axis_size("rows") // 2
-    while bit:
-        whole = join(held, weight) if weight and bit == 1 else jnp.concatenate(held)
-        held.append(swap(whole, bit))
-        bit //= 2
+    for k in range(steps):
+        whole = join(held, JOIN_WEIGHT) if near and k == steps - 1 else jnp.concatenate(held)
+        held.append(swap(whole, 1 << (k if near else steps - 1 - k)))
     return held
 
 
@@ -307,7 +306,7 @@
             got, local_a, part_b, local_b, low_c, rate_a, rate_b
         )
     got = lax.all_to_all(copies, "cols", 0, 0)
-    b_parts = gather_rows(low_b, JOIN_WEIGHT)
+    b_parts = gather_rows(low_b, True)
     shape_half = (n_cols // 2 + 1, rows_a, rank)
     own, other, pieces_b, c = call(
         functools.partial(last_body, rate_c), counts, [got, *b_parts, c],

time: 116 us -> 117 us (level)
  blocking collectives: 22.7 us -> 25.5 us
  waiting for transfers between devices: 31.6 us -> 29 us
    ppermute x11, waiting for transfers between devices: 17.3 us -> 15.6 us  [swap(): return lax.ppermute(piece, 'rows', [(i, i ^ bit) for i in range(n)])]
    all_to_all x1, blocking collectives: 14.4 us -> 16 us  [exchange_chips(): return lax.all_to_all(pieces, 'cols', 0, 0, axis_index_groups=groups)]
    all_to_all x1, blocking collectives: 8.28 us -> 9.48 us  [local(): part_b = total(lax.all_to_all(pieces_b, 'rows', 0, 0))]
where the time goes in v8:
time: 117 us; the launch traced here: 116 us
  starting transfers between devices  40.1 us (34%)
  waiting for transfers between devices  29 us (25%)
  blocking collectives  25.5 us (22%)
  Pallas kernels  20.5 us (18%)
    all_to_all x2, starting transfers between devices, local(): got = lax.all_to_all(copies, 'cols', 0, 0)  21.4 us
    pallas_call x2, Pallas kernels, call(): pl.pallas_call(body, in_specs=[pl.BlockSpec(memory_space=pltpu.HBM)] + [W...  17.6 us
    all_to_all x1, blocking collectives, exchange_chips(): return lax.all_to_all(pieces, 'cols', 0, 0, axis_index_groups=groups)  16 us
    ppermute x11, waiting for transfers between devices, swap(): return lax.ppermute(piece, 'rows', [(i, i ^ bit) for i in range(n)])  15.6 us
    ppermute x11, starting transfers between devices, swap(): return lax.ppermute(piece, 'rows', [(i, i ^ bit) for i in range(n)])  10.5 us
    all_to_all x1, blocking collectives, local(): part_b = total(lax.all_to_all(pieces_b, 'rows', 0, 0))  9.48 us
    all_to_all x2, waiting for transfers between devices, local(): got = lax.all_to_all(copies, 'cols', 0, 0)  9.21 us
    all_to_all x1, starting transfers between devices, local(): got = lax.all_to_all(pieces_a, 'cols', 0, 0)  7.75 us
  transfers between devices with their start and end apart: 15, of which 12 were waited for; matrix products, arithmetic and copies ran while one was open for 0% of the time, Pallas kernels for 0%

profile of v8, /device:TPU:1, one launch (start us, length us, event | category | flops | bytes accessed | tf_op | source)
XLA Modules:
  0.0 116.2 jit_solution(4623228345949867860)
XLA Ops:
  0.6 0.0 copy-start
  0.6 0.0 copy-start.1
  0.7 1.5 %shard_map.67 = (bf16[32,16,128]{2,1,0:T(8,128)(2,1)}, bf16[64,128]{1,0:T(8,128)(2,1)S(1)}, f32[16,128]{1,0:T(8,128)S(1)}) custom-call(f32[16,128]{1,0:T(8,128)} %a_ref.3, f32[64,128]{1,0:T(8,128)} %b_ref.3, f32[16,128]{1,0:T(8,128)} %c_ref.1), custom_call_target="tpu_custom_call" | custom-call | tf_op jit(solution)/shard_map/pallas_call | solution.py:33
  2.2 3.8 %collective-permute-start = (bf16[64,128]{1,0:T(8,128)(2,1)S(1)}, bf16[64,128]{1,0:T(8,128)(2,1)S(1)}, u32[]{:S(2)}, u32[]{:S(2)}) collective-permute-start(bf16[64,128]{1,0:T(8,128)(2,1)S(1)} %get-tuple-element.20.refs_0_), channel_id=1, source_target_pairs={{0,128},{32,160},{64,192},{96,224},{128,0},{160,32},{192,64},{224,... | collective-permute-start | bytes 49160 | tf_op jit(solution)/shard_map/ppermute | solution.py:218
  6.0 12.0 %all-to-all-start = ((bf16[32,16,128]{2,1,0:T(8,128)(2,1)}), bf16[32,16,128]{2,1,0:T(8,128)(2,1)S(1)}, u32[]{:S(2)}, u32[]{:S(2)}) async-start(bf16[32,16,128]{2,1,0:T(8,128)(2,1)} %get-tuple-element.19), calls=%async_computation | async-start | bytes 262144 | tf_op jit(solution)/shard_map/all_to_all | solution.py:296
  18.0 0.0 collective-permute-done.refs_1_
  18.0 0.5 collective-permute-start.1
  18.5 2.4 %collective-permute-done.1.refs_2_ = bf16[128,128]{1,0:T(8,128)(2,1)S(1)} collective-permute-done((bf16[128,128]{1,0:T(8,128)(2,1)S(1)}, bf16[128,128]{1,0:T(8,128)(2,1)S(1)}, u32[]{:S(2)}, u32[]{:S(2)}) %collective-permute-start.1) | collective-permute-done | bytes 32800 | tf_op jit(solution)/shard_map/ppermute | solution.py:218
  20.9 0.3 collective-permute-start.2
  21.2 3.3 %collective-permute-done.2.refs_3_ = bf16[256,128]{1,0:T(8,128)(2,1)S(1)} collective-permute-done((bf16[256,128]{1,0:T(8,128)(2,1)S(1)}, bf16[256,128]{1,0:T(8,128)(2,1)S(1)}, u32[]{:S(2)}, u32[]{:S(2)}) %collective-permute-start.2) | collective-permute-done | bytes 65568 | tf_op jit(solution)/shard_map/ppermute | solution.py:218
  24.5 4.3 %all-to-all-done.a_ref = bf16[32,16,128]{2,1,0:T(8,128)(2,1)S(1)} async-done(((bf16[32,16,128]{2,1,0:T(8,128)(2,1)}), bf16[32,16,128]{2,1,0:T(8,128)(2,1)S(1)}, u32[]{:S(2)}, u32[]{:S(2)}) %all-to-all-start) | async-done | bytes 131104 | tf_op jit(solution)/shard_map/all_to_all | solution.py:296
  28.8 9.1 %shard_map.68 = (bf16[32,16,128]{2,1,0:T(8,128)(2,1)}, bf16[256,128]{1,0:T(8,128)(2,1)S(1)}, bf16[272,128]{1,0:T(8,128)(2,1)S(1)}) custom-call(bf16[512,8192]{1,0:T(8,128)(2,1)} %n_ref.3, bf16[32,16,128]{2,1,0:T(8,128)(2,1)S(1)} %all-to-all-done.a_ref, bf16[64,128]{1,0:T(8,128)(2,1)S(1)} %get-tuple-element.20.refs_0_, ...), custom_call_target="tpu_custom_call" | custom-call | flops 3221225472 | bytes 8388608 | tf_op jit(solution)/shard_map/pallas_call | solution.py:197
  37.9 0.1 collective-permute-start.3
  38.0 7.8 %all-to-all-start.1 = ((bf16[32,16,128]{2,1,0:T(8,128)(2,1)}), bf16[32,16,128]{2,1,0:T(8,128)(2,1)S(1)}, u32[]{:S(2)}, u32[]{:S(2)}) async-start(bf16[32,16,128]{2,1,0:T(8,128)(2,1)} %get-tuple-element.22), calls=%async_computation.1 | async-start | bytes 262144 | tf_op jit(solution)/shard_map/all_to_all | solution.py:304
  45.8 0.0 collective-permute-done.3
  45.8 1.2 %collective-permute-start.6 = (bf16[16,128]{1,0:T(8,128)(2,1)S(1)}, bf16[16,128]{1,0:T(8,128)(2,1)S(1)}, u32[]{:S(2)}, u32[]{:S(2)}) collective-permute-start(bf16[16,128]{1,0:T(8,128)(2,1)S(1)} %fusion.1), channel_id=1, source_target_pairs={{0,64},{32,96},{64,0},{96,32},{128,192},{160,224},{192,128},{224,1... | collective-permute-start | bytes 12296 | tf_op jit(solution)/shard_map/ppermute | solution.py:218
  47.1 0.4 collective-permute-start.4
  47.5 1.2 %collective-permute-done.6 = bf16[16,128]{1,0:T(8,128)(2,1)S(1)} collective-permute-done((bf16[16,128]{1,0:T(8,128)(2,1)S(1)}, bf16[16,128]{1,0:T(8,128)(2,1)S(1)}, u32[]{:S(2)}, u32[]{:S(2)}) %collective-permute-start.6) | collective-permute-done | bytes 4128 | tf_op jit(solution)/shard_map/ppermute | solution.py:218
  48.7 0.3 collective-permute-start.7
  49.0 1.2 %collective-permute-done.4 = bf16[128,128]{1,0:T(8,128)(2,1)S(1)} collective-permute-done((bf16[128,128]{1,0:T(8,128)(2,1)S(1)}, bf16[128,128]{1,0:T(8,128)(2,1)S(1)}, u32[]{:S(2)}, u32[]{:S(2)}) %collective-permute-start.4) | collective-permute-done | bytes 32800 | tf_op jit(solution)/shard_map/ppermute | solution.py:218
  50.3 0.4 collective-permute-start.5
  50.7 0.8 collective-permute-done.7
  51.4 1.8 %collective-permute-done.5 = bf16[64,128]{1,0:T(8,128)(2,1)S(1)} collective-permute-done((bf16[64,128]{1,0:T(8,128)(2,1)S(1)}, bf16[64,128]{1,0:T(8,128)(2,1)S(1)}, u32[]{:S(2)}, u32[]{:S(2)}) %collective-permute-start.5) | collective-permute-done | bytes 16416 | tf_op jit(solution)/shard_map/ppermute | solution.py:218
  53.3 3.3 %all-to-all-done.1.got_ref = bf16[32,16,128]{2,1,0:T(8,128)(2,1)S(1)} async-done(((bf16[32,16,128]{2,1,0:T(8,128)(2,1)}), bf16[32,16,128]{2,1,0:T(8,128)(2,1)S(1)}, u32[]{:S(2)}, u32[]{:S(2)}) %all-to-all-start.1) | async-done | bytes 131104 | tf_op jit(solution)/shard_map/all_to_all | solution.py:304
  56.6 0.0 copy-done
  56.6 0.0 copy-done.1
  56.6 0.8 shard_map.69
  57.3 0.3 collective-permute-start.8
  57.6 9.4 %all-to-all-start.2 = ((bf16[32,32,128]{2,1,0:T(8,128)(2,1)}), bf16[32,32,128]{2,1,0:T(8,128)(2,1)S(1)}, u32[]{:S(2)}, u32[]{:S(2)}) async-start(bf16[32,32,128]{2,1,0:T(8,128)(2,1)} %get-tuple-element.25), calls=%async_computation.2 | async-start | bytes 524288 | tf_op jit(solution)/shard_map/all_to_all | solution.py:308
  67.0 0.0 collective-permute-done.8.refs_1_
  67.0 0.4 collective-permute-start.9
  67.5 2.6 %collective-permute-done.9.refs_2_ = bf16[128,128]{1,0:T(8,128)(2,1)S(1)} collective-permute-done((bf16[128,128]{1,0:T(8,128)(2,1)S(1)}, bf16[128,128]{1,0:T(8,128)(2,1)S(1)}, u32[]{:S(2)}, u32[]{:S(2)}) %collective-permute-start.9) | collective-permute-done | bytes 32800 | tf_op jit(solution)/shard_map/ppermute | solution.py:218
  70.1 2.6 %collective-permute-start.10 = (bf16[256,128]{1,0:T(8,128)(2,1)S(1)}, bf16[256,128]{1,0:T(8,128)(2,1)S(1)}, u32[]{:S(2)}, u32[]{:S(2)}) collective-permute-start(bf16[256,128]{1,0:T(8,128)(2,1)S(1)} %shard_map.70), channel_id=1, source_target_pairs={{0,128},{32,160},{64,192},{96,224},{128,0},{160,32},{192,64},{224,... | collective-permute-start | bytes 196616 | tf_op jit(solution)/shard_map/ppermute | solution.py:218
  72.7 2.3 %collective-permute-done.10.refs_3_ = bf16[256,128]{1,0:T(8,128)(2,1)S(1)} collective-permute-done((bf16[256,128]{1,0:T(8,128)(2,1)S(1)}, bf16[256,128]{1,0:T(8,128)(2,1)S(1)}, u32[]{:S(2)}, u32[]{:S(2)}) %collective-permute-start.10) | collective-permute-done | bytes 65568 | tf_op jit(solution)/shard_map/ppermute | solution.py:218
  75.0 4.9 %all-to-all-done.2.got_ref = bf16[32,32,128]{2,1,0:T(8,128)(2,1)S(1)} async-done(((bf16[32,32,128]{2,1,0:T(8,128)(2,1)}), bf16[32,32,128]{2,1,0:T(8,128)(2,1)S(1)}, u32[]{:S(2)}, u32[]{:S(2)}) %all-to-all-start.2) | async-done | bytes 262176 | tf_op jit(solution)/shard_map/all_to_all | solution.py:308
  79.9 8.5 %shard_map.71 = (bf16[17,16,128]{2,1,0:T(8,128)(2,1)S(1)}, bf16[17,16,128]{2,1,0:T(8,128)(2,1)S(1)}, bf16[8,64,128]{2,1,0:T(8,128)(2,1)S(1)}, f32[16,128]{1,0:T(8,128)S(1)}) custom-call(bf16[512,8192]{1,0:T(8,128)(2,1)} %n_ref.3, bf16[32,32,128]{2,1,0:T(8,128)(2,1)S(1)} %all-to-all-done.2.got_ref, bf16[64,128]{1,0:T(8,128)(2,1)S(1)} %get-tuple-element.26.refs_0_, ...), custom_call_target="tpu_custom_call" | custom-call | flops 3221225472 | bytes 8388608 | tf_op jit(solution)/shard_map/pallas_call | solution.py:197
  88.5 0.5 collective-permute-start.11
  89.0 0.9 collective-permute-done.11
  90.0 9.5 %all_to_all.25 = bf16[8,80,128]{2,1,0:T(8,128)(2,1)S(1)} all-to-all(bf16[8,80,128]{2,1,0:T(8,128)(2,1)S(1)} %pad_maximum_fusion), channel_id=1, replica_groups=mesh['rows'=8,'cols'=32] {'rows'}, dimensions={0} | all-to-all | bytes 327680 | tf_op jit(solution)/shard_map/all_to_all | solution.py:319
  99.5 16.0 %all_to_all.26.got_ref = bf16[16,32,128]{2,1,0:T(8,128)(2,1)S(1)} all-to-all(bf16[16,32,128]{2,1,0:T(8,128)(2,1)S(1)} %pad_maximum_fusion.1), channel_id=1, replica_groups={{0,2,4,6,8,10,12,14,16,18,20,22,24,26,28,30},{1,3,5,7,9,11,13,15,17,19,..., dimensions={0} | all-to-all | bytes 262144 | tf_op jit(solution)/shard_map/all_to_all | solution.py:228
  115.5 0.6 shard_map.72
  (22 shorter events, 0.2 us)
Async XLA Ops:
  0.6 55.9 %copy-start = (f32[64,128]{1,0:T(8,128)S(1)}, f32[64,128]{1,0:T(8,128)}, u32[]{:S(2)}) copy-start(f32[64,128]{1,0:T(8,128)} %b_ref.3) | copy-start | bytes 98308
  0.6 55.9 %copy-start.1 = (f32[16,128]{1,0:T(8,128)S(1)}, f32[16,128]{1,0:T(8,128)}, u32[]{:S(2)}) copy-start(f32[16,128]{1,0:T(8,128)} %a_ref.3) | copy-start | bytes 24580
  2.2 15.9 %collective-permute-start = (bf16[64,128]{1,0:T(8,128)(2,1)S(1)}, bf16[64,128]{1,0:T(8,128)(2,1)S(1)}, u32[]{:S(2)}, u32[]{:S(2)}) collective-permute-start(bf16[64,128]{1,0:T(8,128)(2,1)S(1)} %get-tuple-element.20.refs_0_), channel_id=1, source_target_pairs={{0,128},{32,160},{64,192},{96,224},{128,0},{160,32},{192,64},{224,... | collective-permute-start | bytes 49160 | tf_op jit(solution)/shard_map/ppermute | solution.py:218
  6.0 22.8 %all-to-all-start = ((bf16[32,16,128]{2,1,0:T(8,128)(2,1)}), bf16[32,16,128]{2,1,0:T(8,128)(2,1)S(1)}, u32[]{:S(2)}, u32[]{:S(2)}) async-start(bf16[32,16,128]{2,1,0:T(8,128)(2,1)} %get-tuple-element.19), calls=%async_computation | async-start | bytes 262144 | tf_op jit(solution)/shard_map/all_to_all | solution.py:296
  18.0 2.9 %collective-permute-start.1 = (bf16[128,128]{1,0:T(8,128)(2,1)S(1)}, bf16[128,128]{1,0:T(8,128)(2,1)S(1)}, u32[]{:S(2)}, u32[]{:S(2)}) collective-permute-start(bf16[128,128]{1,0:T(8,128)(2,1)S(1)} %pad_maximum_fusion.3), channel_id=1, source_target_pairs={{0,64},{32,96},{64,0},{96,32},{128,192},{160,224},{192,128},{224,1... | collective-permute-start | bytes 98312 | tf_op jit(solution)/shard_map/ppermute | solution.py:218
  20.9 3.6 %collective-permute-start.2 = (bf16[256,128]{1,0:T(8,128)(2,1)S(1)}, bf16[256,128]{1,0:T(8,128)(2,1)S(1)}, u32[]{:S(2)}, u32[]{:S(2)}) collective-permute-start(bf16[256,128]{1,0:T(8,128)(2,1)S(1)} %pad_maximum_fusion.2), channel_id=1, source_target_pairs={{0,32},{32,0},{64,96},{96,64},{128,160},{160,128},{192,224},{224,1... | collective-permute-start | bytes 196616 | tf_op jit(solution)/shard_map/ppermute | solution.py:218
  37.9 7.9 %collective-permute-start.3 = (bf16[272,128]{1,0:T(8,128)(2,1)S(1)}, bf16[272,128]{1,0:T(8,128)(2,1)S(1)}, u32[]{:S(2)}, u32[]{:S(2)}) collective-permute-start(bf16[272,128]{1,0:T(8,128)(2,1)S(1)} %get-tuple-element.24), channel_id=1, source_target_pairs={{0,128},{32,160},{64,192},{96,224},{128,0},{160,32},{192,64},{224,... | collective-permute-start | bytes 208904 | tf_op jit(solution)/shard_map/ppermute | solution.py:218
  38.0 18.5 %all-to-all-start.1 = ((bf16[32,16,128]{2,1,0:T(8,128)(2,1)}), bf16[32,16,128]{2,1,0:T(8,128)(2,1)S(1)}, u32[]{:S(2)}, u32[]{:S(2)}) async-start(bf16[32,16,128]{2,1,0:T(8,128)(2,1)} %get-tuple-element.22), calls=%async_computation.1 | async-start | bytes 262144 | tf_op jit(solution)/shard_map/all_to_all | solution.py:304
  45.8 2.8 %collective-permute-start.6 = (bf16[16,128]{1,0:T(8,128)(2,1)S(1)}, bf16[16,128]{1,0:T(8,128)(2,1)S(1)}, u32[]{:S(2)}, u32[]{:S(2)}) collective-permute-start(bf16[16,128]{1,0:T(8,128)(2,1)S(1)} %fusion.1), channel_id=1, source_target_pairs={{0,64},{32,96},{64,0},{96,32},{128,192},{160,224},{192,128},{224,1... | collective-permute-start | bytes 12296 | tf_op jit(solution)/shard_map/ppermute | solution.py:218
  47.1 3.1 %collective-permute-start.4 = (bf16[128,128]{1,0:T(8,128)(2,1)S(1)}, bf16[128,128]{1,0:T(8,128)(2,1)S(1)}, u32[]{:S(2)}, u32[]{:S(2)}) collective-permute-start(bf16[128,128]{1,0:T(8,128)(2,1)S(1)} %slice.43), channel_id=1, source_target_pairs={{0,64},{32,96},{64,0},{96,32},{128,192},{160,224},{192,128},{224,1... | collective-permute-start | bytes 98312 | tf_op jit(solution)/shard_map/ppermute | solution.py:218
  48.7 2.8 %collective-permute-start.7 = (bf16[16,128]{1,0:T(8,128)(2,1)S(1)}, bf16[16,128]{1,0:T(8,128)(2,1)S(1)}, u32[]{:S(2)}, u32[]{:S(2)}) collective-permute-start(bf16[16,128]{1,0:T(8,128)(2,1)S(1)} %add_convert_fusion.3), channel_id=1, source_target_pairs={{0,32},{32,0},{64,96},{96,64},{128,160},{160,128},{192,224},{224,1... | collective-permute-start | bytes 12296 | tf_op jit(solution)/shard_map/ppermute | solution.py:218
  50.3 3.0 %collective-permute-start.5 = (bf16[64,128]{1,0:T(8,128)(2,1)S(1)}, bf16[64,128]{1,0:T(8,128)(2,1)S(1)}, u32[]{:S(2)}, u32[]{:S(2)}) collective-permute-start(bf16[64,128]{1,0:T(8,128)(2,1)S(1)} %slice.45), channel_id=1, source_target_pairs={{0,32},{32,0},{64,96},{96,64},{128,160},{160,128},{192,224},{224,1... | collective-permute-start | bytes 49160 | tf_op jit(solution)/shard_map/ppermute | solution.py:218
  57.3 9.7 %collective-permute-start.8 = (bf16[64,128]{1,0:T(8,128)(2,1)S(1)}, bf16[64,128]{1,0:T(8,128)(2,1)S(1)}, u32[]{:S(2)}, u32[]{:S(2)}) collective-permute-start(bf16[64,128]{1,0:T(8,128)(2,1)S(1)} %get-tuple-element.26.refs_0_), channel_id=1, source_target_pairs={{0,32},{32,0},{64,96},{96,64},{128,160},{160,128},{192,224},{224,1... | collective-permute-start | bytes 49160 | tf_op jit(solution)/shard_map/ppermute | solution.py:218
  57.6 22.3 %all-to-all-start.2 = ((bf16[32,32,128]{2,1,0:T(8,128)(2,1)}), bf16[32,32,128]{2,1,0:T(8,128)(2,1)S(1)}, u32[]{:S(2)}, u32[]{:S(2)}) async-start(bf16[32,32,128]{2,1,0:T(8,128)(2,1)} %get-tuple-element.25), calls=%async_computation.2 | async-start | bytes 524288 | tf_op jit(solution)/shard_map/all_to_all | solution.py:308
  67.0 3.1 %collective-permute-start.9 = (bf16[128,128]{1,0:T(8,128)(2,1)S(1)}, bf16[128,128]{1,0:T(8,128)(2,1)S(1)}, u32[]{:S(2)}, u32[]{:S(2)}) collective-permute-start(bf16[128,128]{1,0:T(8,128)(2,1)S(1)} %pad_maximum_fusion.4), channel_id=1, source_target_pairs={{0,64},{32,96},{64,0},{96,32},{128,192},{160,224},{192,128},{224,1... | collective-permute-start | bytes 98312 | tf_op jit(solution)/shard_map/ppermute | solution.py:218
  70.1 4.9 %collective-permute-start.10 = (bf16[256,128]{1,0:T(8,128)(2,1)S(1)}, bf16[256,128]{1,0:T(8,128)(2,1)S(1)}, u32[]{:S(2)}, u32[]{:S(2)}) collective-permute-start(bf16[256,128]{1,0:T(8,128)(2,1)S(1)} %shard_map.70), channel_id=1, source_target_pairs={{0,128},{32,160},{64,192},{96,224},{128,0},{160,32},{192,64},{224,... | collective-permute-start | bytes 196616 | tf_op jit(solution)/shard_map/ppermute | solution.py:218
  88.5 1.4 %collective-permute-start.11 = (bf16[17,16,128]{2,1,0:T(8,128)(2,1)S(1)}, bf16[17,16,128]{2,1,0:T(8,128)(2,1)S(1)}, u32[]{:S(2)}, u32[]{:S(2)}) collective-permute-start(bf16[17,16,128]{2,1,0:T(8,128)(2,1)S(1)} %get-tuple-element.29), channel_id=1, source_target_pairs={{0,1},{1,0},{2,3},{3,2},{4,5},{5,4},{6,7},{7,6},{8,9},{9,8},{10,11... | collective-permute-start | bytes 208904 | tf_op jit(solution)/shard_map/ppermute | solution.py:222
